TPU v7x, 32 devices: a whole 2x2x4 slice. The times are simulated.
32 devices in a mesh: gx: 8 (over z, core), gy: 4 (over y, x).
Axes of the slice: x: 2, y: 2, z: 4, core: 2. Of those that a mesh axis runs over, the one named last changes fastest.
Arguments:
- source: float32 [64, 512, 256], P('gx', 'gy'), may hold values from -8 to 8
- density: float32 [64, 512, 256], P('gx', 'gy'), may hold values from 0.08 to 1.7
Outputs:
- pressure: float32 [64, 512, 256], P('gx', 'gy')
- residual: float32 [64, 512, 256], P('gx', 'gy')
All inputs are finite; a program needn't handle non-finite values.
Results may differ from a plain program's by a relative error of at most 0.00021.
Values sent between devices are 32-bit elements; how exact they have to be, the bound alone decides.
No kernel may reach another device: no remote copies, remote signals or barrier semaphores. Data moves between devices by JAX's collectives and lax.ppermute only.
A program may use at most 64 MiB of HBM per device.

v0:
```python
import jax
import jax.numpy as jnp
from jax import lax
from jax.sharding import PartitionSpec as P

ITERS = 2


def extended(shard, sides, width):
    for axis, dim in sides:
        devices, length = (lax.axis_size(axis), shard.shape[dim])
        up = [(i, (i + 1) % devices) for i in range(devices - 1)]
        down = [(j, i) for i, j in up]
        last = lax.slice_in_dim(shard, length - width, length, axis=dim)
        initial = lax.slice_in_dim(shard, 0, width, axis=dim)
        before = lax.ppermute(last, axis, up)
        after = lax.ppermute(initial, axis, down)
        shard = jnp.concatenate([before, shard, after], axis=dim)
    return shard


def neighbours(padded):
    return [
        padded[2:, 1:-1, 1:-1],
        padded[:-2, 1:-1, 1:-1],
        padded[1:-1, 2:, 1:-1],
        padded[1:-1, :-2, 1:-1],
        padded[1:-1, 1:-1, 2:],
        padded[1:-1, 1:-1, :-2],
    ]


def pad_depth(field):
    return jnp.pad(field, ((0, 0), (0, 0), (1, 1)))


def weights_from(center, padded):
    nearby = neighbours(pad_depth(padded))
    weights = [2.0 / jnp.where(center > 0, center + other, 1.0) for other in nearby]
    diag_sum = weights[0]
    for weight_one in weights[1:]:
        diag_sum = diag_sum + weight_one
    return (weights, lax.rsqrt(diag_sum))


def couple(padded, weights):
    nearby = neighbours(pad_depth(padded))
    total = weights[0] * nearby[0]
    for weight_one, other in zip(weights[1:], nearby[1:]):
        total = total + weight_one * other
    return total


def scaled_apply(field, weights, scale_inv):
    scaled = scale_inv * field
    padded = extended(scaled, (("gx", 0), ("gy", 1)), 1)
    return field - scale_inv * couple(padded, weights)


def inner_pair(residual, shadow):
    gamma_part = jnp.sum(residual * residual)
    delta_part = jnp.sum(shadow * residual)
    first = lax.psum((gamma_part, delta_part), "gx")
    return lax.psum((first[0], first[1]), "gy")


def shards(source, density):
    rim_density = extended(density, (("gx", 0), ("gy", 1)), 1)
    weights, scale_inv = weights_from(density, rim_density)
    residual = scale_inv * source
    shadow = scaled_apply(residual, weights, scale_inv)
    solution = jnp.zeros_like(source)
    direction = jnp.zeros_like(source)
    along = jnp.zeros_like(source)
    pushed = jnp.zeros_like(source)
    gamma_old = jnp.float32(1.0)
    alpha_old = jnp.float32(1.0)
    for iteration in range(ITERS):
        gamma_now, delta_now = inner_pair(residual, shadow)
        fresh = scaled_apply(shadow, weights, scale_inv)
        if iteration == 0:
            beta_now = jnp.float32(0.0)
            alpha_now = gamma_now / delta_now
        else:
            beta_now = gamma_now / gamma_old
            alpha_now = gamma_now / (delta_now - beta_now * gamma_now / alpha_old)
        pushed = fresh + beta_now * pushed
        along = shadow + beta_now * along
        direction = residual + beta_now * direction
        solution = solution + alpha_now * direction
        residual = residual - alpha_now * along
        shadow = shadow - alpha_now * pushed
        gamma_old = gamma_now
        alpha_old = alpha_now
    return (scale_inv * solution, residual)


def solution(mesh):
    in_specs = (P("gx", "gy", None), P("gx", "gy", None))
    out_specs = (P("gx", "gy", None), P("gx", "gy", None))
    return jax.shard_map(shards, mesh=mesh, in_specs=in_specs, out_specs=out_specs, check_vma=False)
```

profile of v0, /device:TPU:0, one launch (start us, length us, event | category | flops | bytes accessed | tf_op | source)
XLA Modules:
  0.0 125.6 jit_solution(16488615657237976535)
XLA Ops:
  0.6 1.0 fusion.49
  1.6 2.4 %collective-permute-start.1 = (f32[1,128,256]{2,1,0:T(8,128)S(1)}, f32[1,128,256]{2,1,0:T(8,128)S(1)}, u32[]{:S(2)}, u32[]{:S(2)}) collective-permute-start(f32[1,128,256]{2,1,0:T(8,128)S(1)} %get-tuple-element.34), channel_id=1, source_target_pairs={{0,4},{4,8},{8,12},{12,16},{16,20},{20,24},{24,28},{1,5},{5,9},{9,... | collective-permute-start | bytes 393224 | tf_op jit(solution)/shard_map/ppermute | solution.py:16
  4.0 1.3 %collective-permute-start = (f32[1,128,256]{2,1,0:T(8,128)S(1)}, f32[1,128,256]{2,1,0:T(8,128)S(1)}, u32[]{:S(2)}, u32[]{:S(2)}) collective-permute-start(f32[1,128,256]{2,1,0:T(8,128)S(1)} %get-tuple-element.33), channel_id=1, source_target_pairs={{4,0},{8,4},{12,8},{16,12},{20,16},{24,20},{28,24},{5,1},{9,5},{13... | collective-permute-start | bytes 393224 | tf_op jit(solution)/shard_map/ppermute | solution.py:17
  5.4 1.3 %constant_dynamic-update-slice_fusion.1 = f32[10,128,256]{2,1,0:T(8,128)S(1)} fusion(f32[10,128,256]{2,1,0:T(8,128)S(1)} %constant_dynamic-update-slice_fusion.2, f32[8,128,256]{2,1,0:T(8,128)} %param.3), kind=kLoop, calls=%fused_computation.95 | loop fusion | bytes 2097152
  6.7 2.8 %collective-permute-done = f32[1,128,256]{2,1,0:T(8,128)S(1)} collective-permute-done((f32[1,128,256]{2,1,0:T(8,128)S(1)}, f32[1,128,256]{2,1,0:T(8,128)S(1)}, u32[]{:S(2)}, u32[]{:S(2)}) %collective-permute-start) | collective-permute-done | bytes 131104 | tf_op jit(solution)/shard_map/ppermute | solution.py:17
  9.5 3.4 %collective-permute-start.3 = (f32[10,1,256]{2,1,0:T(1,128)S(1)}, f32[10,1,256]{2,1,0:T(1,128)S(1)}, u32[]{:S(2)}, u32[]{:S(2)}) collective-permute-start(f32[10,1,256]{2,1,0:T(1,128)S(1)} %get-tuple-element.27), channel_id=1, source_target_pairs={{0,1},{1,2},{2,3},{4,5},{5,6},{6,7},{8,9},{9,10},{10,11},{12,13},{... | collective-permute-start | bytes 30728 | tf_op jit(solution)/shard_map/ppermute | solution.py:16
  12.9 1.3 %collective-permute-start.2 = (f32[10,1,256]{2,1,0:T(1,128)S(1)}, f32[10,1,256]{2,1,0:T(1,128)S(1)}, u32[]{:S(2)}, u32[]{:S(2)}) collective-permute-start(f32[10,1,256]{2,1,0:T(1,128)S(1)} %get-tuple-element.28), channel_id=1, source_target_pairs={{1,0},{2,1},{3,2},{5,4},{6,5},{7,6},{9,8},{10,9},{11,10},{13,12},{... | collective-permute-start | bytes 30728 | tf_op jit(solution)/shard_map/ppermute | solution.py:17
  14.3 4.2 %collective-permute-done.2 = f32[10,1,256]{2,1,0:T(1,128)S(1)} collective-permute-done((f32[10,1,256]{2,1,0:T(1,128)S(1)}, f32[10,1,256]{2,1,0:T(1,128)S(1)}, u32[]{:S(2)}, u32[]{:S(2)}) %collective-permute-start.2) | collective-permute-done | bytes 10272 | tf_op jit(solution)/shard_map/ppermute | solution.py:17
  18.5 0.7 select_maximum_fusion.8
  19.2 2.2 %fusion.43 = (f32[8,128,256]{2,1,0:T(8,128)S(1)}, f32[8,128,256]{2,1,0:T(8,128)S(1)}, f32[8,128,256]{2,1,0:T(8,128)S(1)}, f32[8,128,256]{2,1,0:T(8,128)S(1)}, f32[8,128,256]{2,1,0:T(8,128)S(1)}) fusion(f32[8,128,256]{2,1,0:T(8,128)S(1)} %copy-done.11, f32[8,128,256]{2,1,0:T(8,128)S(1)} %copy-done, f32[10,130,258]{2,1,0:T(8,128)S(1)} %select_maximum_fusion.8, ...), kind=kLoop, calls=%fused_computation.97 | loop fusion | flops 7864320 | bytes 11030528 | tf_op jit(solution)/shard_map/mul | solution.py:55
  21.5 4.0 %collective-permute-start.5 = (f32[1,128,256]{2,1,0:T(8,128)S(1)}, f32[1,128,256]{2,1,0:T(8,128)S(1)}, u32[]{:S(2)}, u32[]{:S(2)}) collective-permute-start(f32[1,128,256]{2,1,0:T(8,128)S(1)} %get-tuple-element.31), channel_id=1, source_target_pairs={{0,4},{4,8},{8,12},{12,16},{16,20},{20,24},{24,28},{1,5},{5,9},{9,... | collective-permute-start | bytes 393224 | tf_op jit(solution)/shard_map/ppermute | solution.py:16
  25.5 1.3 %collective-permute-start.4 = (f32[1,128,256]{2,1,0:T(8,128)S(1)}, f32[1,128,256]{2,1,0:T(8,128)S(1)}, u32[]{:S(2)}, u32[]{:S(2)}) collective-permute-start(f32[1,128,256]{2,1,0:T(8,128)S(1)} %get-tuple-element.32), channel_id=1, source_target_pairs={{4,0},{8,4},{12,8},{16,12},{20,16},{24,20},{28,24},{5,1},{9,5},{13... | collective-permute-start | bytes 393224 | tf_op jit(solution)/shard_map/ppermute | solution.py:17
  26.8 2.9 %collective-permute-done.4 = f32[1,128,256]{2,1,0:T(8,128)S(1)} collective-permute-done((f32[1,128,256]{2,1,0:T(8,128)S(1)}, f32[1,128,256]{2,1,0:T(8,128)S(1)}, u32[]{:S(2)}, u32[]{:S(2)}) %collective-permute-start.4) | collective-permute-done | bytes 131104 | tf_op jit(solution)/shard_map/ppermute | solution.py:17
  29.7 4.3 %collective-permute-start.7 = (f32[10,1,256]{2,1,0:T(1,128)S(1)}, f32[10,1,256]{2,1,0:T(1,128)S(1)}, u32[]{:S(2)}, u32[]{:S(2)}) collective-permute-start(f32[10,1,256]{2,1,0:T(1,128)S(1)} %get-tuple-element.25), channel_id=1, source_target_pairs={{0,1},{1,2},{2,3},{4,5},{5,6},{6,7},{8,9},{9,10},{10,11},{12,13},{... | collective-permute-start | bytes 30728 | tf_op jit(solution)/shard_map/ppermute | solution.py:16
  34.0 1.3 %collective-permute-start.6 = (f32[10,1,256]{2,1,0:T(1,128)S(1)}, f32[10,1,256]{2,1,0:T(1,128)S(1)}, u32[]{:S(2)}, u32[]{:S(2)}) collective-permute-start(f32[10,1,256]{2,1,0:T(1,128)S(1)} %get-tuple-element.26), channel_id=1, source_target_pairs={{1,0},{2,1},{3,2},{5,4},{6,5},{7,6},{9,8},{10,9},{11,10},{13,12},{... | collective-permute-start | bytes 30728 | tf_op jit(solution)/shard_map/ppermute | solution.py:17
  35.4 4.2 %collective-permute-done.6 = f32[10,1,256]{2,1,0:T(1,128)S(1)} collective-permute-done((f32[10,1,256]{2,1,0:T(1,128)S(1)}, f32[10,1,256]{2,1,0:T(1,128)S(1)}, u32[]{:S(2)}, u32[]{:S(2)}) %collective-permute-start.6) | collective-permute-done | bytes 10272 | tf_op jit(solution)/shard_map/ppermute | solution.py:17
  39.6 0.7 select_maximum_fusion.4
  40.4 3.3 %multiply_reduce_fusion.2 = (f32[]{:T(128)}, f32[]{:T(128)}, f32[8,128,256]{2,1,0:T(8,128)S(1)}) fusion(f32[8,128,256]{2,1,0:T(8,128)S(1)} %get-tuple-element.17, f32[8,128,256]{2,1,0:T(8,128)S(1)} %get-tuple-element.18, f32[10,130,258]{2,1,0:T(8,128)S(1)} %select_maximum_fusion.4, f32[8,128,256]{2,1,0:T(8,128)S(1)} %copy-done, ...), kind=kLoop, calls=%fused_computation.84 | loop fusion | flops 10485758 | bytes 12079112 | tf_op jit(solution)/shard_map/reduce_sum | solution.py:62
  43.7 0.1 mul.118
  43.9 4.0 %collective-permute-start.9 = (f32[1,128,256]{2,1,0:T(8,128)S(1)}, f32[1,128,256]{2,1,0:T(8,128)S(1)}, u32[]{:S(2)}, u32[]{:S(2)}) collective-permute-start(f32[1,128,256]{2,1,0:T(8,128)S(1)} %get-tuple-element.29), channel_id=1, source_target_pairs={{0,4},{4,8},{8,12},{12,16},{16,20},{20,24},{24,28},{1,5},{5,9},{9,... | collective-permute-start | bytes 393224 | tf_op jit(solution)/shard_map/ppermute | solution.py:16
  47.9 1.3 %collective-permute-start.8 = (f32[1,128,256]{2,1,0:T(8,128)S(1)}, f32[1,128,256]{2,1,0:T(8,128)S(1)}, u32[]{:S(2)}, u32[]{:S(2)}) collective-permute-start(f32[1,128,256]{2,1,0:T(8,128)S(1)} %get-tuple-element.30), channel_id=1, source_target_pairs={{4,0},{8,4},{12,8},{16,12},{20,16},{24,20},{28,24},{5,1},{9,5},{13... | collective-permute-start | bytes 393224 | tf_op jit(solution)/shard_map/ppermute | solution.py:17
  49.2 2.7 %collective-permute-done.8 = f32[1,128,256]{2,1,0:T(8,128)S(1)} collective-permute-done((f32[1,128,256]{2,1,0:T(8,128)S(1)}, f32[1,128,256]{2,1,0:T(8,128)S(1)}, u32[]{:S(2)}, u32[]{:S(2)}) %collective-permute-start.8) | collective-permute-done | bytes 131104 | tf_op jit(solution)/shard_map/ppermute | solution.py:17
  52.0 0.7 pad_maximum_fusion.20
  52.6 3.4 %collective-permute-start.11 = (f32[10,1,256]{2,1,0:T(1,128)}, f32[10,1,256]{2,1,0:T(1,128)S(1)}, u32[]{:S(2)}, u32[]{:S(2)}) collective-permute-start(f32[10,1,256]{2,1,0:T(1,128)} %get-tuple-element.23), channel_id=1, source_target_pairs={{0,1},{1,2},{2,3},{4,5},{5,6},{6,7},{8,9},{9,10},{10,11},{12,13},{... | collective-permute-start | bytes 30728 | tf_op jit(solution)/shard_map/ppermute | solution.py:16
  56.0 1.3 %collective-permute-start.10 = (f32[10,1,256]{2,1,0:T(1,128)}, f32[10,1,256]{2,1,0:T(1,128)S(1)}, u32[]{:S(2)}, u32[]{:S(2)}) collective-permute-start(f32[10,1,256]{2,1,0:T(1,128)} %get-tuple-element.24), channel_id=1, source_target_pairs={{1,0},{2,1},{3,2},{5,4},{6,5},{7,6},{9,8},{10,9},{11,10},{13,12},{... | collective-permute-start | bytes 30728 | tf_op jit(solution)/shard_map/ppermute | solution.py:17
  57.3 17.4 %all-reduce.4 = (f32[]{:T(128)}, f32[]{:T(128)}) all-reduce(f32[]{:T(128)} %get-tuple-element.5, f32[]{:T(128)} %get-tuple-element.4), channel_id=1, replica_groups=mesh['gx'=8,'gy'=4] {'gx'}, use_global_device_ids=true, to_apply=%region_1.2 | all-reduce | flops 2 | bytes 16 | tf_op jit(solution)/shard_map/psum | solution.py:63
  74.7 10.4 %all-reduce.6 = (f32[]{:T(128)}, f32[]{:T(128)}) all-reduce(f32[]{:T(128)} %get-tuple-element.8, f32[]{:T(128)} %get-tuple-element.9), channel_id=1, replica_groups=mesh['gx'=8,'gy'=4] {'gy'}, use_global_device_ids=true, to_apply=%region_2.3 | all-reduce | flops 2 | bytes 16 | tf_op jit(solution)/shard_map/psum | solution.py:64
  86.4 2.2 %select_maximum_fusion = f32[10,130,258]{2,1,0:T(8,128)S(1)} fusion(f32[10,1,256]{2,1,0:T(1,128)S(1)} %collective-permute-done.10, f32[10,1,256]{2,1,0:T(1,128)S(1)} %collective-permute-done.11, f32[1,128,256]{2,1,0:T(8,128)} %copy-done.9, f32[8,128,256]{2,1,0:T(8,128)} %copy-done.2, f32[1,128,256]{2,1,0:T(8,128)S(1)} %collective-permute-done.9), kind=kLoop, calls=%fused_computation.2 | loop fusion | flops 4024800 | bytes 2672800 | tf_op jit(solution)/shard_map/concatenate | solution.py:18
  88.6 5.7 %multiply_reduce_fusion = (f32[]{:T(128)}, f32[]{:T(128)}, f32[8,128,256]{2,1,0:T(8,128)}) fusion(f32[8,128,256]{2,1,0:T(8,128)S(1)} %copy-done.5, f32[8,128,256]{2,1,0:T(8,128)} %copy-done.6, f32[]{:T(128)S(6)} %div.36, f32[8,128,256]{2,1,0:T(8,128)S(1)} %get-tuple-element.18, f32[10,130,258]{2,1,0:T(8,128)S(1)} %select_maximum_fusion, ...), kind=kLoop, calls=%fused_computation.81 | loop fusion | flops 11534334 | bytes 13127692 | tf_op jit(solution)/shard_map/reduce_sum | solution.py:62
  94.3 14.3 %all-reduce.3 = (f32[]{:T(128)}, f32[]{:T(128)}) all-reduce(f32[]{:T(128)} %get-tuple-element.3, f32[]{:T(128)} %get-tuple-element.2), channel_id=1, replica_groups=mesh['gx'=8,'gy'=4] {'gx'}, use_global_device_ids=true, to_apply=%region_7.8 | all-reduce | flops 2 | bytes 16 | tf_op jit(solution)/shard_map/psum | solution.py:63
  108.5 9.3 %all-reduce.5 = (f32[]{:T(128)}, f32[]{:T(128)}) all-reduce(f32[]{:T(128)} %get-tuple-element.6, f32[]{:T(128)} %get-tuple-element.7), channel_id=1, replica_groups=mesh['gx'=8,'gy'=4] {'gy'}, use_global_device_ids=true, to_apply=%region_8.9 | all-reduce | flops 2 | bytes 16 | tf_op jit(solution)/shard_map/psum | solution.py:64
  122.0 3.6 %multiply_subtract_fusion = (f32[8,128,256]{2,1,0:T(8,128)}, f32[8,128,256]{2,1,0:T(8,128)}) fusion(f32[8,128,256]{2,1,0:T(8,128)} %get-tuple-element.14, f32[8,128,256]{2,1,0:T(8,128)} %copy-done.6, f32[]{:T(128)S(6)} %div.37, f32[]{:T(128)S(6)} %div.39, f32[8,128,256]{2,1,0:T(8,128)} %copy-done.4, f32[]{:T(128)S(6)} %div.36, ...), kind=kLoop, calls=%fused_computation.79 | loop fusion | flops 3145728 | bytes 6291468 | tf_op jit(solution)/shard_map/sub | solution.py:91
  (37 shorter events, 0.3 us)
Async XLA Ops:
  1.6 3.7 %collective-permute-start.1 = (f32[1,128,256]{2,1,0:T(8,128)S(1)}, f32[1,128,256]{2,1,0:T(8,128)S(1)}, u32[]{:S(2)}, u32[]{:S(2)}) collective-permute-start(f32[1,128,256]{2,1,0:T(8,128)S(1)} %get-tuple-element.34), channel_id=1, source_target_pairs={{0,4},{4,8},{8,12},{12,16},{16,20},{20,24},{24,28},{1,5},{5,9},{9,... | collective-permute-start | bytes 393224 | tf_op jit(solution)/shard_map/ppermute | solution.py:16
  4.0 5.4 %collective-permute-start = (f32[1,128,256]{2,1,0:T(8,128)S(1)}, f32[1,128,256]{2,1,0:T(8,128)S(1)}, u32[]{:S(2)}, u32[]{:S(2)}) collective-permute-start(f32[1,128,256]{2,1,0:T(8,128)S(1)} %get-tuple-element.33), channel_id=1, source_target_pairs={{4,0},{8,4},{12,8},{16,12},{20,16},{24,20},{28,24},{5,1},{9,5},{13... | collective-permute-start | bytes 393224 | tf_op jit(solution)/shard_map/ppermute | solution.py:17
  6.7 12.5 %copy-start = (f32[8,128,256]{2,1,0:T(8,128)S(1)}, f32[8,128,256]{2,1,0:T(8,128)}, u32[]{:S(2)}) copy-start(f32[8,128,256]{2,1,0:T(8,128)} %param.3) | copy-start | bytes 3145732
  6.7 12.5 %copy-start.11 = (f32[8,128,256]{2,1,0:T(8,128)S(1)}, f32[8,128,256]{2,1,0:T(8,128)}, u32[]{:S(2)}) copy-start(f32[8,128,256]{2,1,0:T(8,128)} %param.2) | copy-start | bytes 3145732
  9.5 4.8 %collective-permute-start.3 = (f32[10,1,256]{2,1,0:T(1,128)S(1)}, f32[10,1,256]{2,1,0:T(1,128)S(1)}, u32[]{:S(2)}, u32[]{:S(2)}) collective-permute-start(f32[10,1,256]{2,1,0:T(1,128)S(1)} %get-tuple-element.27), channel_id=1, source_target_pairs={{0,1},{1,2},{2,3},{4,5},{5,6},{6,7},{8,9},{9,10},{10,11},{12,13},{... | collective-permute-start | bytes 30728 | tf_op jit(solution)/shard_map/ppermute | solution.py:16
  12.9 5.6 %collective-permute-start.2 = (f32[10,1,256]{2,1,0:T(1,128)S(1)}, f32[10,1,256]{2,1,0:T(1,128)S(1)}, u32[]{:S(2)}, u32[]{:S(2)}) collective-permute-start(f32[10,1,256]{2,1,0:T(1,128)S(1)} %get-tuple-element.28), channel_id=1, source_target_pairs={{1,0},{2,1},{3,2},{5,4},{6,5},{7,6},{9,8},{10,9},{11,10},{13,12},{... | collective-permute-start | bytes 30728 | tf_op jit(solution)/shard_map/ppermute | solution.py:17
  21.4 18.9 %copy-start.4 = (f32[8,128,256]{2,1,0:T(8,128)}, f32[8,128,256]{2,1,0:T(8,128)S(1)}, u32[]{:S(2)}) copy-start(f32[8,128,256]{2,1,0:T(8,128)S(1)} %get-tuple-element.17) | copy-start | bytes 3145732
  21.5 18.9 %copy-start.7 = (f32[8,128,256]{2,1,0:T(8,128)}, f32[8,128,256]{2,1,0:T(8,128)S(1)}, u32[]{:S(2)}) copy-start(f32[8,128,256]{2,1,0:T(8,128)S(1)} %get-tuple-element.19) | copy-start | bytes 3145732
  21.5 18.9 %copy-start.8 = (f32[8,128,256]{2,1,0:T(8,128)}, f32[8,128,256]{2,1,0:T(8,128)S(1)}, u32[]{:S(2)}) copy-start(f32[8,128,256]{2,1,0:T(8,128)S(1)} %get-tuple-element.20) | copy-start | bytes 3145732
  21.5 5.3 %collective-permute-start.5 = (f32[1,128,256]{2,1,0:T(8,128)S(1)}, f32[1,128,256]{2,1,0:T(8,128)S(1)}, u32[]{:S(2)}, u32[]{:S(2)}) collective-permute-start(f32[1,128,256]{2,1,0:T(8,128)S(1)} %get-tuple-element.31), channel_id=1, source_target_pairs={{0,4},{4,8},{8,12},{12,16},{16,20},{20,24},{24,28},{1,5},{5,9},{9,... | collective-permute-start | bytes 393224 | tf_op jit(solution)/shard_map/ppermute | solution.py:16
  25.5 4.2 %collective-permute-start.4 = (f32[1,128,256]{2,1,0:T(8,128)S(1)}, f32[1,128,256]{2,1,0:T(8,128)S(1)}, u32[]{:S(2)}, u32[]{:S(2)}) collective-permute-start(f32[1,128,256]{2,1,0:T(8,128)S(1)} %get-tuple-element.32), channel_id=1, source_target_pairs={{4,0},{8,4},{12,8},{16,12},{20,16},{24,20},{28,24},{5,1},{9,5},{13... | collective-permute-start | bytes 393224 | tf_op jit(solution)/shard_map/ppermute | solution.py:17
  29.7 5.7 %collective-permute-start.7 = (f32[10,1,256]{2,1,0:T(1,128)S(1)}, f32[10,1,256]{2,1,0:T(1,128)S(1)}, u32[]{:S(2)}, u32[]{:S(2)}) collective-permute-start(f32[10,1,256]{2,1,0:T(1,128)S(1)} %get-tuple-element.25), channel_id=1, source_target_pairs={{0,1},{1,2},{2,3},{4,5},{5,6},{6,7},{8,9},{9,10},{10,11},{12,13},{... | collective-permute-start | bytes 30728 | tf_op jit(solution)/shard_map/ppermute | solution.py:16
  34.0 5.6 %collective-permute-start.6 = (f32[10,1,256]{2,1,0:T(1,128)S(1)}, f32[10,1,256]{2,1,0:T(1,128)S(1)}, u32[]{:S(2)}, u32[]{:S(2)}) collective-permute-start(f32[10,1,256]{2,1,0:T(1,128)S(1)} %get-tuple-element.26), channel_id=1, source_target_pairs={{1,0},{2,1},{3,2},{5,4},{6,5},{7,6},{9,8},{10,9},{11,10},{13,12},{... | collective-permute-start | bytes 30728 | tf_op jit(solution)/shard_map/ppermute | solution.py:17
  43.7 8.9 %copy-start.6 = (f32[8,128,256]{2,1,0:T(8,128)}, f32[8,128,256]{2,1,0:T(8,128)S(1)}, u32[]{:S(2)}) copy-start(f32[8,128,256]{2,1,0:T(8,128)S(1)} %get-tuple-element.15) | copy-start | bytes 3145732
  43.8 8.1 %copy-start.2 = (f32[8,128,256]{2,1,0:T(8,128)}, f32[8,128,256]{2,1,0:T(8,128)S(1)}, u32[]{:S(2)}) copy-start(f32[8,128,256]{2,1,0:T(8,128)S(1)} %mul.118) | copy-start | bytes 3145732
  43.9 5.3 %collective-permute-start.9 = (f32[1,128,256]{2,1,0:T(8,128)S(1)}, f32[1,128,256]{2,1,0:T(8,128)S(1)}, u32[]{:S(2)}, u32[]{:S(2)}) collective-permute-start(f32[1,128,256]{2,1,0:T(8,128)S(1)} %get-tuple-element.29), channel_id=1, source_target_pairs={{0,4},{4,8},{8,12},{12,16},{16,20},{20,24},{24,28},{1,5},{5,9},{9,... | collective-permute-start | bytes 393224 | tf_op jit(solution)/shard_map/ppermute | solution.py:16
  47.9 4.0 %collective-permute-start.8 = (f32[1,128,256]{2,1,0:T(8,128)S(1)}, f32[1,128,256]{2,1,0:T(8,128)S(1)}, u32[]{:S(2)}, u32[]{:S(2)}) collective-permute-start(f32[1,128,256]{2,1,0:T(8,128)S(1)} %get-tuple-element.30), channel_id=1, source_target_pairs={{4,0},{8,4},{12,8},{16,12},{20,16},{24,20},{28,24},{5,1},{9,5},{13... | collective-permute-start | bytes 393224 | tf_op jit(solution)/shard_map/ppermute | solution.py:17
  52.0 0.7 copy-start.9
  52.6 33.7 %collective-permute-start.11 = (f32[10,1,256]{2,1,0:T(1,128)}, f32[10,1,256]{2,1,0:T(1,128)S(1)}, u32[]{:S(2)}, u32[]{:S(2)}) collective-permute-start(f32[10,1,256]{2,1,0:T(1,128)} %get-tuple-element.23), channel_id=1, source_target_pairs={{0,1},{1,2},{2,3},{4,5},{5,6},{6,7},{8,9},{9,10},{10,11},{12,13},{... | collective-permute-start | bytes 30728 | tf_op jit(solution)/shard_map/ppermute | solution.py:16
  56.0 30.3 %collective-permute-start.10 = (f32[10,1,256]{2,1,0:T(1,128)}, f32[10,1,256]{2,1,0:T(1,128)S(1)}, u32[]{:S(2)}, u32[]{:S(2)}) collective-permute-start(f32[10,1,256]{2,1,0:T(1,128)} %get-tuple-element.24), channel_id=1, source_target_pairs={{1,0},{2,1},{3,2},{5,4},{6,5},{7,6},{9,8},{10,9},{11,10},{13,12},{... | collective-permute-start | bytes 30728 | tf_op jit(solution)/shard_map/ppermute | solution.py:17
  86.3 2.2 %copy-start.1 = (f32[8,128,256]{2,1,0:T(8,128)S(1)}, f32[8,128,256]{2,1,0:T(8,128)}, u32[]{:S(2)}) copy-start(f32[8,128,256]{2,1,0:T(8,128)} %param.3) | copy-start | bytes 3145732
  86.3 2.2 %copy-start.3 = (f32[8,128,256]{2,1,0:T(8,128)S(1)}, f32[8,128,256]{2,1,0:T(8,128)}, u32[]{:S(2)}) copy-start(f32[8,128,256]{2,1,0:T(8,128)} %copy-done.2) | copy-start | bytes 3145732
  86.3 2.2 %copy-start.5 = (f32[8,128,256]{2,1,0:T(8,128)S(1)}, f32[8,128,256]{2,1,0:T(8,128)}, u32[]{:S(2)}) copy-start(f32[8,128,256]{2,1,0:T(8,128)} %copy-done.4) | copy-start | bytes 3145732
  86.3 2.2 %copy-start.10 = (f32[1,128,256]{2,1,0:T(8,128)S(1)}, f32[1,128,256]{2,1,0:T(8,128)}, u32[]{:S(2)}) copy-start(f32[1,128,256]{2,1,0:T(8,128)} %copy-done.9) | copy-start | bytes 393220
where the time goes:
time: 126 us
  blocking collectives  51.4 us (41%)
  starting transfers between devices  29.3 us (23%)
  other arithmetic  19.3 us (15%)
  waiting for transfers between devices  16.9 us (13%)
  between operations  6.33 us (5%)
  local copies, waits for them, and re-layouts  2.42 us (2%)
    psum x2, blocking collectives, inner_pair(): first = lax.psum((gamma_part, delta_part), 'gx')  31.7 us
    ppermute x6, starting transfers between devices, extended(): before = lax.ppermute(last, axis, up)  21.5 us
    psum x2, blocking collectives, inner_pair(): return lax.psum((first[0], first[1]), 'gy')  19.7 us
    ppermute x6, waiting for transfers between devices, extended(): after = lax.ppermute(initial, axis, down)  16.8 us
    reduce_sum x2, other arithmetic, inner_pair(): delta_part = jnp.sum(shadow * residual)  9 us
    ppermute x6, starting transfers between devices, extended(): after = lax.ppermute(initial, axis, down)  7.75 us
    concatenate x5, other arithmetic, extended(): shard = jnp.concatenate([before, shard, after], axis=dim)  4.32 us
    sub x1, other arithmetic, shards(): residual = residual - alpha_now * along  3.59 us
  transfers between devices with their start and end apart: 12, of which 7 were waited for; matrix products, arithmetic and copies ran while one was open for 1% of the time, Pallas kernels for 0%

commit v1 on v0

v1 whole, which is shorter than its diff:
```python
import functools

import jax
import jax.numpy as jnp
from jax import lax
from jax.experimental import pallas as pl
from jax.experimental.pallas import tpu as pltpu
from jax.sharding import PartitionSpec as P

ITERS = 2
TILE = 8
OFF = 16
TINY = 1e-3
PART = 16
VMEM = pltpu.VMEM


def swaps(nx, ny):
    at = lambda x, y: x * ny + y
    near, far, ynear, yfar = [], [], [], []
    for x in range(nx):
        for y in range(ny):
            near.append((at(x, y), at(x ^ 1, y)))
            other = x - 1 if x % 2 == 0 else x + 1
            inside = 0 <= other < nx
            far.append((at(x, y), at(other, y) if inside else at(x, y ^ 1)))
            ynear.append((at(x, y), at(x, y ^ 1)))
            beside = y - 1 if y % 2 == 0 else y + 1
            within = 0 <= beside < ny
            yfar.append((at(x, y), at(x, beside) if within else at(x ^ 1, y)))
    return near, far, ynear, yfar


def pack_rows(par, dlo, dhi, slo, shi, near, xs_out, dg_out):
    planes = dlo.shape[0]
    row = lax.broadcasted_iota(jnp.int32, (TILE, dlo.shape[2]), 0)

    def tiles(dens_lo, dens_hi, src_lo, src_hi):
        down = jnp.where(row < 3, dens_lo, jnp.where((row >= 4) & (row < 6), pltpu.roll(src_lo, 4, 0), 0.0))
        up = jnp.where(row > 4, dens_hi, jnp.where((row == 2) | (row == 3), pltpu.roll(src_hi, 4, 0), 0.0))
        return down, up

    yodd = par[1] == 1

    def put(k, down, up):
        xs_out[k] = jnp.where(yodd, down, up)
        dg_out[k] = jnp.where(yodd, up, down)

    for k in range(planes):
        put(k, *tiles(dlo[k], dhi[k], slo[k], shi[k]))
    last = near.shape[1] - TILE
    xodd = par[0] == 1

    for k in range(2):
        d = jnp.where(xodd, k + 1, k)
        s = jnp.where(xodd, 3 + k, 3 + k)
        down, up = tiles(near[d, :TILE], near[d, last:], near[s, :TILE], near[s, last:])
        put(planes + k, down, up)


def main_kernel(par, dens, src, near, far, rxs, rdg, rfc, r0_out, w0_out, n0_out, sc_out, mom_out,
                dx, sx, wx, wy, wz, sc, g0, g1):
    nx, ny, nz = dens.shape
    lo_rows, hi_rows = OFF - TILE, OFF + ny
    total = hi_rows + TILE
    xodd, yodd = par[0] == 1, par[1] == 1
    has_lo, has_hi, has_down, has_up = par[2] == 1, par[3] == 1, par[4] == 1, par[5] == 1
    zero_tile = jnp.zeros((TILE, nz), jnp.float32)
    row = lax.broadcasted_iota(jnp.int32, (TILE, nz), 0)
    own = slice(OFF, OFF + ny)

    for k in range(nx):
        dx[k + 3, own] = dens[k]
        sx[k + 3, own] = src[k]

    @pl.when(xodd)
    def _():
        for k in range(3):
            dx[k, own] = jnp.where(has_lo, near[k], 0.0)
            dx[nx + 3 + k, own] = jnp.where(has_hi, far[k], 0.0)
        for k in range(2):
            sx[1 + k, own] = jnp.where(has_lo, near[3 + k], 0.0)
            sx[nx + 3 + k, own] = jnp.where(has_hi, far[3 + k], 0.0)

    @pl.when(jnp.logical_not(xodd))
    def _():
        for k in range(3):
            dx[k, own] = jnp.where(has_lo, far[k], 0.0)
            dx[nx + 3 + k, own] = jnp.where(has_hi, near[k], 0.0)
        for k in range(2):
            sx[1 + k, own] = jnp.where(has_lo, far[3 + k], 0.0)
            sx[nx + 3 + k, own] = jnp.where(has_hi, near[3 + k], 0.0)

    def rows_of(e, lower, upper, inside):
        low = jnp.where(jnp.logical_and(has_down, inside), lower, 0.0)
        high = jnp.where(jnp.logical_and(has_up, inside), upper, 0.0)
        dx[e, lo_rows:OFF] = jnp.where(row > 4, low, 0.0)
        sx[e, lo_rows:OFF] = jnp.where(row > 5, pltpu.roll(low, 4, 0), 0.0)
        dx[e, hi_rows:total] = jnp.where(row < 3, high, 0.0)
        sx[e, hi_rows:total] = jnp.where(row < 2, pltpu.roll(high, 4, 0), 0.0)

    for k in range(nx):
        a, b = rxs[k], rdg[k]
        rows_of(k + 3, jnp.where(yodd, a, b), jnp.where(yodd, b, a), True)
    for k in range(2):
        a, b = rxs[nx + k], rdg[nx + k]
        rows_of(jnp.where(xodd, 1 + k, nx + 3 + k), jnp.where(yodd, a, b), jnp.where(yodd, b, a), jnp.where(xodd, has_lo, has_hi))
        a, b = rfc[k], rfc[2 + k]
        rows_of(jnp.where(xodd, nx + 3 + k, 1 + k), jnp.where(yodd, a, b), jnp.where(yodd, b, a), jnp.where(xodd, has_hi, has_lo))
    for e in (0, nx + 5):
        rows_of(e, zero_tile, zero_tile, False)
    for e in range(nx + 6):
        dx[e, lo_rows - TILE:lo_rows] = zero_tile
        dx[e, total:total + TILE] = zero_tile
        g0[e, lo_rows - TILE:lo_rows] = zero_tile
        g0[e, total:total + TILE] = zero_tile
        wy[e, lo_rows - TILE:lo_rows] = zero_tile
        wy[e, total:total + TILE] = zero_tile

    R = 24 if (total - lo_rows) % 24 == 0 else TILE
    lane = lax.broadcasted_iota(jnp.int32, (R, nz), 1)
    inner = lane < nz - 1
    first = lane == 0

    def weight(total_density):
        return 2.0 / jnp.maximum(total_density, TINY)

    for r in range(lo_rows, total, R):
        wx[0, r:r + R] = weight(dx[0, r:r + R] + dx[1, r:r + R])

    def faces(e, carry):
        for r in range(lo_rows, total, R):
            c = dx[e, r:r + R]
            x_up = weight(c + dx[e + 1, r:r + R])
            y_up = weight(c + dx[e, r + 1:r + R + 1])
            z_up = weight(c + jnp.where(inner, pltpu.roll(c, nz - 1, 1), 0.0))
            wx[e, r:r + R] = x_up
            wy[e, r:r + R] = y_up
            z_in = jnp.where(inner, z_up, 0.0)
            wz[e, r:r + R] = z_in
            z_down = jnp.where(first, weight(c), pltpu.roll(z_in, 1, 1))
            diag = x_up + wx[e - 1, r:r + R] + y_up + wy[e, r - 1:r + R - 1] + z_up + z_down
            s = jnp.where(c > 0, lax.rsqrt(diag), 0.0)
            sc[e, r:r + R] = s
            g0[e, r:r + R] = s * (s * sx[e, r:r + R])
        return carry

    lax.fori_loop(1, nx + 5, faces, 0)

    def couple(g, e, r, n):
        c = g[e, r:r + n]
        w = wz[e, r:r + n]
        t = wx[e, r:r + n] * g[e + 1, r:r + n] + wx[e - 1, r:r + n] * g[e - 1, r:r + n]
        t = t + wy[e, r:r + n] * g[e, r + 1:r + n + 1] + wy[e, r - 1:r + n - 1] * g[e, r - 1:r + n - 1]
        return t + w * pltpu.roll(c, nz - 1, 1) + pltpu.roll(w * c, 1, 1)

    def first_apply(e, carry):
        for r in range(lo_rows, total, R):
            s = sc[e, r:r + R]
            r0 = s * sx[e, r:r + R]
            w0 = r0 - s * couple(g0, e, r, R)
            g1[e, r:r + R] = s * w0
        return carry

    lax.fori_loop(2, nx + 4, first_apply, 0)

    Q = 32 if ny % 32 == 0 else TILE
    zero = jnp.zeros((TILE, nz), jnp.float32)

    def fold(v):
        out = v[:TILE]
        for q in range(TILE, Q, TILE):
            out = out + v[q:q + TILE]
        return out

    def second_apply(i, sums):
        e = i + 3
        sums = list(sums)
        for r in range(OFF, OFF + ny, Q):
            s = sc[e, r:r + Q]
            r0 = s * sx[e, r:r + Q]
            w0 = r0 - s * couple(g0, e, r, Q)
            n0 = w0 - s * couple(g1, e, r, Q)
            sc_out[i, r - OFF:r - OFF + Q] = s
            r0_out[i, r - OFF:r - OFF + Q] = r0
            w0_out[i, r - OFF:r - OFF + Q] = w0
            n0_out[i, r - OFF:r - OFF + Q] = n0
            for k, (a, b) in enumerate(((r0, r0), (w0, r0), (w0, w0), (n0, w0), (n0, r0))):
                sums[k] = sums[k] + fold(a * b)
        return tuple(sums)

    sums = lax.fori_loop(0, nx, second_apply, (zero,) * 5)
    place = lax.broadcasted_iota(jnp.int32, (1, 128), 1) // PART
    out = jnp.zeros((1, 128), jnp.float32)
    for k, v in enumerate(sums):
        v = jnp.sum(v, axis=0, keepdims=True)
        p = v[:, :128]
        for q in range(128, nz, 128):
            p = p + v[:, q:q + 128]
        width = 64
        while width >= PART:
            p = p + pltpu.roll(p, width, 1)
            width //= 2
        out = jnp.where(place == k, p, out)
    mom_out[...] = out


def last_kernel(mom, r0_ref, w0_ref, n0_ref, sc_ref, p_out, r_out):
    place = lax.broadcasted_iota(jnp.int32, mom.shape, 1) // PART
    m = mom[...]

    def whole(v):
        return jnp.sum(jnp.sum(v, axis=0, keepdims=True), axis=1, keepdims=True)

    def lanes(k):
        return pltpu.roll(m, (128 - k * PART) % 128, 1) if k else m

    head = place == 0
    m0, m1, m2, m3, m4 = (jnp.where(head, lanes(k), 0.0) for k in range(5))
    gamma0 = whole(m0)
    delta0 = whole(m1)
    a0 = gamma0 / delta0
    gamma1 = whole(m0 - a0 * (m1 + m1 - a0 * m2))
    delta1 = whole(m1 - a0 * (m4 + m2 - a0 * m3))
    b1 = gamma1 / gamma0
    a1 = gamma1 / (delta1 - b1 * gamma1 / a0)
    nx, ny, nz = r0_ref.shape
    Q = 32 if ny % 32 == 0 else TILE
    for i in range(nx):
        for r in range(0, ny, Q):
            at = (i, slice(r, r + Q))
            r0, w0 = r0_ref[at], w0_ref[at]
            r1 = r0 - a0 * w0
            w1 = w0 - a0 * n0_ref[at]
            along = w1 + b1 * w0
            direction = r1 + b1 * r0
            p_out[at] = sc_ref[at] * (a0 * r0 + a1 * direction)
            r_out[at] = r1 - a1 * along


def shards(nx_dev, ny_dev, source, density):
    both = ("gx", "gy")
    near_pairs, far_pairs, ynear_pairs, yfar_pairs = swaps(nx_dev, ny_dev)
    nx, ny, nz = density.shape
    ix, iy = lax.axis_index("gx"), lax.axis_index("gy")
    xodd, yodd = ix % 2, iy % 2
    flags = [xodd, yodd, ix > 0, ix < nx_dev - 1, iy > 0, iy < ny_dev - 1]
    par = jnp.stack([jnp.asarray(f, jnp.int32) for f in flags])

    def planes(upper):
        d = lax.dynamic_slice_in_dim(density, jnp.where(upper, nx - 3, 0), 3, 0)
        s = lax.dynamic_slice_in_dim(source, jnp.where(upper, nx - 2, 0), 2, 0)
        return jnp.concatenate([d, s], axis=0)

    far = lax.ppermute(planes(xodd == 1), both, far_pairs)
    near = lax.ppermute(planes(xodd == 0), both, near_pairs)

    smem = pl.BlockSpec(memory_space=pltpu.SMEM)
    vmem = pl.BlockSpec(memory_space=VMEM)
    low = pl.BlockSpec((nx, TILE, nz), lambda i: (0, 0, 0))
    high = pl.BlockSpec((nx, TILE, nz), lambda i: (0, ny // TILE - 1, 0))
    rows = jax.ShapeDtypeStruct((nx + 2, TILE, nz), jnp.float32)
    xs, dg = pl.pallas_call(
        pack_rows, grid=(1,), out_shape=(rows, rows),
        in_specs=[smem, low, high, low, high, vmem], out_specs=(vmem, vmem), name="pack_rows",
    )(par, density, density, source, source, near)
    rxs = lax.ppermute(xs, both, ynear_pairs)
    rdg = lax.ppermute(dg, both, yfar_pairs)
    begin = jnp.where(xodd == 1, nx - 2, 0)
    corner = jnp.concatenate([lax.dynamic_slice_in_dim(v, begin, 2, 0) for v in (rxs, rdg)], axis=0)
    rfc = lax.ppermute(corner, both, far_pairs)

    whole = jax.ShapeDtypeStruct(density.shape, jnp.float32)
    ext = VMEM((nx + 6, ny + 2 * OFF, nz), jnp.float32)
    r0, w0, n0, sc, mom = pl.pallas_call(
        main_kernel, out_shape=(whole, whole, whole, whole, jax.ShapeDtypeStruct((1, 128), jnp.float32)),
        in_specs=[smem] + [vmem] * 7, out_specs=(vmem,) * 5, scratch_shapes=[ext] * 8, name="main_kernel",
    )(par, density, source, near, far, rxs, rdg, rfc)

    n = nx_dev * ny_dev
    sent = jnp.broadcast_to(mom[None], (n, 1, 128))
    got = lax.all_to_all(sent, both, 0, 0, tiled=True).reshape(n, 128)
    return pl.pallas_call(
        last_kernel, out_shape=(whole, whole), in_specs=[vmem] * 5, out_specs=(vmem, vmem), name="last_kernel",
    )(got, r0, w0, n0, sc)


def solution(mesh):
    spec = P("gx", "gy", None)
    body = functools.partial(shards, mesh.shape["gx"], mesh.shape["gy"])
    return jax.shard_map(body, mesh=mesh, in_specs=(spec, spec), out_specs=(spec, spec), check_vma=False)
```

time: 126 us -> 49.3 us (0.39)
  blocking collectives: 51.4 us -> 10.3 us
  starting transfers between devices: 29.3 us -> 8.4 us
  other arithmetic: 19.3 us -> 0.09 us
  Pallas kernels: 0 us -> 17.1 us
  waiting for transfers between devices: 16.9 us -> 8.25 us
  between operations: 6.33 us -> 0.74 us
  local copies, waits for them, and re-layouts: 2.42 us -> 4.14 us
    psum x4 -> x0, blocking collectives: 51.4 us -> none  [the longest x2 31.7 us: inner_pair(): first = lax.psum((gamma_part, delta_part), 'gx')]
    ppermute x12 -> x5, starting transfers between devices: 29.3 us -> 8.4 us  [the longest x1 3.88 us: shards(): rfc = lax.ppermute(corner, both, far_pairs)]
    pallas_call x0 -> x3, Pallas kernels: none -> 17.1 us  [the longest x1 10.9 us: shards(): pl.pallas_call(main_kernel, out_shape=(whole, whole, whole, whole, jax.Sh...]
    all_to_all x0 -> x1, blocking collectives: none -> 10.3 us  [shards(): got = lax.all_to_all(sent, both, 0, 0, tiled=True).reshape(n, 128)]
    reduce_sum x2 -> x0, other arithmetic: 9 us -> none  [inner_pair(): delta_part = jnp.sum(shadow * residual)]
    ppermute x12 -> x5, waiting for transfers between devices: 16.9 us -> 8.25 us  [the longest x1 6.36 us: shards(): rxs = lax.ppermute(xs, both, ynear_pairs)]
    concatenate x5 -> x3, other arithmetic: 4.32 us -> 0.09 us  [the longest x2 0.09 us: planes(): return jnp.concatenate([d, s], axis=0)]
    sub x1 -> x0, other arithmetic: 3.59 us -> none  [shards(): residual = residual - alpha_now * along]
  transfers between devices with their start and end apart: 12 -> 5, of which waited for: 7 -> 2; matrix products, arithmetic and copies ran while one was open for 1% -> 1% of each run, Pallas kernels for 0% -> 4%
where the time goes in v1:
time: 49.3 us; the launch traced here: 49.1 us
  Pallas kernels  17.1 us (35%)
  blocking collectives  10.3 us (21%)
  starting transfers between devices  8.4 us (17%)
  waiting for transfers between devices  8.25 us (17%)
  local copies, waits for them, and re-layouts  4.14 us (8%)
  between operations  0.74 us (2%)
    pallas_call x1, Pallas kernels, shards(): pl.pallas_call(main_kernel, out_shape=(whole, whole, whole, whole, jax.Sh...  10.9 us
    all_to_all x1, blocking collectives, shards(): got = lax.all_to_all(sent, both, 0, 0, tiled=True).reshape(n, 128)  10.3 us
    ppermute x1, waiting for transfers between devices, shards(): rxs = lax.ppermute(xs, both, ynear_pairs)  6.36 us
    pallas_call x1, Pallas kernels, shards(): pl.pallas_call(last_kernel, out_shape=(whole, whole), in_specs=[vmem] * 5...  4.24 us
    ppermute x1, starting transfers between devices, shards(): rfc = lax.ppermute(corner, both, far_pairs)  3.88 us
    ppermute x1, starting transfers between devices, shards(): far = lax.ppermute(planes(xodd == 1), both, far_pairs)  2.55 us
    unnamed x14, local copies, waits for them, and re-layouts  2.25 us
    pallas_call x1, Pallas kernels, shards(): pl.pallas_call(pack_rows, grid=(1,), out_shape=(rows, rows), in_specs=[sm...  1.92 us
  transfers between devices with their start and end apart: 5, of which 2 were waited for; matrix products, arithmetic and copies ran while one was open for 1% of the time, Pallas kernels for 4%

profile of v1, /device:TPU:0, one launch (start us, length us, event | category | flops | bytes accessed | tf_op | source)
XLA Modules:
  0.0 49.1 jit_solution(13242459270616291525)
XLA Ops:
  0.6 0.0 copy-start
  0.7 1.1 %constant_dynamic-slice_fusion.2 = (f32[2,128,256]{2,1,0:T(8,128)S(1)}, f32[2,128,256]{2,1,0:T(8,128)S(1)}) fusion(f32[8,128,256]{2,1,0:T(8,128)} %src.1, s32[]{:T(128)S(6)} %select_n.36, s32[]{:T(128)S(6)} %select_n.34), kind=kLoop, calls=%fused_computation.5 | loop fusion | bytes 1048584 | tf_op jit(solution)/shard_map/dynamic_slice | solution.py:252
  1.8 0.2 copy-done
  2.0 0.1 constant_dynamic-slice_fusion.3
  2.1 0.6 %collective-permute-start = (f32[5,128,256]{2,1,0:T(8,128)S(1)}, f32[5,128,256]{2,1,0:T(8,128)S(1)}, u32[]{:S(2)}, u32[]{:S(2)}) collective-permute-start(f32[5,128,256]{2,1,0:T(8,128)S(1)} %pad_maximum_fusion), channel_id=1, source_target_pairs={{0,4},{1,5},{2,6},{3,7},{4,0},{5,1},{6,2},{7,3},{8,12},{9,13},{10,... | collective-permute-start | bytes 1966088 | tf_op jit(solution)/shard_map/ppermute | solution.py:256
  2.7 2.6 %collective-permute-start.1 = (f32[5,128,256]{2,1,0:T(8,128)S(1)}, f32[5,128,256]{2,1,0:T(8,128)S(1)}, u32[]{:S(2)}, u32[]{:S(2)}) collective-permute-start(f32[5,128,256]{2,1,0:T(8,128)S(1)} %pad_maximum_fusion.1), channel_id=1, source_target_pairs={{0,1},{1,0},{2,3},{3,2},{4,8},{5,9},{6,10},{7,11},{8,4},{9,5},{10,... | collective-permute-start | bytes 1966088 | tf_op jit(solution)/shard_map/ppermute | solution.py:255
  5.3 0.7 %stack.43.par = s32[6]{0:T(128)} concatenate(s32[1]{0:T(128)} %bitcast, s32[1]{0:T(128)} %bitcast.1, s32[1]{0:T(128)} %bitcast.2, s32[1]{0:T(128)} %bitcast.3, s32[1]{0:T(128)} %bitcast.4, s32[1]{0:T(128)} %bitcast.5), dimensions={0} | concatenate | bytes 48 | tf_op jit(solution)/shard_map/stack | solution.py:248
  6.0 0.0 collective-permute-done.near
  6.0 0.0 copy-start.1
  6.0 0.8 %copy-done.1 = f32[5,128,256]{2,1,0:T(8,128)} copy-done((f32[5,128,256]{2,1,0:T(8,128)}, f32[5,128,256]{2,1,0:T(8,128)S(1)}, u32[]{:S(2)}) %copy-start.1) | copy-done | bytes 655384
  6.8 1.9 %pack_rows.1 = (f32[10,8,256]{2,1,0:T(8,128)}, f32[10,8,256]{2,1,0:T(8,128)}) custom-call(s32[6]{0:T(128)} %stack.43.par, f32[8,128,256]{2,1,0:T(8,128)} %dens.1, f32[8,128,256]{2,1,0:T(8,128)} %dens.1, f32[8,128,256]{2,1,0:T(8,128)} %src.1, f32[8,128,256]{2,1,0:T(8,128)} %src.1, f32[5,128,256]{2,1,0:T(8,128)} %copy-done.1), custom_call_target="tpu_custom_call" | custom-call | tf_op jit(solution)/shard_map/pack_rows/pallas_call | solution.py:263
  8.7 1.3 %collective-permute-start.2 = (f32[10,8,256]{2,1,0:T(8,128)}, f32[10,8,256]{2,1,0:T(8,128)S(1)}, u32[]{:S(2)}, u32[]{:S(2)}) collective-permute-start(f32[10,8,256]{2,1,0:T(8,128)} %get-tuple-element.9), channel_id=1, source_target_pairs={{0,1},{1,0},{2,3},{3,2},{4,5},{5,4},{6,7},{7,6},{8,9},{9,8},{10,11... | collective-permute-start | bytes 245768 | tf_op jit(solution)/shard_map/ppermute | solution.py:267
  10.0 0.1 collective-permute-start.3
  10.1 6.4 %collective-permute-done.2.rxs = f32[10,8,256]{2,1,0:T(8,128)S(1)} collective-permute-done((f32[10,8,256]{2,1,0:T(8,128)}, f32[10,8,256]{2,1,0:T(8,128)S(1)}, u32[]{:S(2)}, u32[]{:S(2)}) %collective-permute-start.2) | collective-permute-done | bytes 81952 | tf_op jit(solution)/shard_map/ppermute | solution.py:267
  16.5 0.0 copy-start.3
  16.5 0.0 collective-permute-done.3.rdg
  16.5 0.0 copy-start.4
  16.5 3.9 %collective-permute-start.4 = (f32[4,8,256]{2,1,0:T(8,128)S(1)}, f32[4,8,256]{2,1,0:T(8,128)S(1)}, u32[]{:S(2)}, u32[]{:S(2)}) collective-permute-start(f32[4,8,256]{2,1,0:T(8,128)S(1)} %pad_maximum_fusion.2), channel_id=1, source_target_pairs={{0,1},{1,0},{2,3},{3,2},{4,8},{5,9},{6,10},{7,11},{8,4},{9,5},{10,... | collective-permute-start | bytes 98312 | tf_op jit(solution)/shard_map/ppermute | solution.py:271
  20.4 0.0 collective-permute-done.1.far
  20.4 0.0 copy-start.2
  20.4 1.9 %collective-permute-done.4.rfc = f32[4,8,256]{2,1,0:T(8,128)S(1)} collective-permute-done((f32[4,8,256]{2,1,0:T(8,128)S(1)}, f32[4,8,256]{2,1,0:T(8,128)S(1)}, u32[]{:S(2)}, u32[]{:S(2)}) %collective-permute-start.4) | collective-permute-done | bytes 32800 | tf_op jit(solution)/shard_map/ppermute | solution.py:271
  22.3 0.0 copy-done.3
  22.3 0.0 copy-done.4
  22.3 0.0 copy-done.2
  22.3 0.0 copy-start.5
  22.3 0.6 %copy-done.5 = f32[4,8,256]{2,1,0:T(8,128)} copy-done((f32[4,8,256]{2,1,0:T(8,128)}, f32[4,8,256]{2,1,0:T(8,128)S(1)}, u32[]{:S(2)}) %copy-start.5) | copy-done | bytes 32792
  22.9 10.9 %main_kernel.1 = (f32[8,128,256]{2,1,0:T(8,128)}, f32[8,128,256]{2,1,0:T(8,128)}, f32[8,128,256]{2,1,0:T(8,128)}, f32[8,128,256]{2,1,0:T(8,128)}, f32[1,128]{1,0:T(1,128)}) custom-call(s32[6]{0:T(128)} %stack.43.par, f32[8,128,256]{2,1,0:T(8,128)} %dens.1, f32[8,128,256]{2,1,0:T(8,128)} %src.1, f32[5,128,256]{2,1,0:T(8,128)} %copy-done.1, ...), custom_call_target="tpu_custom_call" | custom-call | tf_op jit(solution)/shard_map/main_kernel/pallas_call | solution.py:275
  33.9 0.0 copy-start.6
  33.9 0.6 %copy-done.6 = f32[1,128]{1,0:T(1,128)S(1)} copy-done((f32[1,128]{1,0:T(1,128)S(1)}, f32[1,128]{1,0:T(1,128)}, u32[]{:S(2)}) %copy-start.6) | copy-done | bytes 536
  34.5 10.3 %all_to_all.5 = f32[32,1,128]{2,1,0:T(1,128)} all-to-all(f32[32,1,128]{2,1,0:T(1,128)S(1)} %broadcast_in_dim.9), channel_id=1, replica_groups=mesh['gx'=8,'gy'=4] {'gx','gy'}, dimensions={0} | all-to-all | bytes 32768 | tf_op jit(solution)/shard_map/all_to_all | solution.py:282
  44.8 4.2 %last_kernel.1 = (f32[8,128,256]{2,1,0:T(8,128)}, f32[8,128,256]{2,1,0:T(8,128)}) custom-call(f32[32,128]{1,0:T(8,128)} %bitcast.8, f32[8,128,256]{2,1,0:T(8,128)} %get-tuple-element.12.r0_ref, f32[8,128,256]{2,1,0:T(8,128)} %get-tuple-element.13.w0_ref, f32[8,128,256]{2,1,0:T(8,128)} %get-tuple-element.14.n0_ref, f32[8,128,256]{2,1,0:T(8,128)} %get-tuple-element.15.sc_ref), custom_call_target="tpu_custom_call" | custom-call | tf_op jit(solution)/shard_map/last_kernel/pallas_call | solution.py:283
  (6 shorter events, 0.1 us)
Async XLA Ops:
  0.6 1.4 %copy-start = (f32[8,128,256]{2,1,0:T(8,128)S(1)}, f32[8,128,256]{2,1,0:T(8,128)}, u32[]{:S(2)}) copy-start(f32[8,128,256]{2,1,0:T(8,128)} %dens.1) | copy-start | bytes 3145732
  2.1 3.8 %collective-permute-start = (f32[5,128,256]{2,1,0:T(8,128)S(1)}, f32[5,128,256]{2,1,0:T(8,128)S(1)}, u32[]{:S(2)}, u32[]{:S(2)}) collective-permute-start(f32[5,128,256]{2,1,0:T(8,128)S(1)} %pad_maximum_fusion), channel_id=1, source_target_pairs={{0,4},{1,5},{2,6},{3,7},{4,0},{5,1},{6,2},{7,3},{8,12},{9,13},{10,... | collective-permute-start | bytes 1966088 | tf_op jit(solution)/shard_map/ppermute | solution.py:256
  2.7 17.7 %collective-permute-start.1 = (f32[5,128,256]{2,1,0:T(8,128)S(1)}, f32[5,128,256]{2,1,0:T(8,128)S(1)}, u32[]{:S(2)}, u32[]{:S(2)}) collective-permute-start(f32[5,128,256]{2,1,0:T(8,128)S(1)} %pad_maximum_fusion.1), channel_id=1, source_target_pairs={{0,1},{1,0},{2,3},{3,2},{4,8},{5,9},{6,10},{7,11},{8,4},{9,5},{10,... | collective-permute-start | bytes 1966088 | tf_op jit(solution)/shard_map/ppermute | solution.py:255
  6.0 0.8 %copy-start.1 = (f32[5,128,256]{2,1,0:T(8,128)}, f32[5,128,256]{2,1,0:T(8,128)S(1)}, u32[]{:S(2)}) copy-start(f32[5,128,256]{2,1,0:T(8,128)S(1)} %collective-permute-done.near) | copy-start | bytes 1966084
  8.7 7.8 %collective-permute-start.2 = (f32[10,8,256]{2,1,0:T(8,128)}, f32[10,8,256]{2,1,0:T(8,128)S(1)}, u32[]{:S(2)}, u32[]{:S(2)}) collective-permute-start(f32[10,8,256]{2,1,0:T(8,128)} %get-tuple-element.9), channel_id=1, source_target_pairs={{0,1},{1,0},{2,3},{3,2},{4,5},{5,4},{6,7},{7,6},{8,9},{9,8},{10,11... | collective-permute-start | bytes 245768 | tf_op jit(solution)/shard_map/ppermute | solution.py:267
  10.0 6.5 %collective-permute-start.3 = (f32[10,8,256]{2,1,0:T(8,128)}, f32[10,8,256]{2,1,0:T(8,128)S(1)}, u32[]{:S(2)}, u32[]{:S(2)}) collective-permute-start(f32[10,8,256]{2,1,0:T(8,128)} %get-tuple-element.10), channel_id=1, source_target_pairs={{0,4},{1,2},{2,1},{3,7},{4,0},{5,6},{6,5},{7,3},{8,12},{9,10},{10,... | collective-permute-start | bytes 245768 | tf_op jit(solution)/shard_map/ppermute | solution.py:268
  16.5 5.8 %copy-start.3 = (f32[10,8,256]{2,1,0:T(8,128)}, f32[10,8,256]{2,1,0:T(8,128)S(1)}, u32[]{:S(2)}) copy-start(f32[10,8,256]{2,1,0:T(8,128)S(1)} %collective-permute-done.2.rxs) | copy-start | bytes 245764
  16.5 5.8 %copy-start.4 = (f32[10,8,256]{2,1,0:T(8,128)}, f32[10,8,256]{2,1,0:T(8,128)S(1)}, u32[]{:S(2)}) copy-start(f32[10,8,256]{2,1,0:T(8,128)S(1)} %collective-permute-done.3.rdg) | copy-start | bytes 245764
  16.5 5.8 %collective-permute-start.4 = (f32[4,8,256]{2,1,0:T(8,128)S(1)}, f32[4,8,256]{2,1,0:T(8,128)S(1)}, u32[]{:S(2)}, u32[]{:S(2)}) collective-permute-start(f32[4,8,256]{2,1,0:T(8,128)S(1)} %pad_maximum_fusion.2), channel_id=1, source_target_pairs={{0,1},{1,0},{2,3},{3,2},{4,8},{5,9},{6,10},{7,11},{8,4},{9,5},{10,... | collective-permute-start | bytes 98312 | tf_op jit(solution)/shard_map/ppermute | solution.py:271
  20.4 1.9 %copy-start.2 = (f32[5,128,256]{2,1,0:T(8,128)}, f32[5,128,256]{2,1,0:T(8,128)S(1)}, u32[]{:S(2)}) copy-start(f32[5,128,256]{2,1,0:T(8,128)S(1)} %collective-permute-done.1.far) | copy-start | bytes 1966084
  22.3 0.6 %copy-start.5 = (f32[4,8,256]{2,1,0:T(8,128)}, f32[4,8,256]{2,1,0:T(8,128)S(1)}, u32[]{:S(2)}) copy-start(f32[4,8,256]{2,1,0:T(8,128)S(1)} %collective-permute-done.4.rfc) | copy-start | bytes 98308
  33.9 0.6 %copy-start.6 = (f32[1,128]{1,0:T(1,128)S(1)}, f32[1,128]{1,0:T(1,128)}, u32[]{:S(2)}) copy-start(f32[1,128]{1,0:T(1,128)} %get-tuple-element.11) | copy-start | bytes 1540

commit v2 on v0

v2 whole, which is shorter than its diff:
```python
import functools

import jax
import jax.numpy as jnp
from jax import lax
from jax.experimental import pallas as pl
from jax.experimental.pallas import tpu as pltpu
from jax.sharding import PartitionSpec as P

ITERS = 2
TILE = 8
LANES = 128
OFF = 16
DEEP = 3
PART = 16
SUMS = 5
MIB = 1 << 20
VMEM = pltpu.VMEM


def swaps(nx, ny):
    at = lambda x, y: x * ny + y
    near, far, ynear, yfar = [], [], [], []
    for x in range(nx):
        for y in range(ny):
            near.append((at(x, y), at(x ^ 1, y)))
            other = x - 1 if x % 2 == 0 else x + 1
            inside = 0 <= other < nx
            far.append((at(x, y), at(other, y) if inside else at(x, y ^ 1)))
            ynear.append((at(x, y), at(x, y ^ 1)))
            beside = y - 1 if y % 2 == 0 else y + 1
            within = 0 <= beside < ny
            yfar.append((at(x, y), at(x, beside) if within else at(x ^ 1, y)))
    return near, far, ynear, yfar


def take_planes(par, dens, src, near_out, far_out):
    nx = dens.shape[0]
    xodd = par[0] == 1
    for out, first, second in ((near_out, jnp.where(xodd, 0, nx - 3), jnp.where(xodd, 0, nx - 2)),
                               (far_out, jnp.where(xodd, nx - 3, 0), jnp.where(xodd, nx - 2, 0))):
        for k in range(3):
            out[k] = dens[first + k]
        for k in range(2):
            out[3 + k] = src[second + k]


def take_rows(par, dens, src, near, xs_out, dg_out):
    nx, ny, nz = dens.shape
    row = lax.broadcasted_iota(jnp.int32, (TILE, nz), 0)
    xodd, yodd = par[0] == 1, par[1] == 1

    def put(k, d, s):
        down = jnp.where(row < 3, d(slice(0, TILE)), pltpu.roll(s(slice(0, TILE)), 4, 0))
        up = jnp.where(row > 4, d(slice(ny - TILE, ny)), pltpu.roll(s(slice(ny - TILE, ny)), 4, 0))
        xs_out[k] = jnp.where(yodd, down, up)
        dg_out[k] = jnp.where(yodd, up, down)

    for k in range(nx):
        put(k, lambda rows: dens[k, rows], lambda rows: src[k, rows])
    for k in range(2):
        put(nx + k, lambda rows: near[jnp.where(xodd, k + 1, k), rows], lambda rows: near[3 + k, rows])


def halves(nz):
    return [(h, slice(h * LANES, (h + 1) * LANES)) for h in range(nz // LANES)]


def put_plane(ref, e, rows, value):
    for h, lanes in halves(value.shape[-1]):
        ref[e, h, rows] = value[:, lanes]


def put_rows(dx, sx, e, low, high, ny):
    for value, at, in_rows in ((low, slice(OFF - TILE, OFF), None), (high, slice(OFF + ny, OFF + ny + TILE), None)):
        put_plane(dx, e, at, 0.5 * value)
        put_plane(sx, e, at, pltpu.roll(value, 4, 0))


def weigh(dx, sx, wx, wy, wz, sc, g0, lo, count):
    _, nh, rows, _ = dx.shape
    tiles = range(OFF - TILE, rows - OFF + TILE, TILE)
    lane = lax.broadcasted_iota(jnp.int32, (TILE, LANES), 1)
    inner, first = lane < LANES - 1, lane == 0
    for r in tiles:
        for h in range(nh):
            wx[lo - 1, h, pl.ds(r, TILE)] = 1.0 / (dx[lo - 1, h, pl.ds(r, TILE)] + dx[lo, h, pl.ds(r, TILE)])

    def plane(k, carry):
        e = lo + k
        for r in tiles:
            c = [dx[e, h, pl.ds(r, TILE)] for h in range(nh)]
            turned = [pltpu.roll(v, LANES - 1, 1) for v in c]
            z_up, z_in = [], []
            for h in range(nh):
                after = jnp.where(inner, turned[h], turned[h + 1] if h + 1 < nh else 0.0)
                w = 1.0 / (c[h] + after)
                z_up.append(w)
                z_in.append(w if h + 1 < nh else jnp.where(inner, w, 0.0))
                wz[e, h, pl.ds(r, TILE)] = z_in[h]
            back = [pltpu.roll(v, 1, 1) for v in z_in]
            for h in range(nh):
                x_up = 1.0 / (c[h] + dx[e + 1, h, pl.ds(r, TILE)])
                y_up = 1.0 / (c[h] + dx[e, h, pl.ds(r + 1, TILE)])
                wx[e, h, pl.ds(r, TILE)] = x_up
                wy[e, h, pl.ds(r, TILE)] = y_up
                z_down = jnp.where(first, back[h - 1] if h else 1.0 / c[0], back[h])
                diag = (x_up + wx[e - 1, h, pl.ds(r, TILE)]) + (y_up + wy[e, h, pl.ds(r - 1, TILE)]) + (z_up[h] + z_down)
                s = lax.rsqrt(diag)
                sc[e, h, pl.ds(r, TILE)] = s
                g0[e, h, pl.ds(r, TILE)] = s * (s * sx[e, h, pl.ds(r, TILE)])
        return carry

    lax.fori_loop(0, count, plane, 0)


def couple(g, wx, wy, wz, e, r, nh, inner, first):
    here = pl.ds(r, TILE)
    c = [g[e, h, here] for h in range(nh)]
    w = [wz[e, h, here] for h in range(nh)]
    ahead = [pltpu.roll(v, LANES - 1, 1) for v in c]
    behind = [pltpu.roll(a * b, 1, 1) for a, b in zip(w, c)]
    out = []
    for h in range(nh):
        t = wx[e, h, here] * g[e + 1, h, here] + wx[e - 1, h, here] * g[e - 1, h, here]
        t = t + (wy[e, h, here] * g[e, h, pl.ds(r + 1, TILE)] + wy[e, h, pl.ds(r - 1, TILE)] * g[e, h, pl.ds(r - 1, TILE)])
        after = jnp.where(inner, ahead[h], ahead[h + 1]) if h + 1 < nh else ahead[h]
        before = jnp.where(first, behind[h - 1], behind[h])
        out.append(t + (w[h] * after + before))
    return out


def apply_first(sx, wx, wy, wz, sc, g0, g1, w0, lo, count):
    _, nh, rows, _ = sx.shape
    lane = lax.broadcasted_iota(jnp.int32, (TILE, LANES), 1)
    inner, first = lane < LANES - 1, lane == 0

    def plane(k, carry):
        e = lo + k
        for r in range(OFF - TILE, rows - OFF + TILE, TILE):
            t = couple(g0, wx, wy, wz, e, r, nh, inner, first)
            for h in range(nh):
                s = sc[e, h, pl.ds(r, TILE)]
                v = s * sx[e, h, pl.ds(r, TILE)] - s * t[h]
                w0[e, h, pl.ds(r, TILE)] = v
                g1[e, h, pl.ds(r, TILE)] = s * v
        return carry

    lax.fori_loop(0, count, plane, 0)


def clear_outside(par, g1, e, has_x):
    _, nh, rows, _ = g1.shape
    zero = jnp.zeros((TILE, LANES), jnp.float32)
    for flag, at in ((par[4], OFF - TILE), (par[5], rows - OFF)):

        @pl.when(flag == 0)
        def _():
            for k in range(g1.shape[0]):
                for h in range(nh):
                    g1[k, h, pl.ds(at, TILE)] = zero

    @pl.when(has_x == 0)
    def _():
        for r in range(OFF - TILE, rows - OFF + TILE, TILE):
            for h in range(nh):
                g1[e, h, pl.ds(r, TILE)] = zero


def apply_second(sx, wx, wy, wz, sc, g1, w0, n0, lo, count, sums):
    _, nh, rows, _ = sx.shape
    lane = lax.broadcasted_iota(jnp.int32, (TILE, LANES), 1)
    inner, first = lane < LANES - 1, lane == 0

    def plane(k, sums):
        e = lo + k
        sums = list(sums)
        for r in range(OFF, rows - OFF, TILE):
            t = couple(g1, wx, wy, wz, e, r, nh, inner, first)
            for h in range(nh):
                s = sc[e, h, pl.ds(r, TILE)]
                a = s * sx[e, h, pl.ds(r, TILE)]
                b = w0[e, h, pl.ds(r, TILE)]
                c = b - s * t[h]
                n0[e, h, pl.ds(r, TILE)] = c
                for i, term in enumerate((a * a, b * a, b * b, c * b, c * a)):
                    sums[i] = sums[i] + term
        return tuple(sums)

    return lax.fori_loop(0, count, plane, tuple(sums))


def near_kernel(par, dens, src, near, rxs, rdg, dx, sx, wx, wy, wz, sc, g0, g1, w0, n0, mom):
    nx, ny, nz = dens.shape
    xodd, yodd = par[0] == 1, par[1] == 1
    has_near = jnp.where(xodd, par[2], par[3]) == 1
    has_down, has_up = par[4] == 1, par[5] == 1
    own = slice(OFF, OFF + ny)
    for k in range(nx):
        put_plane(dx, k + DEEP, own, 0.5 * dens[k])
        put_plane(sx, k + DEEP, own, src[k])
    beyond = jnp.where(xodd, 0, nx + 3)
    for k in range(3):
        put_plane(dx, beyond + k, own, jnp.where(has_near, 0.5 * near[k], 0.0))
    beyond = jnp.where(xodd, 1, nx + 3)
    for k in range(2):
        put_plane(sx, beyond + k, own, jnp.where(has_near, near[3 + k], 0.0))
    for k in range(nx + 2):
        a, b = rxs[k], rdg[k]
        low, high = jnp.where(yodd, a, b), jnp.where(yodd, b, a)
        inside = True if k < nx else has_near
        low = jnp.where(jnp.logical_and(has_down, inside), low, 0.0)
        high = jnp.where(jnp.logical_and(has_up, inside), high, 0.0)
        put_rows(dx, sx, k + DEEP if k < nx else beyond + k - nx, low, high, ny)
    weigh(dx, sx, wx, wy, wz, sc, g0, jnp.where(xodd, 1, 4), nx + 1)
    apply_first(sx, wx, wy, wz, sc, g0, g1, w0, jnp.where(xodd, 2, 5), nx - 1)
    clear_outside(par, g1, jnp.where(xodd, 2, nx + 3), jnp.where(xodd, par[2], par[3]))
    zero = jnp.zeros((TILE, LANES), jnp.float32)
    sums = apply_second(sx, wx, wy, wz, sc, g1, w0, n0, jnp.where(xodd, 3, 6), nx - 3, (zero,) * SUMS)
    for i in range(SUMS):
        mom[i] = sums[i]


def far_kernel(par, far, rfc, part, dx_in, sx_in, wx_in, wy_in, wz_in, sc_in, g0_in, g1_in, w0_in, n0_in,
               mom, dx, sx, wx, wy, wz, sc, g0, g1, w0, n0):
    ny, nz = far.shape[1:]
    nx = dx.shape[0] - 2 * DEEP
    xodd, yodd = par[0] == 1, par[1] == 1
    has = jnp.where(xodd, par[3], par[2])
    has_far = has == 1
    has_down, has_up = jnp.logical_and(has_far, par[4] == 1), jnp.logical_and(has_far, par[5] == 1)
    own = slice(OFF, OFF + ny)
    beyond = jnp.where(xodd, nx + 3, 0)
    for k in range(3):
        put_plane(dx, beyond + k, own, jnp.where(has_far, 0.5 * far[k], 0.0))
    beyond = jnp.where(xodd, nx + 3, 1)
    for k in range(2):
        put_plane(sx, beyond + k, own, jnp.where(has_far, far[3 + k], 0.0))
        a, b = rfc[k], rfc[2 + k]
        low, high = jnp.where(yodd, a, b), jnp.where(yodd, b, a)
        put_rows(dx, sx, beyond + k, jnp.where(has_down, low, 0.0), jnp.where(has_up, high, 0.0), ny)
    weigh(dx, sx, wx, wy, wz, sc, g0, jnp.where(xodd, nx + 2, 1), 3)
    apply_first(sx, wx, wy, wz, sc, g0, g1, w0, jnp.where(xodd, nx + 1, 2), 3)
    clear_outside(par, g1, jnp.where(xodd, nx + 3, 2), has)
    sums = apply_second(sx, wx, wy, wz, sc, g1, w0, n0, jnp.where(xodd, nx, 3), 3, [part[i] for i in range(SUMS)])
    place = lax.broadcasted_iota(jnp.int32, (1, LANES), 1) // PART
    out = jnp.zeros((1, LANES), jnp.float32)
    for k, v in enumerate(sums):
        p = jnp.sum(v, axis=0, keepdims=True)
        width = LANES // 2
        while width >= PART:
            p = p + pltpu.roll(p, width, 1)
            width //= 2
        out = jnp.where(place == k, p, out)
    mom[...] = out


def last_kernel(mom, sx, sc, w0, n0, p_out, r_out):
    place = lax.broadcasted_iota(jnp.int32, mom.shape, 1) // PART
    m = mom[...]

    def whole(v):
        return jnp.sum(jnp.sum(v, axis=0, keepdims=True), axis=1, keepdims=True)

    def lanes(k):
        return pltpu.roll(m, (LANES - k * PART) % LANES, 1) if k else m

    head = place == 0
    m0, m1, m2, m3, m4 = (jnp.where(head, lanes(k), 0.0) for k in range(SUMS))
    gamma0 = whole(m0)
    delta0 = whole(m1)
    a0 = gamma0 / delta0
    gamma1 = whole(m0 - a0 * (m1 + m1 - a0 * m2))
    delta1 = whole(m1 - a0 * (m4 + m2 - a0 * m3))
    b1 = gamma1 / gamma0
    a1 = gamma1 / (delta1 - b1 * gamma1 / a0)
    nx, ny, nz = p_out.shape
    a0, b1, a1 = (jnp.broadcast_to(v, (TILE, LANES)) for v in (a0, b1, a1))

    def plane(i, carry):
        e = i + DEEP
        for r in range(0, ny, TILE):
            for h, at in halves(nz):
                here = pl.ds(OFF + r, TILE)
                s = sc[e, h, here]
                r0 = s * sx[e, h, here]
                v0 = w0[e, h, here]
                r1 = r0 - a0 * v0
                along = (v0 - a0 * n0[e, h, here]) + b1 * v0
                direction = r1 + b1 * r0
                p_out[i, pl.ds(r, TILE), at] = s * (a0 * r0 + a1 * direction)
                r_out[i, pl.ds(r, TILE), at] = r1 - a1 * along
        return carry

    lax.fori_loop(0, nx, plane, 0)


def shards(nx_dev, ny_dev, source, density):
    both = ("gx", "gy")
    near_pairs, far_pairs, ynear_pairs, yfar_pairs = swaps(nx_dev, ny_dev)
    nx, ny, nz = density.shape
    ix, iy = lax.axis_index("gx"), lax.axis_index("gy")
    xodd = ix % 2
    flags = [xodd, iy % 2, ix > 0, ix < nx_dev - 1, iy > 0, iy < ny_dev - 1]
    par = jnp.stack([jnp.asarray(f, jnp.int32) for f in flags])
    smem = pl.BlockSpec(memory_space=pltpu.SMEM)
    vmem = pl.BlockSpec(memory_space=VMEM)

    def call(body, n_in, outs, limit, **more):
        specs = [smem] + [vmem] * (n_in - 1)
        return pl.pallas_call(
            body, out_shape=outs, in_specs=specs, out_specs=jax.tree.map(lambda _: vmem, outs), name=body.__name__,
            compiler_params=pltpu.CompilerParams(vmem_limit_bytes=limit * MIB), **more,
        )

    planes = VMEM((5, ny, nz), jnp.float32)
    near, far = call(take_planes, 3, (planes, planes), 8)(par, density, source)
    near = lax.ppermute(near, both, near_pairs)
    far = lax.ppermute(far, both, far_pairs)
    rows = VMEM((nx + 2, TILE, nz), jnp.float32)
    xs, dg = call(take_rows, 4, (rows, rows), 8)(par, density, source, near)
    rxs = lax.ppermute(xs, both, ynear_pairs)
    rdg = lax.ppermute(dg, both, yfar_pairs)
    begin = jnp.where(xodd == 1, nx - 2, 0)
    corner = jnp.concatenate([lax.dynamic_slice_in_dim(v, begin, 2, 0) for v in (rxs, rdg)], axis=0)
    rfc = lax.ppermute(corner, both, far_pairs)

    ext = VMEM((nx + 2 * DEEP, nz // LANES, ny + 2 * OFF, LANES), jnp.float32)
    *held, part = call(near_kernel, 6, (ext,) * 10 + (VMEM((SUMS, TILE, LANES), jnp.float32),), 8)(par, density, source, near, rxs, rdg)
    mom, *held = call(far_kernel, 14, (VMEM((1, LANES), jnp.float32),) + (ext,) * 10, 8, input_output_aliases={4 + k: 1 + k for k in range(10)})(
        par, far, rfc, part, *held)
    dx, sx, wx, wy, wz, sc, g0, g1, w0, n0 = held

    n = nx_dev * ny_dev
    sent = jnp.broadcast_to(mom[None], (n, 1, LANES))
    got = lax.all_to_all(sent, both, 0, 0, tiled=True).reshape(n, LANES)
    whole = jax.ShapeDtypeStruct(density.shape, jnp.float32)
    return pl.pallas_call(
        last_kernel, out_shape=(whole, whole), in_specs=[vmem] * 5, out_specs=(vmem, vmem), name="last_kernel",
        compiler_params=pltpu.CompilerParams(vmem_limit_bytes=8 * MIB),
    )(got, sx, sc, w0, n0)


def solution(mesh):
    spec = P("gx", "gy", None)
    body = functools.partial(shards, mesh.shape["gx"], mesh.shape["gy"])
    return jax.shard_map(body, mesh=mesh, in_specs=(spec, spec), out_specs=(spec, spec), check_vma=False)
```

time: 126 us -> 42.2 us (0.33)
  blocking collectives: 51.4 us -> 9.66 us
  starting transfers between devices: 29.3 us -> 8.91 us
  other arithmetic: 19.3 us -> 0.01 us
  Pallas kernels: 0 us -> 12 us
  waiting for transfers between devices: 16.9 us -> 7.5 us
  between operations: 6.33 us -> 0.71 us
    psum x4 -> x0, blocking collectives: 51.4 us -> none  [the longest x2 31.7 us: inner_pair(): first = lax.psum((gamma_part, delta_part), 'gx')]
    ppermute x12 -> x5, starting transfers between devices: 29.3 us -> 8.91 us  [the longest x1 3.84 us: shards(): rfc = lax.ppermute(corner, both, far_pairs)]
    pallas_call x0 -> x5, Pallas kernels: none -> 12 us  [the longest x1 4.72 us: shards(): call(near_kernel, 6, (ext,) * 10 + (VMEM((SUMS, TILE, LANES), jnp.float32...]
    all_to_all x0 -> x1, blocking collectives: none -> 9.66 us  [shards(): got = lax.all_to_all(sent, both, 0, 0, tiled=True).reshape(n, LANES)]
    ppermute x12 -> x5, waiting for transfers between devices: 16.9 us -> 7.5 us  [the longest x1 7.49 us: shards(): rxs = lax.ppermute(xs, both, ynear_pairs)]
    reduce_sum x2 -> x0, other arithmetic: 9 us -> none  [inner_pair(): delta_part = jnp.sum(shadow * residual)]
    concatenate x5 -> x1, other arithmetic: 4.32 us -> 0.01 us  [shards(): jnp.concatenate([lax.dynamic_slice_in_dim(v, begin, 2, 0) for v in (rxs,...]
    sub x1 -> x0, other arithmetic: 3.59 us -> none  [shards(): residual = residual - alpha_now * along]
  transfers between devices with their start and end apart: 12 -> 5, of which waited for: 7 -> 1; matrix products, arithmetic and copies ran while one was open for 1% -> 0% of each run, Pallas kernels for 0% -> 14%
where the time goes in v2:
time: 42.2 us; the launch traced here: 42 us
  Pallas kernels  12 us (28%)
  blocking collectives  9.66 us (23%)
  starting transfers between devices  8.91 us (21%)
  waiting for transfers between devices  7.5 us (18%)
  local copies, waits for them, and re-layouts  3.18 us (8%)
  between operations  0.71 us (2%)
    all_to_all x1, blocking collectives, shards(): got = lax.all_to_all(sent, both, 0, 0, tiled=True).reshape(n, LANES)  9.66 us
    ppermute x1, waiting for transfers between devices, shards(): rxs = lax.ppermute(xs, both, ynear_pairs)  7.49 us
    pallas_call x1, Pallas kernels, shards(): call(near_kernel, 6, (ext,) * 10 + (VMEM((SUMS, TILE, LANES), jnp.float32...  4.72 us
    ppermute x1, starting transfers between devices, shards(): rfc = lax.ppermute(corner, both, far_pairs)  3.84 us
    unnamed x10, local copies, waits for them, and re-layouts  3.08 us
    pallas_call x1, Pallas kernels, shards(): call(far_kernel, 14, (VMEM((1, LANES), jnp.float32),) + (ext,) * 10, 8, i...  2.51 us
    ppermute x1, starting transfers between devices, shards(): far = lax.ppermute(far, both, far_pairs)  2.48 us
    pallas_call x1, Pallas kernels, shards(): pl.pallas_call(last_kernel, out_shape=(whole, whole), in_specs=[vmem] * 5...  2.13 us
  transfers between devices with their start and end apart: 5, of which 1 were waited for; matrix products, arithmetic and copies ran while one was open for 0% of the time, Pallas kernels for 14%

profile of v2, /device:TPU:0, one launch (start us, length us, event | category | flops | bytes accessed | tf_op | source)
XLA Modules:
  0.0 42.0 jit_solution(15955041847330489376)
XLA Ops:
  0.7 0.1 stack.43.par
  0.7 0.0 copy-start
  0.7 1.2 %copy-done = f32[8,128,256]{2,1,0:T(8,128)S(1)} copy-done((f32[8,128,256]{2,1,0:T(8,128)S(1)}, f32[8,128,256]{2,1,0:T(8,128)}, u32[]{:S(2)}) %copy-start) | copy-done | bytes 1048600
  2.0 0.0 copy-start.2
  2.0 1.2 %copy-done.2 = f32[8,128,256]{2,1,0:T(8,128)S(1)} copy-done((f32[8,128,256]{2,1,0:T(8,128)S(1)}, f32[8,128,256]{2,1,0:T(8,128)}, u32[]{:S(2)}) %copy-start.2) | copy-done | bytes 1048600
  3.2 0.0 copy-start.1
  3.2 0.0 copy-start.3
  3.2 1.5 %take_planes.1 = (f32[5,128,256]{2,1,0:T(8,128)S(1)}, f32[5,128,256]{2,1,0:T(8,128)}) custom-call(s32[6]{0:T(128)S(1)} %stack.43.par, f32[8,128,256]{2,1,0:T(8,128)S(1)} %copy-done, f32[8,128,256]{2,1,0:T(8,128)S(1)} %copy-done.2), custom_call_target="tpu_custom_call" | custom-call | tf_op jit(solution)/shard_map/take_planes/pallas_call | solution.py:317
  4.7 0.5 %collective-permute-start.1 = (f32[5,128,256]{2,1,0:T(8,128)S(1)}, f32[5,128,256]{2,1,0:T(8,128)S(1)}, u32[]{:S(2)}, u32[]{:S(2)}) collective-permute-start(f32[5,128,256]{2,1,0:T(8,128)S(1)} %get-tuple-element.23), channel_id=1, source_target_pairs={{0,4},{1,5},{2,6},{3,7},{4,0},{5,1},{6,2},{7,3},{8,12},{9,13},{10,... | collective-permute-start | bytes 1966088 | tf_op jit(solution)/shard_map/ppermute | solution.py:318
  5.2 2.5 %collective-permute-start = (f32[5,128,256]{2,1,0:T(8,128)}, f32[5,128,256]{2,1,0:T(8,128)S(1)}, u32[]{:S(2)}, u32[]{:S(2)}) collective-permute-start(f32[5,128,256]{2,1,0:T(8,128)} %get-tuple-element.22), channel_id=1, source_target_pairs={{0,1},{1,0},{2,3},{3,2},{4,8},{5,9},{6,10},{7,11},{8,4},{9,5},{10,... | collective-permute-start | bytes 1966088 | tf_op jit(solution)/shard_map/ppermute | solution.py:319
  7.6 0.0 collective-permute-done.1.near
  7.6 1.2 %take_rows.1 = (f32[10,8,256]{2,1,0:T(8,128)}, f32[10,8,256]{2,1,0:T(8,128)S(1)}) custom-call(s32[6]{0:T(128)S(1)} %stack.43.par, f32[8,128,256]{2,1,0:T(8,128)S(1)} %copy-done, f32[8,128,256]{2,1,0:T(8,128)S(1)} %copy-done.2, f32[5,128,256]{2,1,0:T(8,128)S(1)} %collective-permute-done.1.near), custom_call_target="tpu_custom_call" | custom-call | tf_op jit(solution)/shard_map/take_rows/pallas_call | solution.py:321
  8.8 0.0 copy-start.4
  8.8 0.6 %copy-done.4 = f32[10,8,256]{2,1,0:T(8,128)} copy-done((f32[10,8,256]{2,1,0:T(8,128)}, f32[10,8,256]{2,1,0:T(8,128)S(1)}, u32[]{:S(2)}) %copy-start.4) | copy-done | bytes 81944
  9.5 2.1 %collective-permute-start.2 = (f32[10,8,256]{2,1,0:T(8,128)}, f32[10,8,256]{2,1,0:T(8,128)S(1)}, u32[]{:S(2)}, u32[]{:S(2)}) collective-permute-start(f32[10,8,256]{2,1,0:T(8,128)} %get-tuple-element.24), channel_id=1, source_target_pairs={{0,1},{1,0},{2,3},{3,2},{4,5},{5,4},{6,7},{7,6},{8,9},{9,8},{10,11... | collective-permute-start | bytes 245768 | tf_op jit(solution)/shard_map/ppermute | solution.py:322
  11.6 0.0 collective-permute-start.3
  11.6 7.5 %collective-permute-done.2.rxs = f32[10,8,256]{2,1,0:T(8,128)S(1)} collective-permute-done((f32[10,8,256]{2,1,0:T(8,128)}, f32[10,8,256]{2,1,0:T(8,128)S(1)}, u32[]{:S(2)}, u32[]{:S(2)}) %collective-permute-start.2) | collective-permute-done | bytes 81952 | tf_op jit(solution)/shard_map/ppermute | solution.py:322
  19.0 0.0 collective-permute-done.3.rdg
  19.1 3.8 %collective-permute-start.4 = (f32[4,8,256]{2,1,0:T(8,128)S(1)}, f32[4,8,256]{2,1,0:T(8,128)S(1)}, u32[]{:S(2)}, u32[]{:S(2)}) collective-permute-start(f32[4,8,256]{2,1,0:T(8,128)S(1)} %pad_maximum_fusion), channel_id=1, source_target_pairs={{0,1},{1,0},{2,3},{3,2},{4,8},{5,9},{6,10},{7,11},{8,4},{9,5},{10,... | collective-permute-start | bytes 98312 | tf_op jit(solution)/shard_map/ppermute | solution.py:326
  22.9 0.0 copy-done.1
  22.9 0.0 copy-done.3
  22.9 4.7 %near_kernel.1 = (f32[14,2,160,128]{3,2,1,0:T(8,128)S(1)}, f32[14,2,160,128]{3,2,1,0:T(8,128)S(1)}, f32[14,2,160,128]{3,2,1,0:T(8,128)S(1)}, f32[14,2,160,128]{3...) custom-call(s32[6]{0:T(128)S(1)} %stack.43.par, ...), custom_call_target="tpu_custom_call" | custom-call | tf_op jit(solution)/shard_map/near_kernel/pallas_call | solution.py:329
  27.6 0.0 collective-permute-done.far
  27.7 0.0 collective-permute-done.4.rfc
  27.7 2.5 %far_kernel.1 = (f32[1,128]{1,0:T(1,128)S(1)}, f32[14,2,160,128]{3,2,1,0:T(8,128)S(1)}, f32[14,2,160,128]{3,2,1,0:T(8,128)S(1)}, f32[14,2,160,128]{3,2,1,0:T(8,1...) custom-call(s32[6]{0:T(128)S(1)} %stack.43.par, ...), custom_call_target="tpu_custom_call", output_to_operand_aliasing={{1}: (4, {}), {2}: (5, {}), {3}: (6, {}), {4}: (7, {}), {5}... | custom-call | tf_op jit(solution)/shard_map/far_kernel/pallas_call | solution.py:330
  30.2 9.7 %all_to_all.5 = f32[32,1,128]{2,1,0:T(1,128)S(1)} all-to-all(f32[32,1,128]{2,1,0:T(1,128)S(1)} %broadcast_in_dim.9), channel_id=1, replica_groups=mesh['gx'=8,'gy'=4] {'gx','gy'}, dimensions={0} | all-to-all | bytes 32768 | tf_op jit(solution)/shard_map/all_to_all | solution.py:336
  39.8 2.1 %last_kernel.1 = (f32[8,128,256]{2,1,0:T(8,128)}, f32[8,128,256]{2,1,0:T(8,128)}) custom-call(f32[32,128]{1,0:T(8,128)S(1)} %bitcast.8, f32[14,2,160,128]{3,2,1,0:T(8,128)S(1)} %get-tuple-element.38.sx, f32[14,2,160,128]{3,2,1,0:T(8,128)S(1)} %get-tuple-element.39.sc, f32[14,2,160,128]{3,2,1,0:T(8,128)S(1)} %get-tuple-element.40.w0, ...), custom_call_target="tpu_custom_call" | custom-call | tf_op jit(solution)/shard_map/last_kernel/pallas_call | solution.py:338
  (4 shorter events, 0.0 us)
Async XLA Ops:
  0.7 1.2 %copy-start = (f32[8,128,256]{2,1,0:T(8,128)S(1)}, f32[8,128,256]{2,1,0:T(8,128)}, u32[]{:S(2)}) copy-start(f32[8,128,256]{2,1,0:T(8,128)} %dens.5) | copy-start | bytes 3145732
  2.0 1.2 %copy-start.2 = (f32[8,128,256]{2,1,0:T(8,128)S(1)}, f32[8,128,256]{2,1,0:T(8,128)}, u32[]{:S(2)}) copy-start(f32[8,128,256]{2,1,0:T(8,128)} %src.5) | copy-start | bytes 3145732
  3.2 19.7 %copy-start.1 = (f32[8,128,256]{2,1,0:T(8,128)S(1)}, f32[8,128,256]{2,1,0:T(8,128)}, u32[]{:S(2)}) copy-start(f32[8,128,256]{2,1,0:T(8,128)} %dens.5) | copy-start | bytes 3145732
  3.2 19.7 %copy-start.3 = (f32[8,128,256]{2,1,0:T(8,128)S(1)}, f32[8,128,256]{2,1,0:T(8,128)}, u32[]{:S(2)}) copy-start(f32[8,128,256]{2,1,0:T(8,128)} %src.5) | copy-start | bytes 3145732
  4.7 3.0 %collective-permute-start.1 = (f32[5,128,256]{2,1,0:T(8,128)S(1)}, f32[5,128,256]{2,1,0:T(8,128)S(1)}, u32[]{:S(2)}, u32[]{:S(2)}) collective-permute-start(f32[5,128,256]{2,1,0:T(8,128)S(1)} %get-tuple-element.23), channel_id=1, source_target_pairs={{0,4},{1,5},{2,6},{3,7},{4,0},{5,1},{6,2},{7,3},{8,12},{9,13},{10,... | collective-permute-start | bytes 1966088 | tf_op jit(solution)/shard_map/ppermute | solution.py:318
  5.2 22.5 %collective-permute-start = (f32[5,128,256]{2,1,0:T(8,128)}, f32[5,128,256]{2,1,0:T(8,128)S(1)}, u32[]{:S(2)}, u32[]{:S(2)}) collective-permute-start(f32[5,128,256]{2,1,0:T(8,128)} %get-tuple-element.22), channel_id=1, source_target_pairs={{0,1},{1,0},{2,3},{3,2},{4,8},{5,9},{6,10},{7,11},{8,4},{9,5},{10,... | collective-permute-start | bytes 1966088 | tf_op jit(solution)/shard_map/ppermute | solution.py:319
  8.8 0.6 %copy-start.4 = (f32[10,8,256]{2,1,0:T(8,128)}, f32[10,8,256]{2,1,0:T(8,128)S(1)}, u32[]{:S(2)}) copy-start(f32[10,8,256]{2,1,0:T(8,128)S(1)} %get-tuple-element.25) | copy-start | bytes 245764
  9.5 9.6 %collective-permute-start.2 = (f32[10,8,256]{2,1,0:T(8,128)}, f32[10,8,256]{2,1,0:T(8,128)S(1)}, u32[]{:S(2)}, u32[]{:S(2)}) collective-permute-start(f32[10,8,256]{2,1,0:T(8,128)} %get-tuple-element.24), channel_id=1, source_target_pairs={{0,1},{1,0},{2,3},{3,2},{4,5},{5,4},{6,7},{7,6},{8,9},{9,8},{10,11... | collective-permute-start | bytes 245768 | tf_op jit(solution)/shard_map/ppermute | solution.py:322
  11.6 7.5 %collective-permute-start.3 = (f32[10,8,256]{2,1,0:T(8,128)}, f32[10,8,256]{2,1,0:T(8,128)S(1)}, u32[]{:S(2)}, u32[]{:S(2)}) collective-permute-start(f32[10,8,256]{2,1,0:T(8,128)} %copy-done.4), channel_id=1, source_target_pairs={{0,4},{1,2},{2,1},{3,7},{4,0},{5,6},{6,5},{7,3},{8,12},{9,10},{10,... | collective-permute-start | bytes 245768 | tf_op jit(solution)/shard_map/ppermute | solution.py:323
  19.1 8.6 %collective-permute-start.4 = (f32[4,8,256]{2,1,0:T(8,128)S(1)}, f32[4,8,256]{2,1,0:T(8,128)S(1)}, u32[]{:S(2)}, u32[]{:S(2)}) collective-permute-start(f32[4,8,256]{2,1,0:T(8,128)S(1)} %pad_maximum_fusion), channel_id=1, source_target_pairs={{0,1},{1,0},{2,3},{3,2},{4,8},{5,9},{6,10},{7,11},{8,4},{9,5},{10,... | collective-permute-start | bytes 98312 | tf_op jit(solution)/shard_map/ppermute | solution.py:326

commit v3 on v2

--- a/solution.py
+++ b/solution.py
@@ -7,7 +7,7 @@
 from jax.experimental.pallas import tpu as pltpu
 from jax.sharding import PartitionSpec as P
 
-ITERS = 2
+
 TILE = 8
 LANES = 128
 OFF = 16
@@ -34,32 +34,30 @@
     return near, far, ynear, yfar
 
 
-def take_planes(par, dens, src, near_out, far_out):
-    nx = dens.shape[0]
-    xodd = par[0] == 1
-    for out, first, second in ((near_out, jnp.where(xodd, 0, nx - 3), jnp.where(xodd, 0, nx - 2)),
-                               (far_out, jnp.where(xodd, nx - 3, 0), jnp.where(xodd, nx - 2, 0))):
-        for k in range(3):
-            out[k] = dens[first + k]
-        for k in range(2):
-            out[3 + k] = src[second + k]
-
-
-def take_rows(par, dens, src, near, xs_out, dg_out):
+def take_kernel(par, dens, src, near_out, far_out, xs_out, dg_out, dlo, dhi, slo, shi, sems):
     nx, ny, nz = dens.shape
+    xodd, yodd = par[0] == 1, par[1] == 1
+    copies = [
+        (dens.at[:, pl.ds(0, TILE)], dlo), (dens.at[:, pl.ds(ny - TILE, TILE)], dhi),
+        (src.at[:, pl.ds(0, TILE)], slo), (src.at[:, pl.ds(ny - TILE, TILE)], shi),
+    ]
+    for out, d, s in ((near_out, jnp.where(xodd, 0, nx - 3), jnp.where(xodd, 0, nx - 2)),
+                      (far_out, jnp.where(xodd, nx - 3, 0), jnp.where(xodd, nx - 2, 0))):
+        copies += [(dens.at[pl.ds(d + k, 1)], out.at[pl.ds(k, 1)]) for k in range(3)]
+        copies += [(src.at[pl.ds(s + k, 1)], out.at[pl.ds(3 + k, 1)]) for k in range(2)]
+    copies = [pltpu.make_async_copy(a, b, sems.at[i]) for i, (a, b) in enumerate(copies)]
+    for copy in copies:
+        copy.start()
+    for copy in copies[:4]:
+        copy.wait()
     row = lax.broadcasted_iota(jnp.int32, (TILE, nz), 0)
-    xodd, yodd = par[0] == 1, par[1] == 1
-
-    def put(k, d, s):
-        down = jnp.where(row < 3, d(slice(0, TILE)), pltpu.roll(s(slice(0, TILE)), 4, 0))
-        up = jnp.where(row > 4, d(slice(ny - TILE, ny)), pltpu.roll(s(slice(ny - TILE, ny)), 4, 0))
+    for k in range(nx):
+        down = jnp.where(row < 3, dlo[k], pltpu.roll(slo[k], 4, 0))
+        up = jnp.where(row > 4, dhi[k], pltpu.roll(shi[k], 4, 0))
         xs_out[k] = jnp.where(yodd, down, up)
         dg_out[k] = jnp.where(yodd, up, down)
-
-    for k in range(nx):
-        put(k, lambda rows: dens[k, rows], lambda rows: src[k, rows])
-    for k in range(2):
-        put(nx + k, lambda rows: near[jnp.where(xodd, k + 1, k), rows], lambda rows: near[3 + k, rows])
+    for copy in copies[4:]:
+        copy.wait()
 
 
 def halves(nz):
@@ -72,7 +70,7 @@
 
 
 def put_rows(dx, sx, e, low, high, ny):
-    for value, at, in_rows in ((low, slice(OFF - TILE, OFF), None), (high, slice(OFF + ny, OFF + ny + TILE), None)):
+    for value, at in ((low, slice(OFF - TILE, OFF)), (high, slice(OFF + ny, OFF + ny + TILE))):
         put_plane(dx, e, at, 0.5 * value)
         put_plane(sx, e, at, pltpu.roll(value, 4, 0))
 
@@ -105,7 +103,8 @@
                 wx[e, h, pl.ds(r, TILE)] = x_up
                 wy[e, h, pl.ds(r, TILE)] = y_up
                 z_down = jnp.where(first, back[h - 1] if h else 1.0 / c[0], back[h])
-                diag = (x_up + wx[e - 1, h, pl.ds(r, TILE)]) + (y_up + wy[e, h, pl.ds(r - 1, TILE)]) + (z_up[h] + z_down)
+                y_down = 1.0 / (c[h] + dx[e, h, pl.ds(r - 1, TILE)])
+                diag = (x_up + wx[e - 1, h, pl.ds(r, TILE)]) + (y_up + y_down) + (z_up[h] + z_down)
                 s = lax.rsqrt(diag)
                 sc[e, h, pl.ds(r, TILE)] = s
                 g0[e, h, pl.ds(r, TILE)] = s * (s * sx[e, h, pl.ds(r, TILE)])
@@ -190,8 +189,8 @@
     return lax.fori_loop(0, count, plane, tuple(sums))
 
 
-def near_kernel(par, dens, src, near, rxs, rdg, dx, sx, wx, wy, wz, sc, g0, g1, w0, n0, mom):
-    nx, ny, nz = dens.shape
+def near_kernel(par, dens, src, near, rxs, rdg, rnc, dx, sx, wx, wy, wz, sc, g0, g1, w0, n0, mom):
+    nx, ny, _ = dens.shape
     xodd, yodd = par[0] == 1, par[1] == 1
     has_near = jnp.where(xodd, par[2], par[3]) == 1
     has_down, has_up = par[4] == 1, par[5] == 1
@@ -206,9 +205,9 @@
     for k in range(2):
         put_plane(sx, beyond + k, own, jnp.where(has_near, near[3 + k], 0.0))
     for k in range(nx + 2):
-        a, b = rxs[k], rdg[k]
+        inside = True if k < nx else has_near
+        a, b = (rxs[k], rdg[k]) if k < nx else (rnc[k - nx], rnc[2 + k - nx])
         low, high = jnp.where(yodd, a, b), jnp.where(yodd, b, a)
-        inside = True if k < nx else has_near
         low = jnp.where(jnp.logical_and(has_down, inside), low, 0.0)
         high = jnp.where(jnp.logical_and(has_up, inside), high, 0.0)
         put_rows(dx, sx, k + DEEP if k < nx else beyond + k - nx, low, high, ny)
@@ -223,7 +222,7 @@
 
 def far_kernel(par, far, rfc, part, dx_in, sx_in, wx_in, wy_in, wz_in, sc_in, g0_in, g1_in, w0_in, n0_in,
                mom, dx, sx, wx, wy, wz, sc, g0, g1, w0, n0):
-    ny, nz = far.shape[1:]
+    ny, _ = far.shape[1:]
     nx = dx.shape[0] - 2 * DEEP
     xodd, yodd = par[0] == 1, par[1] == 1
     has = jnp.where(xodd, par[3], par[2])
@@ -255,7 +254,7 @@
     mom[...] = out
 
 
-def last_kernel(mom, sx, sc, w0, n0, p_out, r_out):
+def last_kernel(mom, sx, sc, w0, n0, p_out, r_out, p_buf, r_buf, sems):
     place = lax.broadcasted_iota(jnp.int32, mom.shape, 1) // PART
     m = mom[...]
 
@@ -275,7 +274,12 @@
     b1 = gamma1 / gamma0
     a1 = gamma1 / (delta1 - b1 * gamma1 / a0)
     nx, ny, nz = p_out.shape
-    a0, b1, a1 = (jnp.broadcast_to(v, (TILE, LANES)) for v in (a0, b1, a1))
+    c = jnp.broadcast_to(a0 + (a1 + a1 * b1), (TILE, LANES))
+    d = jnp.broadcast_to(a0 * a1, (TILE, LANES))
+
+    def out(i):
+        return (pltpu.make_async_copy(p_buf.at[pl.ds(i, 1)], p_out.at[pl.ds(i, 1)], sems.at[0, i]),
+                pltpu.make_async_copy(r_buf.at[pl.ds(i, 1)], r_out.at[pl.ds(i, 1)], sems.at[1, i]))
 
     def plane(i, carry):
         e = i + DEEP
@@ -285,14 +289,16 @@
                 s = sc[e, h, here]
                 r0 = s * sx[e, h, here]
                 v0 = w0[e, h, here]
-                r1 = r0 - a0 * v0
-                along = (v0 - a0 * n0[e, h, here]) + b1 * v0
-                direction = r1 + b1 * r0
-                p_out[i, pl.ds(r, TILE), at] = s * (a0 * r0 + a1 * direction)
-                r_out[i, pl.ds(r, TILE), at] = r1 - a1 * along
+                p_buf[i, pl.ds(r, TILE), at] = s * (c * r0 - d * v0)
+                r_buf[i, pl.ds(r, TILE), at] = r0 - c * v0 + d * n0[e, h, here]
+        for copy in out(i):
+            copy.start()
         return carry
 
     lax.fori_loop(0, nx, plane, 0)
+    for i in range(nx):
+        for copy in out(i):
+            copy.wait()
 
 
 def shards(nx_dev, ny_dev, source, density):
@@ -309,34 +315,46 @@
     def call(body, n_in, outs, limit, **more):
         specs = [smem] + [vmem] * (n_in - 1)
         return pl.pallas_call(
-            body, out_shape=outs, in_specs=specs, out_specs=jax.tree.map(lambda _: vmem, outs), name=body.__name__,
+            body, out_shape=outs, in_specs=specs, out_specs=jax.tree.map(lambda _: vmem, outs),
             compiler_params=pltpu.CompilerParams(vmem_limit_bytes=limit * MIB), **more,
         )
 
-    planes = VMEM((5, ny, nz), jnp.float32)
-    near, far = call(take_planes, 3, (planes, planes), 8)(par, density, source)
-    near = lax.ppermute(near, both, near_pairs)
-    far = lax.ppermute(far, both, far_pairs)
-    rows = VMEM((nx + 2, TILE, nz), jnp.float32)
-    xs, dg = call(take_rows, 4, (rows, rows), 8)(par, density, source, near)
-    rxs = lax.ppermute(xs, both, ynear_pairs)
-    rdg = lax.ppermute(dg, both, yfar_pairs)
-    begin = jnp.where(xodd == 1, nx - 2, 0)
-    corner = jnp.concatenate([lax.dynamic_slice_in_dim(v, begin, 2, 0) for v in (rxs, rdg)], axis=0)
-    rfc = lax.ppermute(corner, both, far_pairs)
+    hbm = pl.BlockSpec(memory_space=pltpu.HBM)
+
+    def send(value, pairs):
+        return lax.ppermute(value, both, pairs)
+
+    planes, rows = VMEM((5, ny, nz), jnp.float32), VMEM((nx, TILE, nz), jnp.float32)
+    near, far, xs, dg = pl.pallas_call(
+        take_kernel, out_shape=(planes, planes, rows, rows), in_specs=[smem, hbm, hbm], out_specs=(vmem,) * 4,
+        scratch_shapes=[rows] * 4 + [pltpu.SemaphoreType.DMA((14,))], name="take_kernel",
+        compiler_params=pltpu.CompilerParams(vmem_limit_bytes=8 * MIB),
+    )(par, *(pltpu.with_memory_space_constraint(v, pltpu.HBM) for v in (density, source)))
+    near = send(near, near_pairs)
+    rxs = send(xs, ynear_pairs)
+    rdg = send(dg, yfar_pairs)
+    far = send(far, far_pairs)
+
+    def corner(begin):
+        return jnp.concatenate([lax.dynamic_slice_in_dim(v, begin, 2, 0) for v in (rxs, rdg)], axis=0)
+
+    rfc = send(corner(jnp.where(xodd == 1, nx - 2, 0)), far_pairs)
+    rnc = send(corner(jnp.where(xodd == 1, 0, nx - 2)), near_pairs)
 
     ext = VMEM((nx + 2 * DEEP, nz // LANES, ny + 2 * OFF, LANES), jnp.float32)
-    *held, part = call(near_kernel, 6, (ext,) * 10 + (VMEM((SUMS, TILE, LANES), jnp.float32),), 8)(par, density, source, near, rxs, rdg)
+    *held, part = call(near_kernel, 7, (ext,) * 10 + (VMEM((SUMS, TILE, LANES), jnp.float32),), 8)(par, density, source, near, rxs, rdg, rnc)
     mom, *held = call(far_kernel, 14, (VMEM((1, LANES), jnp.float32),) + (ext,) * 10, 8, input_output_aliases={4 + k: 1 + k for k in range(10)})(
         par, far, rfc, part, *held)
-    dx, sx, wx, wy, wz, sc, g0, g1, w0, n0 = held
+    _, sx, _, _, _, sc, _, _, w0, n0 = held
 
     n = nx_dev * ny_dev
     sent = jnp.broadcast_to(mom[None], (n, 1, LANES))
     got = lax.all_to_all(sent, both, 0, 0, tiled=True).reshape(n, LANES)
     whole = jax.ShapeDtypeStruct(density.shape, jnp.float32)
+    plane = VMEM(density.shape, jnp.float32)
     return pl.pallas_call(
-        last_kernel, out_shape=(whole, whole), in_specs=[vmem] * 5, out_specs=(vmem, vmem), name="last_kernel",
+        last_kernel, out_shape=(whole, whole), in_specs=[vmem] * 5, out_specs=(hbm, hbm), name="last_kernel",
+        scratch_shapes=[plane, plane, pltpu.SemaphoreType.DMA((2, nx))],
         compiler_params=pltpu.CompilerParams(vmem_limit_bytes=8 * MIB),
     )(got, sx, sc, w0, n0)
 

time: 42.2 us -> 41.9 us (level)
  local copies, waits for them, and re-layouts: 3.18 us -> 0.12 us
  waiting for transfers between devices: 7.5 us -> 9.48 us
  blocking collectives: 9.66 us -> 10.4 us
  Pallas kernels: 12 us -> 12.6 us
  starting transfers between devices: 8.91 us -> 8.31 us
    unnamed x10 -> x4, local copies, waits for them, and re-layouts: 3.08 us -> 0.01 us
    ppermute x5 -> x6, waiting for transfers between devices: 7.5 us -> 9.48 us  [send(): return lax.ppermute(value, both, pairs)]
    pallas_call x3 -> x2, Pallas kernels: 7.38 us -> 8.24 us  [the longest x1 5.05 us: shards(): call(near_kernel, 7, (ext,) * 10 + (VMEM((SUMS, TILE, LANES), jnp.float32...]
    all_to_all x1, blocking collectives: 9.66 us -> 10.4 us  [shards(): got = lax.all_to_all(sent, both, 0, 0, tiled=True).reshape(n, LANES)]
    ppermute x5 -> x6, starting transfers between devices: 8.91 us -> 8.31 us  [send(): return lax.ppermute(value, both, pairs)]
  transfers between devices with their start and end apart: 5 -> 6, of which waited for: 1 -> 1; matrix products, arithmetic and copies ran while one was open for 0% -> 0% of each run, Pallas kernels for 14% -> 12%
where the time goes in v3:
time: 41.9 us; the launch traced here: 41.7 us
  Pallas kernels  12.6 us (30%)
  blocking collectives  10.4 us (25%)
  waiting for transfers between devices  9.48 us (23%)
  starting transfers between devices  8.31 us (20%)
  between operations  0.75 us (2%)
    all_to_all x1, blocking collectives, shards(): got = lax.all_to_all(sent, both, 0, 0, tiled=True).reshape(n, LANES)  10.4 us
    ppermute x6, waiting for transfers between devices, send(): return lax.ppermute(value, both, pairs)  9.48 us
    ppermute x6, starting transfers between devices, send(): return lax.ppermute(value, both, pairs)  8.31 us
    pallas_call x1, Pallas kernels, shards(): call(near_kernel, 7, (ext,) * 10 + (VMEM((SUMS, TILE, LANES), jnp.float32...  5.05 us
    pallas_call x1, Pallas kernels, shards(): pl.pallas_call(take_kernel, out_shape=(planes, planes, rows, rows), in_sp...  3.19 us
    pallas_call x1, Pallas kernels, shards(): call(far_kernel, 14, (VMEM((1, LANES), jnp.float32),) + (ext,) * 10, 8, i...  2.66 us
    pallas_call x1, Pallas kernels, shards(): pl.pallas_call(last_kernel, out_shape=(whole, whole), in_specs=[vmem] * 5...  1.73 us
  transfers between devices with their start and end apart: 6, of which 1 were waited for; matrix products, arithmetic and copies ran while one was open for 0% of the time, Pallas kernels for 12%

profile of v3, /device:TPU:0, one launch (start us, length us, event | category | flops | bytes accessed | tf_op | source)
XLA Modules:
  0.0 41.7 jit_solution(9687579091148106177)
XLA Ops:
  0.6 0.0 copy-start
  0.6 0.0 copy-start.1
  0.7 0.1 stack.43.par
  0.8 3.2 %take_kernel.1 = (f32[5,128,256]{2,1,0:T(8,128)}, f32[5,128,256]{2,1,0:T(8,128)}, f32[8,8,256]{2,1,0:T(8,128)}, f32[8,8,256]{2,1,0:T(8,128)}) custom-call(s32[6]{0:T(128)S(1)} %stack.43.par, f32[8,128,256]{2,1,0:T(8,128)} %dens.3, f32[8,128,256]{2,1,0:T(8,128)} %src.3), custom_call_target="tpu_custom_call" | custom-call | tf_op jit(solution)/shard_map/take_kernel/pallas_call | solution.py:328
  4.0 0.6 %collective-permute-start.4 = (f32[5,128,256]{2,1,0:T(8,128)}, f32[5,128,256]{2,1,0:T(8,128)S(1)}, u32[]{:S(2)}, u32[]{:S(2)}) collective-permute-start(f32[5,128,256]{2,1,0:T(8,128)} %get-tuple-element.25), channel_id=1, source_target_pairs={{0,4},{1,5},{2,6},{3,7},{4,0},{5,1},{6,2},{7,3},{8,12},{9,13},{10,... | collective-permute-start | bytes 1966088 | tf_op jit(solution)/shard_map/ppermute | solution.py:325
  4.5 2.6 %collective-permute-start = (f32[5,128,256]{2,1,0:T(8,128)}, f32[5,128,256]{2,1,0:T(8,128)S(1)}, u32[]{:S(2)}, u32[]{:S(2)}) collective-permute-start(f32[5,128,256]{2,1,0:T(8,128)} %get-tuple-element.22), channel_id=1, source_target_pairs={{0,1},{1,0},{2,3},{3,2},{4,8},{5,9},{6,10},{7,11},{8,4},{9,5},{10,... | collective-permute-start | bytes 1966088 | tf_op jit(solution)/shard_map/ppermute | solution.py:325
  7.1 0.1 collective-permute-start.1
  7.2 1.3 %collective-permute-start.2 = (f32[8,8,256]{2,1,0:T(8,128)}, f32[8,8,256]{2,1,0:T(8,128)S(1)}, u32[]{:S(2)}, u32[]{:S(2)}) collective-permute-start(f32[8,8,256]{2,1,0:T(8,128)} %get-tuple-element.24), channel_id=1, source_target_pairs={{0,4},{1,2},{2,1},{3,7},{4,0},{5,6},{6,5},{7,3},{8,12},{9,10},{10,... | collective-permute-start | bytes 196616 | tf_op jit(solution)/shard_map/ppermute | solution.py:325
  8.5 9.5 %collective-permute-done.1.rxs = f32[8,8,256]{2,1,0:T(8,128)S(1)} collective-permute-done((f32[8,8,256]{2,1,0:T(8,128)}, f32[8,8,256]{2,1,0:T(8,128)S(1)}, u32[]{:S(2)}, u32[]{:S(2)}) %collective-permute-start.1) | collective-permute-done | bytes 65568 | tf_op jit(solution)/shard_map/ppermute | solution.py:325
  18.0 0.0 collective-permute-done.2.rdg
  18.0 0.1 collective-permute-start.5
  18.1 3.7 %collective-permute-start.3 = (f32[4,8,256]{2,1,0:T(8,128)S(1)}, f32[4,8,256]{2,1,0:T(8,128)S(1)}, u32[]{:S(2)}, u32[]{:S(2)}) collective-permute-start(f32[4,8,256]{2,1,0:T(8,128)S(1)} %pad_maximum_fusion), channel_id=1, source_target_pairs={{0,1},{1,0},{2,3},{3,2},{4,8},{5,9},{6,10},{7,11},{8,4},{9,5},{10,... | collective-permute-start | bytes 98312 | tf_op jit(solution)/shard_map/ppermute | solution.py:325
  21.8 0.0 collective-permute-done.5.rnc
  21.8 0.0 collective-permute-done.4.near
  21.8 0.0 copy-done
  21.8 0.0 copy-done.1
  21.8 5.1 %shard_map.41 = (f32[14,2,160,128]{3,2,1,0:T(8,128)S(1)}, f32[14,2,160,128]{3,2,1,0:T(8,128)S(1)}, f32[14,2,160,128]{3,2,1,0:T(8,128)S(1)}, f32[14,2,160,128]{3,...) custom-call(s32[6]{0:T(128)S(1)} %stack.43.par, ...), custom_call_target="tpu_custom_call" | custom-call | tf_op jit(solution)/shard_map/pallas_call | solution.py:345
  26.9 0.0 collective-permute-done.3.rfc
  26.9 0.0 collective-permute-done.far
  26.9 2.7 %shard_map.42 = (f32[1,128]{1,0:T(1,128)S(1)}, f32[14,2,160,128]{3,2,1,0:T(8,128)S(1)}, f32[14,2,160,128]{3,2,1,0:T(8,128)S(1)}, f32[14,2,160,128]{3,2,1,0:T(8,1...) custom-call(s32[6]{0:T(128)S(1)} %stack.43.par, ...), custom_call_target="tpu_custom_call", output_to_operand_aliasing={{1}: (4, {}), {2}: (5, {}), {3}: (6, {}), {4}: (7, {}), {5}... | custom-call | tf_op jit(solution)/shard_map/pallas_call | solution.py:346
  29.6 10.4 %all_to_all.5 = f32[32,1,128]{2,1,0:T(1,128)S(1)} all-to-all(f32[32,1,128]{2,1,0:T(1,128)S(1)} %broadcast_in_dim.9), channel_id=1, replica_groups=mesh['gx'=8,'gy'=4] {'gx','gy'}, dimensions={0} | all-to-all | bytes 32768 | tf_op jit(solution)/shard_map/all_to_all | solution.py:352
  40.0 1.7 %last_kernel.1 = (f32[8,128,256]{2,1,0:T(8,128)}, f32[8,128,256]{2,1,0:T(8,128)}) custom-call(f32[32,128]{1,0:T(8,128)S(1)} %bitcast.8, f32[14,2,160,128]{3,2,1,0:T(8,128)S(1)} %get-tuple-element.38.sx, f32[14,2,160,128]{3,2,1,0:T(8,128)S(1)} %get-tuple-element.39.sc, f32[14,2,160,128]{3,2,1,0:T(8,128)S(1)} %get-tuple-element.40.w0, ...), custom_call_target="tpu_custom_call" | custom-call | tf_op jit(solution)/shard_map/last_kernel/pallas_call | solution.py:355
  (5 shorter events, 0.0 us)
Async XLA Ops:
  0.6 21.2 %copy-start = (f32[8,128,256]{2,1,0:T(8,128)S(1)}, f32[8,128,256]{2,1,0:T(8,128)}, u32[]{:S(2)}) copy-start(f32[8,128,256]{2,1,0:T(8,128)} %dens.3) | copy-start | bytes 3145732
  0.6 21.2 %copy-start.1 = (f32[8,128,256]{2,1,0:T(8,128)S(1)}, f32[8,128,256]{2,1,0:T(8,128)}, u32[]{:S(2)}) copy-start(f32[8,128,256]{2,1,0:T(8,128)} %src.3) | copy-start | bytes 3145732
  4.0 17.8 %collective-permute-start.4 = (f32[5,128,256]{2,1,0:T(8,128)}, f32[5,128,256]{2,1,0:T(8,128)S(1)}, u32[]{:S(2)}, u32[]{:S(2)}) collective-permute-start(f32[5,128,256]{2,1,0:T(8,128)} %get-tuple-element.25), channel_id=1, source_target_pairs={{0,4},{1,5},{2,6},{3,7},{4,0},{5,1},{6,2},{7,3},{8,12},{9,13},{10,... | collective-permute-start | bytes 1966088 | tf_op jit(solution)/shard_map/ppermute | solution.py:325
  4.5 22.4 %collective-permute-start = (f32[5,128,256]{2,1,0:T(8,128)}, f32[5,128,256]{2,1,0:T(8,128)S(1)}, u32[]{:S(2)}, u32[]{:S(2)}) collective-permute-start(f32[5,128,256]{2,1,0:T(8,128)} %get-tuple-element.22), channel_id=1, source_target_pairs={{0,1},{1,0},{2,3},{3,2},{4,8},{5,9},{6,10},{7,11},{8,4},{9,5},{10,... | collective-permute-start | bytes 1966088 | tf_op jit(solution)/shard_map/ppermute | solution.py:325
  7.1 10.9 %collective-permute-start.1 = (f32[8,8,256]{2,1,0:T(8,128)}, f32[8,8,256]{2,1,0:T(8,128)S(1)}, u32[]{:S(2)}, u32[]{:S(2)}) collective-permute-start(f32[8,8,256]{2,1,0:T(8,128)} %get-tuple-element.23), channel_id=1, source_target_pairs={{0,1},{1,0},{2,3},{3,2},{4,5},{5,4},{6,7},{7,6},{8,9},{9,8},{10,11... | collective-permute-start | bytes 196616 | tf_op jit(solution)/shard_map/ppermute | solution.py:325
  7.2 10.8 %collective-permute-start.2 = (f32[8,8,256]{2,1,0:T(8,128)}, f32[8,8,256]{2,1,0:T(8,128)S(1)}, u32[]{:S(2)}, u32[]{:S(2)}) collective-permute-start(f32[8,8,256]{2,1,0:T(8,128)} %get-tuple-element.24), channel_id=1, source_target_pairs={{0,4},{1,2},{2,1},{3,7},{4,0},{5,6},{6,5},{7,3},{8,12},{9,10},{10,... | collective-permute-start | bytes 196616 | tf_op jit(solution)/shard_map/ppermute | solution.py:325
  18.0 3.8 %collective-permute-start.5 = (f32[4,8,256]{2,1,0:T(8,128)S(1)}, f32[4,8,256]{2,1,0:T(8,128)S(1)}, u32[]{:S(2)}, u32[]{:S(2)}) collective-permute-start(f32[4,8,256]{2,1,0:T(8,128)S(1)} %pad_maximum_fusion.1), channel_id=1, source_target_pairs={{0,4},{1,5},{2,6},{3,7},{4,0},{5,1},{6,2},{7,3},{8,12},{9,13},{10,... | collective-permute-start | bytes 98312 | tf_op jit(solution)/shard_map/ppermute | solution.py:325
  18.1 8.8 %collective-permute-start.3 = (f32[4,8,256]{2,1,0:T(8,128)S(1)}, f32[4,8,256]{2,1,0:T(8,128)S(1)}, u32[]{:S(2)}, u32[]{:S(2)}) collective-permute-start(f32[4,8,256]{2,1,0:T(8,128)S(1)} %pad_maximum_fusion), channel_id=1, source_target_pairs={{0,1},{1,0},{2,3},{3,2},{4,8},{5,9},{6,10},{7,11},{8,4},{9,5},{10,... | collective-permute-start | bytes 98312 | tf_op jit(solution)/shard_map/ppermute | solution.py:325

commit v4 on v3

--- a/solution.py
+++ b/solution.py
@@ -26,7 +26,7 @@
             near.append((at(x, y), at(x ^ 1, y)))
             other = x - 1 if x % 2 == 0 else x + 1
             inside = 0 <= other < nx
-            far.append((at(x, y), at(other, y) if inside else at(x, y ^ 1)))
+            far.append((at(x, y), at(other, y) if inside else at(x, (y + ny // 2) % ny)))
             ynear.append((at(x, y), at(x, y ^ 1)))
             beside = y - 1 if y % 2 == 0 else y + 1
             within = 0 <= beside < ny
@@ -34,29 +34,38 @@
     return near, far, ynear, yfar
 
 
-def take_kernel(par, dens, src, near_out, far_out, xs_out, dg_out, dlo, dhi, slo, shi, sems):
+def take_kernel(par, dens, src, far_out, near_out, xs_out, dg_out, dlo, dhi, slo, shi, far_buf, near_buf, xs_buf, dg_buf, sems, out_sems):
     nx, ny, nz = dens.shape
     xodd, yodd = par[0] == 1, par[1] == 1
-    copies = [
-        (dens.at[:, pl.ds(0, TILE)], dlo), (dens.at[:, pl.ds(ny - TILE, TILE)], dhi),
-        (src.at[:, pl.ds(0, TILE)], slo), (src.at[:, pl.ds(ny - TILE, TILE)], shi),
-    ]
-    for out, d, s in ((near_out, jnp.where(xodd, 0, nx - 3), jnp.where(xodd, 0, nx - 2)),
-                      (far_out, jnp.where(xodd, nx - 3, 0), jnp.where(xodd, nx - 2, 0))):
-        copies += [(dens.at[pl.ds(d + k, 1)], out.at[pl.ds(k, 1)]) for k in range(3)]
-        copies += [(src.at[pl.ds(s + k, 1)], out.at[pl.ds(3 + k, 1)]) for k in range(2)]
-    copies = [pltpu.make_async_copy(a, b, sems.at[i]) for i, (a, b) in enumerate(copies)]
-    for copy in copies:
+    moves = []
+    for buf, out, d, s in ((far_buf, far_out, jnp.where(xodd, nx - 3, 0), jnp.where(xodd, nx - 2, 0)),
+                           (near_buf, near_out, jnp.where(xodd, 0, nx - 3), jnp.where(xodd, 0, nx - 2))):
+        for ref, first, count, at in ((dens, d, 3, 0), (src, s, 2, 3)):
+            for k in range(count):
+                here = pl.ds(at + k, 1)
+                moves.append((ref.at[pl.ds(first + k, 1)], buf.at[here], out.at[here]))
+    slabs = [(dens.at[:, pl.ds(0, TILE)], dlo), (dens.at[:, pl.ds(ny - TILE, TILE)], dhi),
+             (src.at[:, pl.ds(0, TILE)], slo), (src.at[:, pl.ds(ny - TILE, TILE)], shi)]
+    slabs = [pltpu.make_async_copy(a, b, sems.at[len(moves) + i]) for i, (a, b) in enumerate(slabs)]
+    reads = [pltpu.make_async_copy(a, b, sems.at[i]) for i, (a, b, _) in enumerate(moves)]
+    writes = [pltpu.make_async_copy(b, c, out_sems.at[i]) for i, (_, b, c) in enumerate(moves)]
+    writes += [pltpu.make_async_copy(b, c, out_sems.at[len(moves) + i]) for i, (b, c) in enumerate(((xs_buf, xs_out), (dg_buf, dg_out)))]
+    for copy in slabs + reads:
         copy.start()
-    for copy in copies[:4]:
+    for copy in slabs:
         copy.wait()
     row = lax.broadcasted_iota(jnp.int32, (TILE, nz), 0)
     for k in range(nx):
         down = jnp.where(row < 3, dlo[k], pltpu.roll(slo[k], 4, 0))
         up = jnp.where(row > 4, dhi[k], pltpu.roll(shi[k], 4, 0))
-        xs_out[k] = jnp.where(yodd, down, up)
-        dg_out[k] = jnp.where(yodd, up, down)
-    for copy in copies[4:]:
+        xs_buf[k] = jnp.where(yodd, down, up)
+        dg_buf[k] = jnp.where(yodd, up, down)
+    for copy in writes[len(moves):]:
+        copy.start()
+    for read, write in zip(reads, writes):
+        read.wait()
+        write.start()
+    for copy in writes:
         copy.wait()
 
 
@@ -75,9 +84,8 @@
         put_plane(sx, e, at, pltpu.roll(value, 4, 0))
 
 
-def weigh(dx, sx, wx, wy, wz, sc, g0, lo, count):
-    _, nh, rows, _ = dx.shape
-    tiles = range(OFF - TILE, rows - OFF + TILE, TILE)
+def weigh(dx, sx, wx, wy, wz, sc, g0, lo, count, tiles):
+    nh = dx.shape[1]
     lane = lax.broadcasted_iota(jnp.int32, (TILE, LANES), 1)
     inner, first = lane < LANES - 1, lane == 0
     for r in tiles:
@@ -129,14 +137,14 @@
     return out
 
 
-def apply_first(sx, wx, wy, wz, sc, g0, g1, w0, lo, count):
-    _, nh, rows, _ = sx.shape
+def apply_first(sx, wx, wy, wz, sc, g0, g1, w0, lo, count, tiles):
+    nh = sx.shape[1]
     lane = lax.broadcasted_iota(jnp.int32, (TILE, LANES), 1)
     inner, first = lane < LANES - 1, lane == 0
 
     def plane(k, carry):
         e = lo + k
-        for r in range(OFF - TILE, rows - OFF + TILE, TILE):
+        for r in tiles:
             t = couple(g0, wx, wy, wz, e, r, nh, inner, first)
             for h in range(nh):
                 s = sc[e, h, pl.ds(r, TILE)]
@@ -148,7 +156,7 @@
     lax.fori_loop(0, count, plane, 0)
 
 
-def clear_outside(par, g1, e, has_x):
+def clear_rows(par, g1):
     _, nh, rows, _ = g1.shape
     zero = jnp.zeros((TILE, LANES), jnp.float32)
     for flag, at in ((par[4], OFF - TILE), (par[5], rows - OFF)):
@@ -159,22 +167,26 @@
                 for h in range(nh):
                     g1[k, h, pl.ds(at, TILE)] = zero
 
-    @pl.when(has_x == 0)
+
+def clear_plane(g1, e, has, tiles):
+    zero = jnp.zeros((TILE, LANES), jnp.float32)
+
+    @pl.when(has == 0)
     def _():
-        for r in range(OFF - TILE, rows - OFF + TILE, TILE):
-            for h in range(nh):
+        for r in tiles:
+            for h in range(g1.shape[1]):
                 g1[e, h, pl.ds(r, TILE)] = zero
 
 
-def apply_second(sx, wx, wy, wz, sc, g1, w0, n0, lo, count, sums):
-    _, nh, rows, _ = sx.shape
+def apply_second(sx, wx, wy, wz, sc, g1, w0, n0, lo, count, tiles, sums):
+    nh = sx.shape[1]
     lane = lax.broadcasted_iota(jnp.int32, (TILE, LANES), 1)
     inner, first = lane < LANES - 1, lane == 0
 
     def plane(k, sums):
         e = lo + k
         sums = list(sums)
-        for r in range(OFF, rows - OFF, TILE):
+        for r in tiles:
             t = couple(g1, wx, wy, wz, e, r, nh, inner, first)
             for h in range(nh):
                 s = sc[e, h, pl.ds(r, TILE)]
@@ -189,11 +201,25 @@
     return lax.fori_loop(0, count, plane, tuple(sums))
 
 
-def near_kernel(par, dens, src, near, rxs, rdg, rnc, dx, sx, wx, wy, wz, sc, g0, g1, w0, n0, mom):
+def row_tiles(ny, inset):
+    return list(range(OFF + inset * TILE, OFF + ny - inset * TILE, TILE))
+
+
+def outer_tiles(ny, reach, inset):
+    inside = row_tiles(ny, inset)
+    return [r for r in row_tiles(ny, -reach) if r not in inside]
+
+
+def near_side(par):
+    xodd = par[0] == 1
+    return jnp.where(xodd, 1, 4), jnp.where(xodd, 2, 5), jnp.where(xodd, 3, 6), jnp.where(xodd, par[2], par[3])
+
+
+def inner_kernel(par, dens, src, near, dx, sx, wx, wy, wz, sc, g0, g1, w0, n0, mom):
     nx, ny, _ = dens.shape
-    xodd, yodd = par[0] == 1, par[1] == 1
-    has_near = jnp.where(xodd, par[2], par[3]) == 1
-    has_down, has_up = par[4] == 1, par[5] == 1
+    xodd = par[0] == 1
+    first, second, third, has = near_side(par)
+    has_near = has == 1
     own = slice(OFF, OFF + ny)
     for k in range(nx):
         put_plane(dx, k + DEEP, own, 0.5 * dens[k])
@@ -204,6 +230,23 @@
     beyond = jnp.where(xodd, 1, nx + 3)
     for k in range(2):
         put_plane(sx, beyond + k, own, jnp.where(has_near, near[3 + k], 0.0))
+    weigh(dx, sx, wx, wy, wz, sc, g0, first, nx + 1, row_tiles(ny, 1))
+    apply_first(sx, wx, wy, wz, sc, g0, g1, w0, second, nx - 1, row_tiles(ny, 2))
+    clear_plane(g1, jnp.where(xodd, 2, nx + 3), has, row_tiles(ny, 2))
+    zero = jnp.zeros((TILE, LANES), jnp.float32)
+    sums = apply_second(sx, wx, wy, wz, sc, g1, w0, n0, third, nx - 3, row_tiles(ny, 3), (zero,) * SUMS)
+    for i in range(SUMS):
+        mom[i] = sums[i]
+
+
+def edge_kernel(par, rxs, rdg, rnc, part, *refs):
+    mom, dx, sx, wx, wy, wz, sc, g0, g1, w0, n0 = refs[10:]
+    nx = dx.shape[0] - 2 * DEEP
+    ny = dx.shape[2] - 2 * OFF
+    xodd, yodd = par[0] == 1, par[1] == 1
+    first, second, third, has = near_side(par)
+    has_near, has_down, has_up = has == 1, par[4] == 1, par[5] == 1
+    beyond = jnp.where(xodd, 1, nx + 3)
     for k in range(nx + 2):
         inside = True if k < nx else has_near
         a, b = (rxs[k], rdg[k]) if k < nx else (rnc[k - nx], rnc[2 + k - nx])
@@ -211,11 +254,11 @@
         low = jnp.where(jnp.logical_and(has_down, inside), low, 0.0)
         high = jnp.where(jnp.logical_and(has_up, inside), high, 0.0)
         put_rows(dx, sx, k + DEEP if k < nx else beyond + k - nx, low, high, ny)
-    weigh(dx, sx, wx, wy, wz, sc, g0, jnp.where(xodd, 1, 4), nx + 1)
-    apply_first(sx, wx, wy, wz, sc, g0, g1, w0, jnp.where(xodd, 2, 5), nx - 1)
-    clear_outside(par, g1, jnp.where(xodd, 2, nx + 3), jnp.where(xodd, par[2], par[3]))
-    zero = jnp.zeros((TILE, LANES), jnp.float32)
-    sums = apply_second(sx, wx, wy, wz, sc, g1, w0, n0, jnp.where(xodd, 3, 6), nx - 3, (zero,) * SUMS)
+    weigh(dx, sx, wx, wy, wz, sc, g0, first, nx + 1, outer_tiles(ny, 1, 1))
+    apply_first(sx, wx, wy, wz, sc, g0, g1, w0, second, nx - 1, outer_tiles(ny, 1, 2))
+    clear_plane(g1, jnp.where(xodd, 2, nx + 3), has, outer_tiles(ny, 1, 2))
+    clear_rows(par, g1)
+    sums = apply_second(sx, wx, wy, wz, sc, g1, w0, n0, third, nx - 3, outer_tiles(ny, 0, 3), [part[i] for i in range(SUMS)])
     for i in range(SUMS):
         mom[i] = sums[i]
 
@@ -238,10 +281,11 @@
         a, b = rfc[k], rfc[2 + k]
         low, high = jnp.where(yodd, a, b), jnp.where(yodd, b, a)
         put_rows(dx, sx, beyond + k, jnp.where(has_down, low, 0.0), jnp.where(has_up, high, 0.0), ny)
-    weigh(dx, sx, wx, wy, wz, sc, g0, jnp.where(xodd, nx + 2, 1), 3)
-    apply_first(sx, wx, wy, wz, sc, g0, g1, w0, jnp.where(xodd, nx + 1, 2), 3)
-    clear_outside(par, g1, jnp.where(xodd, nx + 3, 2), has)
-    sums = apply_second(sx, wx, wy, wz, sc, g1, w0, n0, jnp.where(xodd, nx, 3), 3, [part[i] for i in range(SUMS)])
+    weigh(dx, sx, wx, wy, wz, sc, g0, jnp.where(xodd, nx + 2, 1), 3, row_tiles(ny, -1))
+    apply_first(sx, wx, wy, wz, sc, g0, g1, w0, jnp.where(xodd, nx + 1, 2), 3, row_tiles(ny, -1))
+    clear_plane(g1, jnp.where(xodd, nx + 3, 2), has, row_tiles(ny, -1))
+    clear_rows(par, g1)
+    sums = apply_second(sx, wx, wy, wz, sc, g1, w0, n0, jnp.where(xodd, nx, 3), 3, row_tiles(ny, 0), [part[i] for i in range(SUMS)])
     place = lax.broadcasted_iota(jnp.int32, (1, LANES), 1) // PART
     out = jnp.zeros((1, LANES), jnp.float32)
     for k, v in enumerate(sums):
@@ -324,11 +368,12 @@
     def send(value, pairs):
         return lax.ppermute(value, both, pairs)
 
-    planes, rows = VMEM((5, ny, nz), jnp.float32), VMEM((nx, TILE, nz), jnp.float32)
-    near, far, xs, dg = pl.pallas_call(
-        take_kernel, out_shape=(planes, planes, rows, rows), in_specs=[smem, hbm, hbm], out_specs=(vmem,) * 4,
-        scratch_shapes=[rows] * 4 + [pltpu.SemaphoreType.DMA((14,))], name="take_kernel",
-        compiler_params=pltpu.CompilerParams(vmem_limit_bytes=8 * MIB),
+    planes, rows = ((5, ny, nz), jnp.float32), ((nx, TILE, nz), jnp.float32)
+    shapes = (planes, planes, rows, rows)
+    far, near, xs, dg = pl.pallas_call(
+        take_kernel, out_shape=tuple(jax.ShapeDtypeStruct(*v) for v in shapes), in_specs=[smem, hbm, hbm], out_specs=(hbm,) * 4,
+        scratch_shapes=[VMEM(*rows)] * 4 + [VMEM(*v) for v in shapes] + [pltpu.SemaphoreType.DMA((14,)), pltpu.SemaphoreType.DMA((12,))],
+        name="take_kernel", compiler_params=pltpu.CompilerParams(vmem_limit_bytes=8 * MIB),
     )(par, *(pltpu.with_memory_space_constraint(v, pltpu.HBM) for v in (density, source)))
     near = send(near, near_pairs)
     rxs = send(xs, ynear_pairs)
@@ -342,7 +387,10 @@
     rnc = send(corner(jnp.where(xodd == 1, 0, nx - 2)), near_pairs)
 
     ext = VMEM((nx + 2 * DEEP, nz // LANES, ny + 2 * OFF, LANES), jnp.float32)
-    *held, part = call(near_kernel, 7, (ext,) * 10 + (VMEM((SUMS, TILE, LANES), jnp.float32),), 8)(par, density, source, near, rxs, rdg, rnc)
+    sums = VMEM((SUMS, TILE, LANES), jnp.float32)
+    *held, part = call(inner_kernel, 4, (ext,) * 10 + (sums,), 8)(par, density, source, near)
+    part, *held = call(edge_kernel, 15, (sums,) + (ext,) * 10, 8, input_output_aliases={5 + k: 1 + k for k in range(10)})(
+        par, rxs, rdg, rnc, part, *held)
     mom, *held = call(far_kernel, 14, (VMEM((1, LANES), jnp.float32),) + (ext,) * 10, 8, input_output_aliases={4 + k: 1 + k for k in range(10)})(
         par, far, rfc, part, *held)
     _, sx, _, _, _, sc, _, _, w0, n0 = held

time: 41.9 us -> 38.3 us (0.914)
  waiting for transfers between devices: 9.48 us -> 2.99 us
  Pallas kernels: 12.6 us -> 15 us
  blocking collectives: 10.4 us -> 10.9 us
    ppermute x6, waiting for transfers between devices: 9.48 us -> 2.99 us  [send(): return lax.ppermute(value, both, pairs)]
    pallas_call x2 -> x3, Pallas kernels: 8.24 us -> 10.6 us  [the longest x1 4.3 us: shards(): call(inner_kernel, 4, (ext,) * 10 + (sums,), 8)(par, density, source, near)]
    all_to_all x1, blocking collectives: 10.4 us -> 10.9 us  [shards(): got = lax.all_to_all(sent, both, 0, 0, tiled=True).reshape(n, LANES)]
  transfers between devices with their start and end apart: 6 -> 6, of which waited for: 1 -> 1; matrix products, arithmetic and copies ran while one was open for 0% -> 0% of each run, Pallas kernels for 12% -> 20%
where the time goes in v4:
time: 38.3 us; the launch traced here: 38.2 us
  Pallas kernels  15 us (39%)
  blocking collectives  10.9 us (28%)
  starting transfers between devices  8.38 us (22%)
  waiting for transfers between devices  2.99 us (8%)
  between operations  0.75 us (2%)
    all_to_all x1, blocking collectives, shards(): got = lax.all_to_all(sent, both, 0, 0, tiled=True).reshape(n, LANES)  10.9 us
    ppermute x6, starting transfers between devices, send(): return lax.ppermute(value, both, pairs)  8.38 us
    pallas_call x1, Pallas kernels, shards(): call(inner_kernel, 4, (ext,) * 10 + (sums,), 8)(par, density, source, near)  4.3 us
    pallas_call x1, Pallas kernels, shards(): call(edge_kernel, 15, (sums,) + (ext,) * 10, 8, input_output_aliases={5 +...  3.38 us
    ppermute x6, waiting for transfers between devices, send(): return lax.ppermute(value, both, pairs)  2.99 us
    pallas_call x1, Pallas kernels, shards(): pl.pallas_call(take_kernel, out_shape=tuple((jax.ShapeDtypeStruct(*v) for...  2.9 us
    pallas_call x1, Pallas kernels, shards(): call(far_kernel, 14, (VMEM((1, LANES), jnp.float32),) + (ext,) * 10, 8, i...  2.69 us
    pallas_call x1, Pallas kernels, shards(): pl.pallas_call(last_kernel, out_shape=(whole, whole), in_specs=[vmem] * 5...  1.73 us
  transfers between devices with their start and end apart: 6, of which 1 were waited for; matrix products, arithmetic and copies ran while one was open for 0% of the time, Pallas kernels for 20%

profile of v4, /device:TPU:0, one launch (start us, length us, event | category | flops | bytes accessed | tf_op | source)
XLA Modules:
  0.0 38.2 jit_solution(15886285677489503417)
XLA Ops:
  0.6 0.0 copy-start
  0.6 0.0 copy-start.1
  0.7 0.1 stack.43.par
  0.8 2.9 %take_kernel.1 = (f32[5,128,256]{2,1,0:T(8,128)}, f32[5,128,256]{2,1,0:T(8,128)}, f32[8,8,256]{2,1,0:T(8,128)}, f32[8,8,256]{2,1,0:T(8,128)}) custom-call(s32[6]{0:T(128)S(1)} %stack.43.par, f32[8,128,256]{2,1,0:T(8,128)} %dens.3, f32[8,128,256]{2,1,0:T(8,128)} %src.3), custom_call_target="tpu_custom_call" | custom-call | tf_op jit(solution)/shard_map/take_kernel/pallas_call | solution.py:373
  3.7 0.6 %collective-permute-start.5 = (f32[5,128,256]{2,1,0:T(8,128)}, f32[5,128,256]{2,1,0:T(8,128)S(1)}, u32[]{:S(2)}, u32[]{:S(2)}) collective-permute-start(f32[5,128,256]{2,1,0:T(8,128)} %get-tuple-element.36), channel_id=1, source_target_pairs={{0,4},{1,5},{2,6},{3,7},{4,0},{5,1},{6,2},{7,3},{8,12},{9,13},{10,... | collective-permute-start | bytes 1966088 | tf_op jit(solution)/shard_map/ppermute | solution.py:369
  4.2 2.6 %collective-permute-start = (f32[5,128,256]{2,1,0:T(8,128)}, f32[5,128,256]{2,1,0:T(8,128)S(1)}, u32[]{:S(2)}, u32[]{:S(2)}) collective-permute-start(f32[5,128,256]{2,1,0:T(8,128)} %get-tuple-element.33), channel_id=1, source_target_pairs={{0,2},{1,3},{2,0},{3,1},{4,8},{5,9},{6,10},{7,11},{8,4},{9,5},{10,... | collective-permute-start | bytes 1966088 | tf_op jit(solution)/shard_map/ppermute | solution.py:369
  6.8 1.5 %collective-permute-start.1 = (f32[8,8,256]{2,1,0:T(8,128)}, f32[8,8,256]{2,1,0:T(8,128)S(1)}, u32[]{:S(2)}, u32[]{:S(2)}) collective-permute-start(f32[8,8,256]{2,1,0:T(8,128)} %get-tuple-element.34), channel_id=1, source_target_pairs={{0,1},{1,0},{2,3},{3,2},{4,5},{5,4},{6,7},{7,6},{8,9},{9,8},{10,11... | collective-permute-start | bytes 196616 | tf_op jit(solution)/shard_map/ppermute | solution.py:369
  8.3 0.0 collective-permute-start.2
  8.3 3.0 %collective-permute-done.1.rxs = f32[8,8,256]{2,1,0:T(8,128)S(1)} collective-permute-done((f32[8,8,256]{2,1,0:T(8,128)}, f32[8,8,256]{2,1,0:T(8,128)S(1)}, u32[]{:S(2)}, u32[]{:S(2)}) %collective-permute-start.1) | collective-permute-done | bytes 65568 | tf_op jit(solution)/shard_map/ppermute | solution.py:369
  11.3 0.0 collective-permute-done.2.rdg
  11.3 0.1 collective-permute-start.4
  11.4 3.7 %collective-permute-start.3 = (f32[4,8,256]{2,1,0:T(8,128)S(1)}, f32[4,8,256]{2,1,0:T(8,128)S(1)}, u32[]{:S(2)}, u32[]{:S(2)}) collective-permute-start(f32[4,8,256]{2,1,0:T(8,128)S(1)} %pad_maximum_fusion), channel_id=1, source_target_pairs={{0,2},{1,3},{2,0},{3,1},{4,8},{5,9},{6,10},{7,11},{8,4},{9,5},{10,... | collective-permute-start | bytes 98312 | tf_op jit(solution)/shard_map/ppermute | solution.py:369
  15.1 0.0 collective-permute-done.5.near
  15.1 0.0 copy-done
  15.1 0.0 copy-done.1
  15.1 4.3 %shard_map.41 = (f32[14,2,160,128]{3,2,1,0:T(8,128)S(1)}, f32[14,2,160,128]{3,2,1,0:T(8,128)S(1)}, f32[14,2,160,128]{3,2,1,0:T(8,128)S(1)}, f32[14,2,160,128]{3,...) custom-call(s32[6]{0:T(128)S(1)} %stack.43.par, ...), custom_call_target="tpu_custom_call" | custom-call | tf_op jit(solution)/shard_map/pallas_call | solution.py:391
  19.4 0.0 collective-permute-done.4.rnc
  19.4 3.4 %shard_map.42 = (f32[5,8,128]{2,1,0:T(8,128)S(1)}, f32[14,2,160,128]{3,2,1,0:T(8,128)S(1)}, f32[14,2,160,128]{3,2,1,0:T(8,128)S(1)}, f32[14,2,160,128]{3,2,1,0:T...) custom-call(s32[6]{0:T(128)S(1)} %stack.43.par, ...), custom_call_target="tpu_custom_call", output_to_operand_aliasing={{1}: (5, {}), {2}: (6, {}), {3}: (7, {}), {4}: (8, {}), {5}... | custom-call | tf_op jit(solution)/shard_map/pallas_call | solution.py:392
  22.8 0.0 collective-permute-done.3.rfc
  22.8 0.0 collective-permute-done.far
  22.8 2.7 %shard_map.43 = (f32[1,128]{1,0:T(1,128)S(1)}, f32[14,2,160,128]{3,2,1,0:T(8,128)S(1)}, f32[14,2,160,128]{3,2,1,0:T(8,128)S(1)}, f32[14,2,160,128]{3,2,1,0:T(8,1...) custom-call(s32[6]{0:T(128)S(1)} %stack.43.par, ...), custom_call_target="tpu_custom_call", output_to_operand_aliasing={{1}: (4, {}), {2}: (5, {}), {3}: (6, {}), {4}: (7, {}), {5}... | custom-call | tf_op jit(solution)/shard_map/pallas_call | solution.py:394
  25.5 10.9 %all_to_all.5 = f32[32,1,128]{2,1,0:T(1,128)S(1)} all-to-all(f32[32,1,128]{2,1,0:T(1,128)S(1)} %broadcast_in_dim.9), channel_id=1, replica_groups=mesh['gx'=8,'gy'=4] {'gx','gy'}, dimensions={0} | all-to-all | bytes 32768 | tf_op jit(solution)/shard_map/all_to_all | solution.py:400
  36.4 1.7 %last_kernel.1 = (f32[8,128,256]{2,1,0:T(8,128)}, f32[8,128,256]{2,1,0:T(8,128)}) custom-call(f32[32,128]{1,0:T(8,128)S(1)} %bitcast.8, f32[14,2,160,128]{3,2,1,0:T(8,128)S(1)} %get-tuple-element.60.sx, f32[14,2,160,128]{3,2,1,0:T(8,128)S(1)} %get-tuple-element.61.sc, f32[14,2,160,128]{3,2,1,0:T(8,128)S(1)} %get-tuple-element.62.w0, ...), custom_call_target="tpu_custom_call" | custom-call | tf_op jit(solution)/shard_map/last_kernel/pallas_call | solution.py:403
  (5 shorter events, 0.0 us)
Async XLA Ops:
  0.6 14.5 %copy-start = (f32[8,128,256]{2,1,0:T(8,128)S(1)}, f32[8,128,256]{2,1,0:T(8,128)}, u32[]{:S(2)}) copy-start(f32[8,128,256]{2,1,0:T(8,128)} %dens.3) | copy-start | bytes 3145732
  0.6 14.5 %copy-start.1 = (f32[8,128,256]{2,1,0:T(8,128)S(1)}, f32[8,128,256]{2,1,0:T(8,128)}, u32[]{:S(2)}) copy-start(f32[8,128,256]{2,1,0:T(8,128)} %src.3) | copy-start | bytes 3145732
  3.7 11.4 %collective-permute-start.5 = (f32[5,128,256]{2,1,0:T(8,128)}, f32[5,128,256]{2,1,0:T(8,128)S(1)}, u32[]{:S(2)}, u32[]{:S(2)}) collective-permute-start(f32[5,128,256]{2,1,0:T(8,128)} %get-tuple-element.36), channel_id=1, source_target_pairs={{0,4},{1,5},{2,6},{3,7},{4,0},{5,1},{6,2},{7,3},{8,12},{9,13},{10,... | collective-permute-start | bytes 1966088 | tf_op jit(solution)/shard_map/ppermute | solution.py:369
  4.2 18.6 %collective-permute-start = (f32[5,128,256]{2,1,0:T(8,128)}, f32[5,128,256]{2,1,0:T(8,128)S(1)}, u32[]{:S(2)}, u32[]{:S(2)}) collective-permute-start(f32[5,128,256]{2,1,0:T(8,128)} %get-tuple-element.33), channel_id=1, source_target_pairs={{0,2},{1,3},{2,0},{3,1},{4,8},{5,9},{6,10},{7,11},{8,4},{9,5},{10,... | collective-permute-start | bytes 1966088 | tf_op jit(solution)/shard_map/ppermute | solution.py:369
  6.8 4.5 %collective-permute-start.1 = (f32[8,8,256]{2,1,0:T(8,128)}, f32[8,8,256]{2,1,0:T(8,128)S(1)}, u32[]{:S(2)}, u32[]{:S(2)}) collective-permute-start(f32[8,8,256]{2,1,0:T(8,128)} %get-tuple-element.34), channel_id=1, source_target_pairs={{0,1},{1,0},{2,3},{3,2},{4,5},{5,4},{6,7},{7,6},{8,9},{9,8},{10,11... | collective-permute-start | bytes 196616 | tf_op jit(solution)/shard_map/ppermute | solution.py:369
  8.3 3.0 %collective-permute-start.2 = (f32[8,8,256]{2,1,0:T(8,128)}, f32[8,8,256]{2,1,0:T(8,128)S(1)}, u32[]{:S(2)}, u32[]{:S(2)}) collective-permute-start(f32[8,8,256]{2,1,0:T(8,128)} %get-tuple-element.35), channel_id=1, source_target_pairs={{0,4},{1,2},{2,1},{3,7},{4,0},{5,6},{6,5},{7,3},{8,12},{9,10},{10,... | collective-permute-start | bytes 196616 | tf_op jit(solution)/shard_map/ppermute | solution.py:369
  11.3 8.1 %collective-permute-start.4 = (f32[4,8,256]{2,1,0:T(8,128)S(1)}, f32[4,8,256]{2,1,0:T(8,128)S(1)}, u32[]{:S(2)}, u32[]{:S(2)}) collective-permute-start(f32[4,8,256]{2,1,0:T(8,128)S(1)} %pad_maximum_fusion.1), channel_id=1, source_target_pairs={{0,4},{1,5},{2,6},{3,7},{4,0},{5,1},{6,2},{7,3},{8,12},{9,13},{10,... | collective-permute-start | bytes 98312 | tf_op jit(solution)/shard_map/ppermute | solution.py:369
  11.4 11.4 %collective-permute-start.3 = (f32[4,8,256]{2,1,0:T(8,128)S(1)}, f32[4,8,256]{2,1,0:T(8,128)S(1)}, u32[]{:S(2)}, u32[]{:S(2)}) collective-permute-start(f32[4,8,256]{2,1,0:T(8,128)S(1)} %pad_maximum_fusion), channel_id=1, source_target_pairs={{0,2},{1,3},{2,0},{3,1},{4,8},{5,9},{6,10},{7,11},{8,4},{9,5},{10,... | collective-permute-start | bytes 98312 | tf_op jit(solution)/shard_map/ppermute | solution.py:369

commit v5 on v4

--- a/solution.py
+++ b/solution.py
@@ -34,39 +34,45 @@
     return near, far, ynear, yfar
 
 
-def take_kernel(par, dens, src, far_out, near_out, xs_out, dg_out, dlo, dhi, slo, shi, far_buf, near_buf, xs_buf, dg_buf, sems, out_sems):
+def position(sizes):
+    ix, iy = lax.axis_index("gx"), lax.axis_index("gy")
+    flags = (ix % 2 == 1, iy % 2 == 1, ix > 0, ix < sizes[0] - 1, iy > 0, iy < sizes[1] - 1)
+    return [jnp.where(f, 1, 0) for f in flags]
+
+
+def load_kernel(sizes, dens_hbm, src_hbm, far, near, xs, dg, dens, src, sems):
+    par = position(sizes)
     nx, ny, nz = dens.shape
     xodd, yodd = par[0] == 1, par[1] == 1
-    moves = []
-    for buf, out, d, s in ((far_buf, far_out, jnp.where(xodd, nx - 3, 0), jnp.where(xodd, nx - 2, 0)),
-                           (near_buf, near_out, jnp.where(xodd, 0, nx - 3), jnp.where(xodd, 0, nx - 2))):
-        for ref, first, count, at in ((dens, d, 3, 0), (src, s, 2, 3)):
-            for k in range(count):
-                here = pl.ds(at + k, 1)
-                moves.append((ref.at[pl.ds(first + k, 1)], buf.at[here], out.at[here]))
-    slabs = [(dens.at[:, pl.ds(0, TILE)], dlo), (dens.at[:, pl.ds(ny - TILE, TILE)], dhi),
-             (src.at[:, pl.ds(0, TILE)], slo), (src.at[:, pl.ds(ny - TILE, TILE)], shi)]
-    slabs = [pltpu.make_async_copy(a, b, sems.at[len(moves) + i]) for i, (a, b) in enumerate(slabs)]
-    reads = [pltpu.make_async_copy(a, b, sems.at[i]) for i, (a, b, _) in enumerate(moves)]
-    writes = [pltpu.make_async_copy(b, c, out_sems.at[i]) for i, (_, b, c) in enumerate(moves)]
-    writes += [pltpu.make_async_copy(b, c, out_sems.at[len(moves) + i]) for i, (b, c) in enumerate(((xs_buf, xs_out), (dg_buf, dg_out)))]
-    for copy in slabs + reads:
+    copies = []
+    for k in range(nx):
+        for i, (a, b) in enumerate(((dens_hbm, dens), (src_hbm, src))):
+            copies.append(pltpu.make_async_copy(a.at[pl.ds(k, 1)], b.at[pl.ds(k, 1)], sems.at[2 * k + i]))
+    for copy in copies:
         copy.start()
-    for copy in slabs:
+    for copy in copies:
         copy.wait()
+    for out, d, s in ((far, jnp.where(xodd, nx - 3, 0), jnp.where(xodd, nx - 2, 0)),
+                      (near, jnp.where(xodd, 0, nx - 3), jnp.where(xodd, 0, nx - 2))):
+        for k in range(3):
+            out[k] = dens[d + k]
+        for k in range(2):
+            out[3 + k] = src[s + k]
     row = lax.broadcasted_iota(jnp.int32, (TILE, nz), 0)
     for k in range(nx):
-        down = jnp.where(row < 3, dlo[k], pltpu.roll(slo[k], 4, 0))
-        up = jnp.where(row > 4, dhi[k], pltpu.roll(shi[k], 4, 0))
-        xs_buf[k] = jnp.where(yodd, down, up)
-        dg_buf[k] = jnp.where(yodd, up, down)
-    for copy in writes[len(moves):]:
-        copy.start()
-    for read, write in zip(reads, writes):
-        read.wait()
-        write.start()
-    for copy in writes:
-        copy.wait()
+        down = jnp.where(row < 3, dens[k, :TILE], pltpu.roll(src[k, :TILE], 4, 0))
+        up = jnp.where(row > 4, dens[k, ny - TILE:], pltpu.roll(src[k, ny - TILE:], 4, 0))
+        xs[k] = jnp.where(yodd, down, up)
+        dg[k] = jnp.where(yodd, up, down)
+
+
+def corner_kernel(sizes, rxs, rdg, far, near):
+    xodd = position(sizes)[0] == 1
+    nx = rxs.shape[0]
+    for out, begin in ((far, jnp.where(xodd, nx - 2, 0)), (near, jnp.where(xodd, 0, nx - 2))):
+        for k in range(2):
+            out[k] = rxs[begin + k]
+            out[2 + k] = rdg[begin + k]
 
 
 def halves(nz):
@@ -215,7 +221,8 @@
     return jnp.where(xodd, 1, 4), jnp.where(xodd, 2, 5), jnp.where(xodd, 3, 6), jnp.where(xodd, par[2], par[3])
 
 
-def inner_kernel(par, dens, src, near, dx, sx, wx, wy, wz, sc, g0, g1, w0, n0, mom):
+def inner_kernel(sizes, dens, src, near, dx, sx, wx, wy, wz, sc, g0, g1, w0, n0, mom):
+    par = position(sizes)
     nx, ny, _ = dens.shape
     xodd = par[0] == 1
     first, second, third, has = near_side(par)
@@ -239,7 +246,8 @@
         mom[i] = sums[i]
 
 
-def edge_kernel(par, rxs, rdg, rnc, part, *refs):
+def edge_kernel(sizes, rxs, rdg, rnc, part, *refs):
+    par = position(sizes)
     mom, dx, sx, wx, wy, wz, sc, g0, g1, w0, n0 = refs[10:]
     nx = dx.shape[0] - 2 * DEEP
     ny = dx.shape[2] - 2 * OFF
@@ -263,8 +271,9 @@
         mom[i] = sums[i]
 
 
-def far_kernel(par, far, rfc, part, dx_in, sx_in, wx_in, wy_in, wz_in, sc_in, g0_in, g1_in, w0_in, n0_in,
+def far_kernel(sizes, far, rfc, part, dx_in, sx_in, wx_in, wy_in, wz_in, sc_in, g0_in, g1_in, w0_in, n0_in,
                mom, dx, sx, wx, wy, wz, sc, g0, g1, w0, n0):
+    par = position(sizes)
     ny, _ = far.shape[1:]
     nx = dx.shape[0] - 2 * DEEP
     xodd, yodd = par[0] == 1, par[1] == 1
@@ -349,50 +358,41 @@
     both = ("gx", "gy")
     near_pairs, far_pairs, ynear_pairs, yfar_pairs = swaps(nx_dev, ny_dev)
     nx, ny, nz = density.shape
-    ix, iy = lax.axis_index("gx"), lax.axis_index("gy")
-    xodd = ix % 2
-    flags = [xodd, iy % 2, ix > 0, ix < nx_dev - 1, iy > 0, iy < ny_dev - 1]
-    par = jnp.stack([jnp.asarray(f, jnp.int32) for f in flags])
-    smem = pl.BlockSpec(memory_space=pltpu.SMEM)
+    sizes = (nx_dev, ny_dev)
     vmem = pl.BlockSpec(memory_space=VMEM)
+    hbm = pl.BlockSpec(memory_space=pltpu.HBM)
 
     def call(body, n_in, outs, limit, **more):
-        specs = [smem] + [vmem] * (n_in - 1)
         return pl.pallas_call(
-            body, out_shape=outs, in_specs=specs, out_specs=jax.tree.map(lambda _: vmem, outs),
+            functools.partial(body, sizes), out_shape=outs, in_specs=[vmem] * n_in, out_specs=jax.tree.map(lambda _: vmem, outs),
             compiler_params=pltpu.CompilerParams(vmem_limit_bytes=limit * MIB), **more,
         )
 
-    hbm = pl.BlockSpec(memory_space=pltpu.HBM)
-
     def send(value, pairs):
         return lax.ppermute(value, both, pairs)
 
-    planes, rows = ((5, ny, nz), jnp.float32), ((nx, TILE, nz), jnp.float32)
-    shapes = (planes, planes, rows, rows)
-    far, near, xs, dg = pl.pallas_call(
-        take_kernel, out_shape=tuple(jax.ShapeDtypeStruct(*v) for v in shapes), in_specs=[smem, hbm, hbm], out_specs=(hbm,) * 4,
-        scratch_shapes=[VMEM(*rows)] * 4 + [VMEM(*v) for v in shapes] + [pltpu.SemaphoreType.DMA((14,)), pltpu.SemaphoreType.DMA((12,))],
-        name="take_kernel", compiler_params=pltpu.CompilerParams(vmem_limit_bytes=8 * MIB),
-    )(par, *(pltpu.with_memory_space_constraint(v, pltpu.HBM) for v in (density, source)))
+    planes, rows, block = (VMEM(v, jnp.float32) for v in ((5, ny, nz), (nx, TILE, nz), density.shape))
+    shapes = (planes, planes, rows, rows, block, block)
+    far, near, xs, dg, dens, src = pl.pallas_call(
+        functools.partial(load_kernel, sizes), out_shape=shapes, in_specs=[hbm] * 2, out_specs=(vmem,) * 6, name="load_kernel",
+        scratch_shapes=[pltpu.SemaphoreType.DMA((2 * nx,))], compiler_params=pltpu.CompilerParams(vmem_limit_bytes=8 * MIB),
+    )(*(pltpu.with_memory_space_constraint(v, pltpu.HBM) for v in (density, source)))
+    far = send(far, far_pairs)
     near = send(near, near_pairs)
     rxs = send(xs, ynear_pairs)
     rdg = send(dg, yfar_pairs)
-    far = send(far, far_pairs)
-
-    def corner(begin):
-        return jnp.concatenate([lax.dynamic_slice_in_dim(v, begin, 2, 0) for v in (rxs, rdg)], axis=0)
-
-    rfc = send(corner(jnp.where(xodd == 1, nx - 2, 0)), far_pairs)
-    rnc = send(corner(jnp.where(xodd == 1, 0, nx - 2)), near_pairs)
+    corner = VMEM((4, TILE, nz), jnp.float32)
+    rfc, rnc = call(corner_kernel, 2, (corner, corner), 4)(rxs, rdg)
+    rfc = send(rfc, far_pairs)
+    rnc = send(rnc, near_pairs)
 
     ext = VMEM((nx + 2 * DEEP, nz // LANES, ny + 2 * OFF, LANES), jnp.float32)
     sums = VMEM((SUMS, TILE, LANES), jnp.float32)
-    *held, part = call(inner_kernel, 4, (ext,) * 10 + (sums,), 8)(par, density, source, near)
-    part, *held = call(edge_kernel, 15, (sums,) + (ext,) * 10, 8, input_output_aliases={5 + k: 1 + k for k in range(10)})(
-        par, rxs, rdg, rnc, part, *held)
-    mom, *held = call(far_kernel, 14, (VMEM((1, LANES), jnp.float32),) + (ext,) * 10, 8, input_output_aliases={4 + k: 1 + k for k in range(10)})(
-        par, far, rfc, part, *held)
+    *held, part = call(inner_kernel, 3, (ext,) * 10 + (sums,), 8)(dens, src, near)
+    part, *held = call(edge_kernel, 14, (sums,) + (ext,) * 10, 8, input_output_aliases={4 + k: 1 + k for k in range(10)})(
+        rxs, rdg, rnc, part, *held)
+    mom, *held = call(far_kernel, 13, (VMEM((1, LANES), jnp.float32),) + (ext,) * 10, 8, input_output_aliases={3 + k: 1 + k for k in range(10)})(
+        far, rfc, part, *held)
     _, sx, _, _, _, sc, _, _, w0, n0 = held
 
     n = nx_dev * ny_dev

time: 38.3 us -> 35.2 us (0.919)
  Pallas kernels: 15 us -> 12.3 us
    pallas_call x4 -> x5, Pallas kernels: 13.3 us -> 10.5 us  [the longest x1 3.72 us: shards(): call(inner_kernel, 3, (ext,) * 10 + (sums,), 8)(dens, src, near)]
  transfers between devices with their start and end apart: 6 -> 6, of which waited for: 1 -> 1; matrix products, arithmetic and copies ran while one was open for 0% -> 0% of each run, Pallas kernels for 20% -> 19%
where the time goes in v5:
time: 35.2 us; the launch traced here: 35 us
  Pallas kernels  12.3 us (35%)
  blocking collectives  10.9 us (31%)
  starting transfers between devices  8.33 us (24%)
  waiting for transfers between devices  2.78 us (8%)
  between operations  0.69 us (2%)
    all_to_all x1, blocking collectives, shards(): got = lax.all_to_all(sent, both, 0, 0, tiled=True).reshape(n, LANES)  10.9 us
    ppermute x6, starting transfers between devices, send(): return lax.ppermute(value, both, pairs)  8.33 us
    pallas_call x1, Pallas kernels, shards(): call(inner_kernel, 3, (ext,) * 10 + (sums,), 8)(dens, src, near)  3.72 us
    pallas_call x1, Pallas kernels, shards(): call(edge_kernel, 14, (sums,) + (ext,) * 10, 8, input_output_aliases={4 +...  2.85 us
    ppermute x6, waiting for transfers between devices, send(): return lax.ppermute(value, both, pairs)  2.78 us
    pallas_call x1, Pallas kernels, shards(): call(far_kernel, 13, (VMEM((1, LANES), jnp.float32),) + (ext,) * 10, 8, i...  2.12 us
    pallas_call x1, Pallas kernels, shards(): pl.pallas_call(functools.partial(load_kernel, sizes), out_shape=shapes, i...  1.84 us
    pallas_call x1, Pallas kernels, shards(): pl.pallas_call(last_kernel, out_shape=(whole, whole), in_specs=[vmem] * 5...  1.73 us
  transfers between devices with their start and end apart: 6, of which 1 were waited for; matrix products, arithmetic and copies ran while one was open for 0% of the time, Pallas kernels for 19%

profile of v5, /device:TPU:0, one launch (start us, length us, event | category | flops | bytes accessed | tf_op | source)
XLA Modules:
  0.0 35.0 jit_solution(14548263159444058995)
XLA Ops:
  0.6 1.8 %load_kernel.1 = (f32[5,128,256]{2,1,0:T(8,128)S(1)}, f32[5,128,256]{2,1,0:T(8,128)S(1)}, f32[8,8,256]{2,1,0:T(8,128)S(1)}, f32[8,8,256]{2,1,0:T(8,128)S(1)}, f3...) custom-call(f32[8,128,256]{2,1,0:T(8,128)} %dens_hbm.1, f32[8,128,256]{2,1,0:T(8,128)} %src_hbm.1), custom_call_target="tpu_custom_call" | custom-call | tf_op jit(solution)/shard_map/load_kernel/pallas_call | solution.py:376
  2.5 0.6 %collective-permute-start.5 = (f32[5,128,256]{2,1,0:T(8,128)S(1)}, f32[5,128,256]{2,1,0:T(8,128)S(1)}, u32[]{:S(2)}, u32[]{:S(2)}) collective-permute-start(f32[5,128,256]{2,1,0:T(8,128)S(1)} %get-tuple-element.44), channel_id=1, source_target_pairs={{0,4},{1,5},{2,6},{3,7},{4,0},{5,1},{6,2},{7,3},{8,12},{9,13},{10,... | collective-permute-start | bytes 1966088 | tf_op jit(solution)/shard_map/ppermute | solution.py:372
  3.0 2.6 %collective-permute-start = (f32[5,128,256]{2,1,0:T(8,128)S(1)}, f32[5,128,256]{2,1,0:T(8,128)S(1)}, u32[]{:S(2)}, u32[]{:S(2)}) collective-permute-start(f32[5,128,256]{2,1,0:T(8,128)S(1)} %get-tuple-element.37), channel_id=1, source_target_pairs={{0,2},{1,3},{2,0},{3,1},{4,8},{5,9},{6,10},{7,11},{8,4},{9,5},{10,... | collective-permute-start | bytes 1966088 | tf_op jit(solution)/shard_map/ppermute | solution.py:372
  5.6 1.5 %collective-permute-start.1 = (f32[8,8,256]{2,1,0:T(8,128)S(1)}, f32[8,8,256]{2,1,0:T(8,128)S(1)}, u32[]{:S(2)}, u32[]{:S(2)}) collective-permute-start(f32[8,8,256]{2,1,0:T(8,128)S(1)} %get-tuple-element.38), channel_id=1, source_target_pairs={{0,1},{1,0},{2,3},{3,2},{4,5},{5,4},{6,7},{7,6},{8,9},{9,8},{10,11... | collective-permute-start | bytes 196616 | tf_op jit(solution)/shard_map/ppermute | solution.py:372
  7.1 0.0 collective-permute-start.2
  7.1 2.8 %collective-permute-done.1.rxs = f32[8,8,256]{2,1,0:T(8,128)S(1)} collective-permute-done((f32[8,8,256]{2,1,0:T(8,128)S(1)}, f32[8,8,256]{2,1,0:T(8,128)S(1)}, u32[]{:S(2)}, u32[]{:S(2)}) %collective-permute-start.1) | collective-permute-done | bytes 65568 | tf_op jit(solution)/shard_map/ppermute | solution.py:372
  9.9 0.0 collective-permute-done.2.rdg
  9.9 0.1 collective-permute-start.4
  10.0 3.6 %collective-permute-start.3 = (f32[4,8,256]{2,1,0:T(8,128)S(1)}, f32[4,8,256]{2,1,0:T(8,128)S(1)}, u32[]{:S(2)}, u32[]{:S(2)}) collective-permute-start(f32[4,8,256]{2,1,0:T(8,128)S(1)} %get-tuple-element.40), channel_id=1, source_target_pairs={{0,2},{1,3},{2,0},{3,1},{4,8},{5,9},{6,10},{7,11},{8,4},{9,5},{10,... | collective-permute-start | bytes 98312 | tf_op jit(solution)/shard_map/ppermute | solution.py:372
  13.6 0.0 collective-permute-done.5.near
  13.6 3.7 %shard_map.42 = (f32[14,2,160,128]{3,2,1,0:T(8,128)S(1)}, f32[14,2,160,128]{3,2,1,0:T(8,128)S(1)}, f32[14,2,160,128]{3,2,1,0:T(8,128)S(1)}, f32[14,2,160,128]{3,...) custom-call(f32[8,128,256]{2,1,0:T(8,128)S(1)} %get-tuple-element.42, ...), custom_call_target="tpu_custom_call" | custom-call | tf_op jit(solution)/shard_map/pallas_call | solution.py:391
  17.3 0.0 collective-permute-done.4.rnc
  17.3 2.8 %shard_map.43 = (f32[5,8,128]{2,1,0:T(8,128)S(1)}, f32[14,2,160,128]{3,2,1,0:T(8,128)S(1)}, f32[14,2,160,128]{3,2,1,0:T(8,128)S(1)}, f32[14,2,160,128]{3,2,1,0:T...) custom-call(f32[8,8,256]{2,1,0:T(8,128)S(1)} %collective-permute-don, ...), custom_call_target="tpu_custom_call", output_to_operand_aliasing={{1}: (4, {}), {2}: (5, {}), {3}: (6, {}), {4}: (7, {}), {5}... | custom-call | tf_op jit(solution)/shard_map/pallas_call | solution.py:392
  20.2 0.0 collective-permute-done.3.rfc
  20.2 0.0 collective-permute-done.far
  20.2 2.1 %shard_map.44 = (f32[1,128]{1,0:T(1,128)S(1)}, f32[14,2,160,128]{3,2,1,0:T(8,128)S(1)}, f32[14,2,160,128]{3,2,1,0:T(8,128)S(1)}, f32[14,2,160,128]{3,2,1,0:T(8,1...) custom-call(f32[5,128,256]{2,1,0:T(8,128)S(1)} %collective-permute-d, ...), custom_call_target="tpu_custom_call", output_to_operand_aliasing={{1}: (3, {}), {2}: (4, {}), {3}: (5, {}), {4}: (6, {}), {5}... | custom-call | tf_op jit(solution)/shard_map/pallas_call | solution.py:394
  22.4 10.9 %all_to_all.5 = f32[32,1,128]{2,1,0:T(1,128)S(1)} all-to-all(f32[32,1,128]{2,1,0:T(1,128)S(1)} %broadcast_in_dim.9), channel_id=1, replica_groups=mesh['gx'=8,'gy'=4] {'gx','gy'}, dimensions={0} | all-to-all | bytes 32768 | tf_op jit(solution)/shard_map/all_to_all | solution.py:400
  33.3 1.7 %last_kernel.1 = (f32[8,128,256]{2,1,0:T(8,128)}, f32[8,128,256]{2,1,0:T(8,128)}) custom-call(f32[32,128]{1,0:T(8,128)S(1)} %bitcast.2, f32[14,2,160,128]{3,2,1,0:T(8,128)S(1)} %get-tuple-element.68.sx, f32[14,2,160,128]{3,2,1,0:T(8,128)S(1)} %get-tuple-element.69.sc, f32[14,2,160,128]{3,2,1,0:T(8,128)S(1)} %get-tuple-element.70.w0, ...), custom_call_target="tpu_custom_call" | custom-call | tf_op jit(solution)/shard_map/last_kernel/pallas_call | solution.py:403
  (2 shorter events, 0.0 us)
Async XLA Ops:
  2.5 11.1 %collective-permute-start.5 = (f32[5,128,256]{2,1,0:T(8,128)S(1)}, f32[5,128,256]{2,1,0:T(8,128)S(1)}, u32[]{:S(2)}, u32[]{:S(2)}) collective-permute-start(f32[5,128,256]{2,1,0:T(8,128)S(1)} %get-tuple-element.44), channel_id=1, source_target_pairs={{0,4},{1,5},{2,6},{3,7},{4,0},{5,1},{6,2},{7,3},{8,12},{9,13},{10,... | collective-permute-start | bytes 1966088 | tf_op jit(solution)/shard_map/ppermute | solution.py:372
  3.0 17.2 %collective-permute-start = (f32[5,128,256]{2,1,0:T(8,128)S(1)}, f32[5,128,256]{2,1,0:T(8,128)S(1)}, u32[]{:S(2)}, u32[]{:S(2)}) collective-permute-start(f32[5,128,256]{2,1,0:T(8,128)S(1)} %get-tuple-element.37), channel_id=1, source_target_pairs={{0,2},{1,3},{2,0},{3,1},{4,8},{5,9},{6,10},{7,11},{8,4},{9,5},{10,... | collective-permute-start | bytes 1966088 | tf_op jit(solution)/shard_map/ppermute | solution.py:372
  5.6 4.3 %collective-permute-start.1 = (f32[8,8,256]{2,1,0:T(8,128)S(1)}, f32[8,8,256]{2,1,0:T(8,128)S(1)}, u32[]{:S(2)}, u32[]{:S(2)}) collective-permute-start(f32[8,8,256]{2,1,0:T(8,128)S(1)} %get-tuple-element.38), channel_id=1, source_target_pairs={{0,1},{1,0},{2,3},{3,2},{4,5},{5,4},{6,7},{7,6},{8,9},{9,8},{10,11... | collective-permute-start | bytes 196616 | tf_op jit(solution)/shard_map/ppermute | solution.py:372
  7.1 2.8 %collective-permute-start.2 = (f32[8,8,256]{2,1,0:T(8,128)S(1)}, f32[8,8,256]{2,1,0:T(8,128)S(1)}, u32[]{:S(2)}, u32[]{:S(2)}) collective-permute-start(f32[8,8,256]{2,1,0:T(8,128)S(1)} %get-tuple-element.39), channel_id=1, source_target_pairs={{0,4},{1,2},{2,1},{3,7},{4,0},{5,6},{6,5},{7,3},{8,12},{9,10},{10,... | collective-permute-start | bytes 196616 | tf_op jit(solution)/shard_map/ppermute | solution.py:372
  9.9 7.4 %collective-permute-start.4 = (f32[4,8,256]{2,1,0:T(8,128)S(1)}, f32[4,8,256]{2,1,0:T(8,128)S(1)}, u32[]{:S(2)}, u32[]{:S(2)}) collective-permute-start(f32[4,8,256]{2,1,0:T(8,128)S(1)} %get-tuple-element.41), channel_id=1, source_target_pairs={{0,4},{1,5},{2,6},{3,7},{4,0},{5,1},{6,2},{7,3},{8,12},{9,13},{10,... | collective-permute-start | bytes 98312 | tf_op jit(solution)/shard_map/ppermute | solution.py:372
  10.0 10.2 %collective-permute-start.3 = (f32[4,8,256]{2,1,0:T(8,128)S(1)}, f32[4,8,256]{2,1,0:T(8,128)S(1)}, u32[]{:S(2)}, u32[]{:S(2)}) collective-permute-start(f32[4,8,256]{2,1,0:T(8,128)S(1)} %get-tuple-element.40), channel_id=1, source_target_pairs={{0,2},{1,3},{2,0},{3,1},{4,8},{5,9},{6,10},{7,11},{8,4},{9,5},{10,... | collective-permute-start | bytes 98312 | tf_op jit(solution)/shard_map/ppermute | solution.py:372

commit v6 on v5

v6 whole, which is shorter than its diff:
```python
import functools

import jax
import jax.numpy as jnp
from jax import lax
from jax.experimental import pallas as pl
from jax.experimental.pallas import tpu as pltpu
from jax.sharding import PartitionSpec as P


TILE = 8
LANES = 128
OFF = 16
DEEP = 3
ROWS = 5
PART = 16
SUMS = 5
MIB = 1 << 20
VMEM = pltpu.VMEM


def swaps(nx, ny):
    at = lambda x, y: x * ny + y
    near, far, ynear, yfar = [], [], [], []
    for x in range(nx):
        for y in range(ny):
            near.append((at(x, y), at(x ^ 1, y)))
            other = x - 1 if x % 2 == 0 else x + 1
            inside = 0 <= other < nx
            far.append((at(x, y), at(other, y) if inside else at(x, (y + ny // 2) % ny)))
            ynear.append((at(x, y), at(x, y ^ 1)))
            beside = y - 1 if y % 2 == 0 else y + 1
            within = 0 <= beside < ny
            yfar.append((at(x, y), at(x, beside) if within else at(x ^ 1, y)))
    return near, far, ynear, yfar


def position(sizes):
    ix, iy = lax.axis_index("gx"), lax.axis_index("gy")
    flags = (ix % 2 == 1, iy % 2 == 1, ix > 0, ix < sizes[0] - 1, iy > 0, iy < sizes[1] - 1)
    return [jnp.where(f, 1, 0) for f in flags]


def load_kernel(sizes, dens_hbm, src_hbm, far, near, xs, dg, dens, src, tall, sems):
    par = position(sizes)
    nx, ny, nz = dens.shape
    xodd, yodd = par[0] == 1, par[1] == 1
    order = [jnp.where(xodd, nx - 1 - k, k) for k in range(nx)]
    copies = []
    for k, at in enumerate(order):
        for i, (a, b) in enumerate(((dens_hbm, dens), (src_hbm, src))):
            copies.append(pltpu.make_async_copy(a.at[pl.ds(at, 1)], b.at[pl.ds(at, 1)], sems.at[2 * k + i]))
    for copy in copies:
        copy.start()
    for copy in copies[:6]:
        copy.wait()
    far[0] = dens[order[0]]
    far[1] = dens[order[1]]
    far[2] = src[order[0]]
    second = dens[order[1]]
    put_plane(tall, 0, slice(TILE, TILE + ny), 0.5 * second)
    lane = lax.broadcasted_iota(jnp.int32, (TILE, LANES), 1)
    inner, first = lane < LANES - 1, lane == 0
    for r in range(0, ny, TILE):
        here = pl.ds(r + TILE, TILE)
        c = [tall[0, h, here] for h, _ in halves(nz)]
        z_up, z_down, _ = depth_weights(c, inner, first)
        for h, lanes in halves(nz):
            beside = [0.5 * dens[order[k], pl.ds(r, TILE), lanes] for k in (0, 2)]
            beside += [tall[0, h, pl.ds(r + TILE + 1, TILE)], tall[0, h, pl.ds(r + TILE - 1, TILE)]]
            w = [1.0 / (c[h] + v) for v in beside]
            s = lax.rsqrt((w[0] + w[1]) + (w[2] + w[3]) + (z_up[h] + z_down[h]))
            far[3, pl.ds(r, TILE), lanes] = s * (s * src[order[1], pl.ds(r, TILE), lanes])
    for copy in copies[6:]:
        copy.wait()
    d, s = jnp.where(xodd, 0, nx - 3), jnp.where(xodd, 0, nx - 2)
    for k in range(3):
        near[k] = dens[d + k]
    for k in range(2):
        near[3 + k] = src[s + k]
    for j in range(ROWS):
        ref, at = (dens, j) if j < DEEP else (src, j - DEEP)
        down, up = ref[:, at, :], ref[:, ny - 1 - at, :]
        xs[j] = jnp.where(yodd, down, up)
        dg[j] = jnp.where(yodd, up, down)


def corner_kernel(sizes, rxs, rdg, dens, src, far, near):
    par = position(sizes)
    xodd, yodd = par[0] == 1, par[1] == 1
    nx, ny, _ = dens.shape
    for out, backward in ((far, xodd), (near, jnp.logical_not(xodd))):
        at = [jnp.where(backward, nx - 1 - k, k) for k in range(3)]
        for k in range(2):
            for j in range(ROWS):
                a, b = rxs[j, pl.ds(at[k], 1), :], rdg[j, pl.ds(at[k], 1), :]
                out[k, j:j + 1] = jnp.where(yodd, a, b)
                out[2 + k, j:j + 1] = jnp.where(yodd, b, a)
        for side, row in ((0, 0), (1, ny - 1)):
            out[2 * side + 1, ROWS:ROWS + 1] = dens[at[2], row:row + 1]
            out[2 * side + 1, ROWS + 1:ROWS + 2] = src[at[1], row:row + 1]


class Stores:
    def __init__(self, depth):
        self.depth, self.held = depth, []

    def put(self, items):
        self.held.append(items)
        if len(self.held) > self.depth:
            self.flush(1)

    def flush(self, count=None):
        for items in self.held[:count]:
            for ref, at, value in items:
                ref[at] = value
        self.held = [] if count is None else self.held[count:]


def halves(nz):
    return [(h, slice(h * LANES, (h + 1) * LANES)) for h in range(nz // LANES)]


def loop(count, step):
    def body(k, carry):
        step(k)
        return carry

    lax.fori_loop(0, count, body, 0)


def put_plane(ref, e, rows, value):
    for h, lanes in halves(value.shape[-1]):
        ref[e, h, rows] = value[:, lanes]


def put_row(dx, sx, planes, ny, j, low, high):
    ref, depth = (dx, j) if j < DEEP else (sx, j - DEEP)
    if j < DEEP:
        low, high = 0.5 * low, 0.5 * high
    for value, at in ((low, OFF - 1 - depth), (high, OFF + ny + depth)):
        for h, lanes in halves(value.shape[-1]):
            ref[planes, h, at, :] = value[:, lanes]


def depth_weights(c, inner, first):
    nh = len(c)
    turned = [pltpu.roll(v, LANES - 1, 1) for v in c]
    z_up, z_in = [], []
    for h in range(nh):
        w = 1.0 / (c[h] + jnp.where(inner, turned[h], turned[h + 1] if h + 1 < nh else 0.0))
        z_up.append(w)
        z_in.append(w if h + 1 < nh else jnp.where(inner, w, 0.0))
    back = [pltpu.roll(v, 1, 1) for v in z_in]
    z_down = [jnp.where(first, back[h - 1] if h else 1.0 / c[0], back[h]) for h in range(nh)]
    return z_up, z_down, z_in


def weigh(dx, sx, wx, wy, wz, sc, g0, lo, count, tiles, unroll=1):
    nh = dx.shape[1]
    lane = lax.broadcasted_iota(jnp.int32, (TILE, LANES), 1)
    inner, first = lane < LANES - 1, lane == 0
    for r in tiles:
        for h in range(nh):
            wx[lo - 1, h, pl.ds(r, TILE)] = 1.0 / (dx[lo - 1, h, pl.ds(r, TILE)] + dx[lo, h, pl.ds(r, TILE)])

    def plane(k, carry):
        e = lo + k
        stores = Stores(1)
        for r in tiles:
            here = pl.ds(r, TILE)
            c = [dx[e, h, here] for h in range(nh)]
            beside = [(dx[e + 1, h, here], wx[e - 1, h, here], dx[e, h, pl.ds(r + 1, TILE)], dx[e, h, pl.ds(r - 1, TILE)], sx[e, h, here])
                      for h in range(nh)]
            z_up, z_down, z_in = depth_weights(c, inner, first)
            items = [(wz, (e, h, here), z_in[h]) for h in range(nh)]
            for h in range(nh):
                above, x_down, after, before, source = beside[h]
                x_up = 1.0 / (c[h] + above)
                y_up = 1.0 / (c[h] + after)
                y_down = 1.0 / (c[h] + before)
                diag = (x_up + x_down) + (y_up + y_down) + (z_up[h] + z_down[h])
                s = lax.rsqrt(diag)
                items += [(wx, (e, h, here), x_up), (wy, (e, h, here), y_up), (sc, (e, h, here), s), (g0, (e, h, here), s * (s * source))]
            stores.put(items)
        stores.flush()
        return carry

    lax.fori_loop(0, count, plane, 0, unroll=unroll)


def couple(g, wx, wy, wz, e, r, nh, inner, first):
    here = pl.ds(r, TILE)
    c = [g[e, h, here] for h in range(nh)]
    w = [wz[e, h, here] for h in range(nh)]
    ahead = [pltpu.roll(v, LANES - 1, 1) for v in c]
    behind = [pltpu.roll(a * b, 1, 1) for a, b in zip(w, c)]
    out = []
    for h in range(nh):
        t = wx[e, h, here] * g[e + 1, h, here] + wx[e - 1, h, here] * g[e - 1, h, here]
        t = t + (wy[e, h, here] * g[e, h, pl.ds(r + 1, TILE)] + wy[e, h, pl.ds(r - 1, TILE)] * g[e, h, pl.ds(r - 1, TILE)])
        after = jnp.where(inner, ahead[h], ahead[h + 1]) if h + 1 < nh else ahead[h]
        before = jnp.where(first, behind[h - 1], behind[h])
        out.append(t + (w[h] * after + before))
    return out


def apply_first(sx, wx, wy, wz, sc, g0, g1, w0, lo, count, tiles, unroll=1):
    nh = sx.shape[1]
    lane = lax.broadcasted_iota(jnp.int32, (TILE, LANES), 1)
    inner, first = lane < LANES - 1, lane == 0

    def plane(k, carry):
        e = lo + k
        stores = Stores(1)
        for r in tiles:
            here = pl.ds(r, TILE)
            t = couple(g0, wx, wy, wz, e, r, nh, inner, first)
            items = []
            for h in range(nh):
                s = sc[e, h, here]
                v = s * sx[e, h, here] - s * t[h]
                items += [(w0, (e, h, here), v), (g1, (e, h, here), s * v)]
            stores.put(items)
        stores.flush()
        return carry

    lax.fori_loop(0, count, plane, 0, unroll=unroll)


def clear_rows(par, g1):
    _, nh, rows, _ = g1.shape
    zero = jnp.zeros((TILE, LANES), jnp.float32)
    for flag, at in ((par[4], OFF - TILE), (par[5], rows - OFF)):

        @pl.when(flag == 0)
        def _():
            for k in range(g1.shape[0]):
                for h in range(nh):
                    g1[k, h, pl.ds(at, TILE)] = zero


def clear_plane(g1, e, has, tiles):
    zero = jnp.zeros((TILE, LANES), jnp.float32)

    @pl.when(has == 0)
    def _():
        for r in tiles:
            for h in range(g1.shape[1]):
                g1[e, h, pl.ds(r, TILE)] = zero


def apply_second(sx, wx, wy, wz, sc, g1, w0, n0, lo, count, tiles, sums, unroll=1):
    nh = sx.shape[1]
    lane = lax.broadcasted_iota(jnp.int32, (TILE, LANES), 1)
    inner, first = lane < LANES - 1, lane == 0

    def plane(k, sums):
        e = lo + k
        sums = list(sums)
        stores = Stores(2)
        for r in tiles:
            t = couple(g1, wx, wy, wz, e, r, nh, inner, first)
            for h in range(nh):
                s = sc[e, h, pl.ds(r, TILE)]
                a = s * sx[e, h, pl.ds(r, TILE)]
                b = w0[e, h, pl.ds(r, TILE)]
                c = b - s * t[h]
                stores.put([(n0, (e, h, pl.ds(r, TILE)), c)])
                for i, term in enumerate((a * a, b * a, b * b, c * b, c * a)):
                    sums[i] = sums[i] + term
        stores.flush()
        return tuple(sums)

    return lax.fori_loop(0, count, plane, tuple(sums), unroll=unroll)


def beyond(nx, upper, depth):
    return jnp.where(upper, nx + DEEP - 1 + depth, DEEP - depth)


def put_corners(dx, sx, corners, upper, has_down, has_up):
    nx, ny = dx.shape[0] - 2 * DEEP, dx.shape[2] - 2 * OFF
    for k in range(2):
        e = beyond(nx, upper, k + 1)
        for j in range(ROWS):
            low, high = corners[k, j:j + 1], corners[2 + k, j:j + 1]
            put_row(dx, sx, pl.ds(e, 1), ny, j, jnp.where(has_down, low, 0.0), jnp.where(has_up, high, 0.0))


def row_tiles(ny, inset):
    return list(range(OFF + inset * TILE, OFF + ny - inset * TILE, TILE))


def outer_tiles(ny, reach, inset):
    inside = row_tiles(ny, inset)
    return [r for r in row_tiles(ny, -reach) if r not in inside]


def near_side(par):
    xodd = par[0] == 1
    return jnp.where(xodd, 1, 4), jnp.where(xodd, 2, 5), jnp.where(xodd, 3, 6), jnp.where(xodd, par[2], par[3])


def inner_kernel(sizes, dens, src, near, dx, sx, wx, wy, wz, sc, g0, g1, w0):
    par = position(sizes)
    nx, ny, _ = dens.shape
    xodd = par[0] == 1
    first, second, _, has = near_side(par)
    has_near = has == 1
    own = slice(OFF, OFF + ny)

    def fill(k):
        put_plane(dx, k + DEEP, own, 0.5 * dens[k])
        put_plane(sx, k + DEEP, own, src[k])

    loop(nx, fill)
    near_third, near_beyond = jnp.where(xodd, 0, nx + 3), jnp.where(xodd, 1, nx + 3)
    loop(3, lambda k: put_plane(dx, near_third + k, own, jnp.where(has_near, 0.5 * near[k], 0.0)))
    loop(2, lambda k: put_plane(sx, near_beyond + k, own, jnp.where(has_near, near[3 + k], 0.0)))
    weigh(dx, sx, wx, wy, wz, sc, g0, first, nx + 1, row_tiles(ny, 1), unroll=3)
    apply_first(sx, wx, wy, wz, sc, g0, g1, w0, second, nx - 1, row_tiles(ny, 2), unroll=7)
    clear_plane(g1, jnp.where(xodd, 2, nx + 3), has, row_tiles(ny, 2))


def inner_second_kernel(sizes, sx, wx, wy, wz, sc, g1, w0, n0, mom):
    par = position(sizes)
    nx, ny = sx.shape[0] - 2 * DEEP, sx.shape[2] - 2 * OFF
    third = near_side(par)[2]
    zero = jnp.zeros((TILE, LANES), jnp.float32)
    sums = apply_second(sx, wx, wy, wz, sc, g1, w0, n0, third, nx - 3, row_tiles(ny, 3), (zero,) * SUMS, unroll=5)
    for i in range(SUMS):
        mom[i] = sums[i]


def edge_kernel(sizes, rxs, rdg, rnc, part, *refs):
    par = position(sizes)
    mom, dx, sx, wx, wy, wz, sc, g0, g1, w0, n0 = refs[10:]
    nx = dx.shape[0] - 2 * DEEP
    ny = dx.shape[2] - 2 * OFF
    xodd, yodd = par[0] == 1, par[1] == 1
    first, second, third, has = near_side(par)
    has_near, has_down, has_up = has == 1, par[4] == 1, par[5] == 1
    for j in range(ROWS):
        a, b = rxs[j], rdg[j]
        low, high = jnp.where(yodd, a, b), jnp.where(yodd, b, a)
        put_row(dx, sx, pl.ds(DEEP, nx), ny, j, jnp.where(has_down, low, 0.0), jnp.where(has_up, high, 0.0))
    put_corners(dx, sx, rnc, jnp.logical_not(xodd), jnp.logical_and(has_near, has_down), jnp.logical_and(has_near, has_up))
    weigh(dx, sx, wx, wy, wz, sc, g0, first, nx + 1, outer_tiles(ny, 1, 1), unroll=3)
    apply_first(sx, wx, wy, wz, sc, g0, g1, w0, second, nx - 1, outer_tiles(ny, 1, 2), unroll=7)
    clear_plane(g1, jnp.where(xodd, 2, nx + 3), has, outer_tiles(ny, 1, 2))
    clear_rows(par, g1)
    sums = apply_second(sx, wx, wy, wz, sc, g1, w0, n0, third, nx - 3, outer_tiles(ny, 0, 3), [part[i] for i in range(SUMS)], unroll=5)
    for i in range(SUMS):
        mom[i] = sums[i]


def far_kernel(sizes, far, rfc, part, dx_in, sx_in, wx_in, wy_in, wz_in, sc_in, g0_in, g1_in, w0_in, n0_in,
               mom, dx, sx, wx, wy, wz, sc, g0, g1, w0, n0):
    par = position(sizes)
    ny, nz = far.shape[1:]
    nx = dx.shape[0] - 2 * DEEP
    xodd = par[0] == 1
    has = jnp.where(xodd, par[3], par[2])
    has_far = has == 1
    has_down, has_up = jnp.logical_and(has_far, par[4] == 1), jnp.logical_and(has_far, par[5] == 1)
    own = slice(OFF, OFF + ny)
    e1, e2, _ = (beyond(nx, xodd, d) for d in (1, 2, 3))
    put_plane(dx, e1, own, jnp.where(has_far, 0.5 * far[0], 0.0))
    put_plane(dx, e2, own, jnp.where(has_far, 0.5 * far[1], 0.0))
    put_plane(sx, e1, own, jnp.where(has_far, far[2], 0.0))
    put_plane(g0, e2, own, jnp.where(has_far, far[3], 0.0))
    put_corners(dx, sx, rfc, xodd, has_down, has_up)
    lane = lax.broadcasted_iota(jnp.int32, (TILE, LANES), 1)
    row = lax.broadcasted_iota(jnp.int32, (TILE, LANES), 0)
    inner, first = lane < LANES - 1, lane == 0
    for side, r in ((0, OFF), (1, OFF + ny - TILE)):
        here = pl.ds(r, TILE)
        c = [dx[e2, h, here] for h, _ in halves(nz)]
        z_up, z_down, _ = depth_weights(c, inner, first)
        for h, lanes in halves(nz):
            third = jnp.where(has_far, 0.5 * rfc[2 * side + 1, ROWS:ROWS + 1, lanes], 0.0)
            source = jnp.where(has_far, rfc[2 * side + 1, ROWS + 1:ROWS + 2, lanes], 0.0)
            w = [1.0 / (c[h] + v) for v in (third, dx[e1, h, here], dx[e2, h, pl.ds(r + 1, TILE)], dx[e2, h, pl.ds(r - 1, TILE)])]
            s = lax.rsqrt((w[0] + w[1]) + (w[2] + w[3]) + (z_up[h] + z_down[h]))
            g0[e2, h, here] = jnp.where(row == side * (TILE - 1), s * (s * source), g0[e2, h, here])
    weigh(dx, sx, wx, wy, wz, sc, g0, jnp.where(xodd, nx + 2, 2), 2, row_tiles(ny, -1))
    apply_first(sx, wx, wy, wz, sc, g0, g1, w0, jnp.where(xodd, nx + 1, 2), 3, row_tiles(ny, -1), unroll=3)
    clear_plane(g1, e1, has, row_tiles(ny, -1))
    clear_rows(par, g1)
    sums = apply_second(sx, wx, wy, wz, sc, g1, w0, n0, jnp.where(xodd, nx, 3), 3, row_tiles(ny, 0), [part[i] for i in range(SUMS)], unroll=3)
    place = lax.broadcasted_iota(jnp.int32, (1, LANES), 1) // PART
    out = jnp.zeros((1, LANES), jnp.float32)
    for k, v in enumerate(sums):
        p = jnp.sum(v, axis=0, keepdims=True)
        width = LANES // 2
        while width >= PART:
            p = p + pltpu.roll(p, width, 1)
            width //= 2
        out = jnp.where(place == k, p, out)
    mom[...] = out


def last_kernel(mom, sx, sc, w0, n0, p_out, r_out, p_buf, r_buf, sems):
    place = lax.broadcasted_iota(jnp.int32, mom.shape, 1) // PART
    m = mom[...]

    def whole(v):
        return jnp.sum(jnp.sum(v, axis=0, keepdims=True), axis=1, keepdims=True)

    def lanes(k):
        return pltpu.roll(m, (LANES - k * PART) % LANES, 1) if k else m

    head = place == 0
    m0, m1, m2, m3, m4 = (jnp.where(head, lanes(k), 0.0) for k in range(SUMS))
    gamma0 = whole(m0)
    delta0 = whole(m1)
    a0 = gamma0 / delta0
    gamma1 = whole(m0 - a0 * (m1 + m1 - a0 * m2))
    delta1 = whole(m1 - a0 * (m4 + m2 - a0 * m3))
    b1 = gamma1 / gamma0
    a1 = gamma1 / (delta1 - b1 * gamma1 / a0)
    nx, ny, nz = p_out.shape
    c = jnp.broadcast_to(a0 + (a1 + a1 * b1), (TILE, LANES))
    d = jnp.broadcast_to(a0 * a1, (TILE, LANES))

    def out(i):
        return (pltpu.make_async_copy(p_buf.at[pl.ds(i, 1)], p_out.at[pl.ds(i, 1)], sems.at[0, i]),
                pltpu.make_async_copy(r_buf.at[pl.ds(i, 1)], r_out.at[pl.ds(i, 1)], sems.at[1, i]))

    def plane(i, carry):
        e = i + DEEP
        for r in range(0, ny, TILE):
            for h, at in halves(nz):
                here = pl.ds(OFF + r, TILE)
                s = sc[e, h, here]
                r0 = s * sx[e, h, here]
                v0 = w0[e, h, here]
                p_buf[i, pl.ds(r, TILE), at] = s * (c * r0 - d * v0)
                r_buf[i, pl.ds(r, TILE), at] = r0 - c * v0 + d * n0[e, h, here]
        for copy in out(i):
            copy.start()
        return carry

    lax.fori_loop(0, nx, plane, 0)
    for i in range(nx):
        for copy in out(i):
            copy.wait()


def shards(nx_dev, ny_dev, source, density):
    both = ("gx", "gy")
    near_pairs, far_pairs, ynear_pairs, yfar_pairs = swaps(nx_dev, ny_dev)
    nx, ny, nz = density.shape
    sizes = (nx_dev, ny_dev)
    vmem = pl.BlockSpec(memory_space=VMEM)
    hbm = pl.BlockSpec(memory_space=pltpu.HBM)

    def call(body, n_in, outs, limit, **more):
        return pl.pallas_call(
            functools.partial(body, sizes), out_shape=outs, in_specs=[vmem] * n_in, out_specs=jax.tree.map(lambda _: vmem, outs),
            compiler_params=pltpu.CompilerParams(vmem_limit_bytes=limit * MIB), **more,
        )

    def send(value, pairs):
        return lax.ppermute(value, both, pairs)

    few, planes, rows, block = (VMEM(v, jnp.float32) for v in ((4, ny, nz), (5, ny, nz), (ROWS, nx, nz), density.shape))
    shapes = (few, planes, rows, rows, block, block)
    far, near, xs, dg, dens, src = pl.pallas_call(
        functools.partial(load_kernel, sizes), out_shape=shapes, in_specs=[hbm] * 2, out_specs=(vmem,) * 6, name="load_kernel",
        scratch_shapes=[VMEM((1, nz // LANES, ny + 2 * TILE, LANES), jnp.float32), pltpu.SemaphoreType.DMA((2 * nx,))], compiler_params=pltpu.CompilerParams(vmem_limit_bytes=8 * MIB),
    )(*(pltpu.with_memory_space_constraint(v, pltpu.HBM) for v in (density, source)))
    far = send(far, far_pairs)
    near = send(near, near_pairs)
    rxs = send(xs, ynear_pairs)
    rdg = send(dg, yfar_pairs)
    corner = VMEM((4, TILE, nz), jnp.float32)
    rfc, rnc = call(corner_kernel, 4, (corner, corner), 4)(rxs, rdg, dens, src)
    rfc = send(rfc, far_pairs)
    rnc = send(rnc, near_pairs)

    ext = VMEM((nx + 2 * DEEP, nz // LANES, ny + 2 * OFF, LANES), jnp.float32)
    sums = VMEM((SUMS, TILE, LANES), jnp.float32)
    held = call(inner_kernel, 3, (ext,) * 9, 8)(dens, src, near)
    dx, sx, wx, wy, wz, sc, g0, g1, w0 = held
    n0, part = call(inner_second_kernel, 7, (ext, sums), 8)(sx, wx, wy, wz, sc, g1, w0)
    held = (*held, n0)
    part, *held = call(edge_kernel, 14, (sums,) + (ext,) * 10, 8, input_output_aliases={4 + k: 1 + k for k in range(10)})(
        rxs, rdg, rnc, part, *held)
    mom, *held = call(far_kernel, 13, (VMEM((1, LANES), jnp.float32),) + (ext,) * 10, 8, input_output_aliases={3 + k: 1 + k for k in range(10)})(
        far, rfc, part, *held)
    dx, sx, wx, wy, wz, sc, g0, g1, w0, n0 = held

    n = nx_dev * ny_dev
    sent = jnp.broadcast_to(mom[None], (n, 1, LANES))
    got = lax.all_to_all(sent, both, 0, 0, tiled=True).reshape(n, LANES)
    whole = jax.ShapeDtypeStruct(density.shape, jnp.float32)
    plane = VMEM(density.shape, jnp.float32)
    return pl.pallas_call(
        last_kernel, out_shape=(whole, whole), in_specs=[vmem] * 5, out_specs=(hbm, hbm), name="last_kernel",
        scratch_shapes=[plane, plane, pltpu.SemaphoreType.DMA((2, nx))],
        compiler_params=pltpu.CompilerParams(vmem_limit_bytes=8 * MIB),
    )(got, sx, sc, w0, n0)


def solution(mesh):
    spec = P("gx", "gy", None)
    body = functools.partial(shards, mesh.shape["gx"], mesh.shape["gy"])
    return jax.shard_map(body, mesh=mesh, in_specs=(spec, spec), out_specs=(spec, spec), check_vma=False)
```

time: 35.2 us -> 32.3 us (0.918)
  Pallas kernels: 12.3 us -> 9.95 us
    pallas_call x1, Pallas kernels: 2.85 us -> 1.42 us  [shards(): call(edge_kernel, 14, (sums,) + (ext,) * 10, 8, input_output_aliases={4 +...]
    pallas_call x2 -> x3, Pallas kernels: 3.73 us -> 3.1 us  [the longest x1 2.55 us: shards(): held = call(inner_kernel, 3, (ext,) * 9, 8)(dens, src, near)]
  transfers between devices with their start and end apart: 6 -> 6, of which waited for: 1 -> 1; matrix products, arithmetic and copies ran while one was open for 0% -> 0% of each run, Pallas kernels for 19% -> 14%
where the time goes in v6:
time: 32.3 us; the launch traced here: 32.1 us
  blocking collectives  10.8 us (33%)
  Pallas kernels  9.95 us (31%)
  starting transfers between devices  8.14 us (25%)
  waiting for transfers between devices  2.52 us (8%)
  between operations  0.7 us (2%)
    all_to_all x1, blocking collectives, shards(): got = lax.all_to_all(sent, both, 0, 0, tiled=True).reshape(n, LANES)  10.8 us
    ppermute x6, starting transfers between devices, send(): return lax.ppermute(value, both, pairs)  8.14 us
    pallas_call x1, Pallas kernels, shards(): held = call(inner_kernel, 3, (ext,) * 9, 8)(dens, src, near)  2.55 us
    ppermute x6, waiting for transfers between devices, send(): return lax.ppermute(value, both, pairs)  2.52 us
    pallas_call x1, Pallas kernels, shards(): call(far_kernel, 13, (VMEM((1, LANES), jnp.float32),) + (ext,) * 10, 8, i...  1.86 us
    pallas_call x1, Pallas kernels, shards(): pl.pallas_call(functools.partial(load_kernel, sizes), out_shape=shapes, i...  1.84 us
    pallas_call x1, Pallas kernels, shards(): pl.pallas_call(last_kernel, out_shape=(whole, whole), in_specs=[vmem] * 5...  1.73 us
    pallas_call x1, Pallas kernels, shards(): call(edge_kernel, 14, (sums,) + (ext,) * 10, 8, input_output_aliases={4 +...  1.42 us
  transfers between devices with their start and end apart: 6, of which 1 were waited for; matrix products, arithmetic and copies ran while one was open for 0% of the time, Pallas kernels for 14%

profile of v6, /device:TPU:0, one launch (start us, length us, event | category | flops | bytes accessed | tf_op | source)
XLA Modules:
  0.0 32.1 jit_solution(17137628940738459050)
XLA Ops:
  0.6 1.8 %load_kernel.1 = (f32[4,128,256]{2,1,0:T(8,128)S(1)}, f32[5,128,256]{2,1,0:T(8,128)S(1)}, f32[5,8,256]{2,1,0:T(8,128)S(1)}, f32[5,8,256]{2,1,0:T(8,128)S(1)}, f3...) custom-call(f32[8,128,256]{2,1,0:T(8,128)} %dens_hbm.1, f32[8,128,256]{2,1,0:T(8,128)} %src_hbm.1), custom_call_target="tpu_custom_call" | custom-call | tf_op jit(solution)/shard_map/load_kernel/pallas_call | solution.py:470
  2.5 0.6 %collective-permute-start.5 = (f32[5,128,256]{2,1,0:T(8,128)S(1)}, f32[5,128,256]{2,1,0:T(8,128)S(1)}, u32[]{:S(2)}, u32[]{:S(2)}) collective-permute-start(f32[5,128,256]{2,1,0:T(8,128)S(1)} %get-tuple-element.44), channel_id=1, source_target_pairs={{0,4},{1,5},{2,6},{3,7},{4,0},{5,1},{6,2},{7,3},{8,12},{9,13},{10,... | collective-permute-start | bytes 1966088 | tf_op jit(solution)/shard_map/ppermute | solution.py:466
  3.0 2.6 %collective-permute-start = (f32[4,128,256]{2,1,0:T(8,128)S(1)}, f32[4,128,256]{2,1,0:T(8,128)S(1)}, u32[]{:S(2)}, u32[]{:S(2)}) collective-permute-start(f32[4,128,256]{2,1,0:T(8,128)S(1)} %get-tuple-element.37), channel_id=1, source_target_pairs={{0,2},{1,3},{2,0},{3,1},{4,8},{5,9},{6,10},{7,11},{8,4},{9,5},{10,... | collective-permute-start | bytes 1572872 | tf_op jit(solution)/shard_map/ppermute | solution.py:466
  5.6 1.5 %collective-permute-start.1 = (f32[5,8,256]{2,1,0:T(8,128)S(1)}, f32[5,8,256]{2,1,0:T(8,128)S(1)}, u32[]{:S(2)}, u32[]{:S(2)}) collective-permute-start(f32[5,8,256]{2,1,0:T(8,128)S(1)} %get-tuple-element.38), channel_id=1, source_target_pairs={{0,1},{1,0},{2,3},{3,2},{4,5},{5,4},{6,7},{7,6},{8,9},{9,8},{10,11... | collective-permute-start | bytes 122888 | tf_op jit(solution)/shard_map/ppermute | solution.py:466
  7.1 0.0 collective-permute-start.2
  7.1 2.5 %collective-permute-done.1.rxs = f32[5,8,256]{2,1,0:T(8,128)S(1)} collective-permute-done((f32[5,8,256]{2,1,0:T(8,128)S(1)}, f32[5,8,256]{2,1,0:T(8,128)S(1)}, u32[]{:S(2)}, u32[]{:S(2)}) %collective-permute-start.1) | collective-permute-done | bytes 40992 | tf_op jit(solution)/shard_map/ppermute | solution.py:466
  9.6 0.0 collective-permute-done.2.rdg
  9.7 0.1 collective-permute-start.4
  9.7 3.4 %collective-permute-start.3 = (f32[4,8,256]{2,1,0:T(8,128)S(1)}, f32[4,8,256]{2,1,0:T(8,128)S(1)}, u32[]{:S(2)}, u32[]{:S(2)}) collective-permute-start(f32[4,8,256]{2,1,0:T(8,128)S(1)} %get-tuple-element.42), channel_id=1, source_target_pairs={{0,2},{1,3},{2,0},{3,1},{4,8},{5,9},{6,10},{7,11},{8,4},{9,5},{10,... | collective-permute-start | bytes 98312 | tf_op jit(solution)/shard_map/ppermute | solution.py:466
  13.2 0.0 collective-permute-done.5.near
  13.2 2.6 %shard_map.42 = (f32[14,2,160,128]{3,2,1,0:T(8,128)S(1)}, f32[14,2,160,128]{3,2,1,0:T(8,128)S(1)}, f32[14,2,160,128]{3,2,1,0:T(8,128)S(1)}, f32[14,2,160,128]{3,...) custom-call(f32[8,128,256]{2,1,0:T(8,128)S(1)} %get-tuple-element.40, ...), custom_call_target="tpu_custom_call" | custom-call | tf_op jit(solution)/shard_map/pallas_call | solution.py:485
  15.7 0.5 %shard_map.43 = (f32[14,2,160,128]{3,2,1,0:T(8,128)S(1)}, f32[5,8,128]{2,1,0:T(8,128)S(1)}) custom-call(f32[14,2,160,128]{3,2,1,0:T(8,128)S(1)} %get-tuple-element.45.sx.refs_1_, f32[14,2,160,128]{3,2,1,0:T(8,128)S(1)} %get-tuple-element.46.wx.refs_2_, f32[14,2,160,128]{3,2,1,0:T(8,128)S(1)} %get-tuple-element.47.wy.refs_3_, ...), custom_call_target="tpu_custom_call" | custom-call | tf_op jit(solution)/shard_map/pallas_call | solution.py:487
  16.3 0.0 collective-permute-done.4.rnc
  16.3 1.4 %shard_map.44 = (f32[5,8,128]{2,1,0:T(8,128)S(1)}, f32[14,2,160,128]{3,2,1,0:T(8,128)S(1)}, f32[14,2,160,128]{3,2,1,0:T(8,128)S(1)}, f32[14,2,160,128]{3,2,1,0:T...) custom-call(f32[5,8,256]{2,1,0:T(8,128)S(1)} %collective-permute-don, ...), custom_call_target="tpu_custom_call", output_to_operand_aliasing={{1}: (4, {}), {2}: (5, {}), {3}: (6, {}), {4}: (7, {}), {5}... | custom-call | tf_op jit(solution)/shard_map/pallas_call | solution.py:489
  17.7 0.0 collective-permute-done.3.rfc
  17.7 0.0 collective-permute-done.far
  17.7 1.9 %shard_map.45 = (f32[1,128]{1,0:T(1,128)S(1)}, f32[14,2,160,128]{3,2,1,0:T(8,128)S(1)}, f32[14,2,160,128]{3,2,1,0:T(8,128)S(1)}, f32[14,2,160,128]{3,2,1,0:T(8,1...) custom-call(f32[4,128,256]{2,1,0:T(8,128)S(1)} %collective-permute-d, ...), custom_call_target="tpu_custom_call", output_to_operand_aliasing={{1}: (3, {}), {2}: (4, {}), {3}: (5, {}), {4}: (6, {}), {5}... | custom-call | tf_op jit(solution)/shard_map/pallas_call | solution.py:491
  19.6 10.8 %all_to_all.5 = f32[32,1,128]{2,1,0:T(1,128)S(1)} all-to-all(f32[32,1,128]{2,1,0:T(1,128)S(1)} %broadcast_in_dim.9), channel_id=1, replica_groups=mesh['gx'=8,'gy'=4] {'gx','gy'}, dimensions={0} | all-to-all | bytes 32768 | tf_op jit(solution)/shard_map/all_to_all | solution.py:497
  30.4 1.7 %last_kernel.1 = (f32[8,128,256]{2,1,0:T(8,128)}, f32[8,128,256]{2,1,0:T(8,128)}) custom-call(f32[32,128]{1,0:T(8,128)S(1)} %bitcast.2, f32[14,2,160,128]{3,2,1,0:T(8,128)S(1)} %get-tuple-element.68.sx, f32[14,2,160,128]{3,2,1,0:T(8,128)S(1)} %get-tuple-element.69.sc, f32[14,2,160,128]{3,2,1,0:T(8,128)S(1)} %get-tuple-element.70.w0, ...), custom_call_target="tpu_custom_call" | custom-call | tf_op jit(solution)/shard_map/last_kernel/pallas_call | solution.py:500
  (2 shorter events, 0.0 us)
Async XLA Ops:
  2.5 10.7 %collective-permute-start.5 = (f32[5,128,256]{2,1,0:T(8,128)S(1)}, f32[5,128,256]{2,1,0:T(8,128)S(1)}, u32[]{:S(2)}, u32[]{:S(2)}) collective-permute-start(f32[5,128,256]{2,1,0:T(8,128)S(1)} %get-tuple-element.44), channel_id=1, source_target_pairs={{0,4},{1,5},{2,6},{3,7},{4,0},{5,1},{6,2},{7,3},{8,12},{9,13},{10,... | collective-permute-start | bytes 1966088 | tf_op jit(solution)/shard_map/ppermute | solution.py:466
  3.0 14.7 %collective-permute-start = (f32[4,128,256]{2,1,0:T(8,128)S(1)}, f32[4,128,256]{2,1,0:T(8,128)S(1)}, u32[]{:S(2)}, u32[]{:S(2)}) collective-permute-start(f32[4,128,256]{2,1,0:T(8,128)S(1)} %get-tuple-element.37), channel_id=1, source_target_pairs={{0,2},{1,3},{2,0},{3,1},{4,8},{5,9},{6,10},{7,11},{8,4},{9,5},{10,... | collective-permute-start | bytes 1572872 | tf_op jit(solution)/shard_map/ppermute | solution.py:466
  5.6 4.0 %collective-permute-start.1 = (f32[5,8,256]{2,1,0:T(8,128)S(1)}, f32[5,8,256]{2,1,0:T(8,128)S(1)}, u32[]{:S(2)}, u32[]{:S(2)}) collective-permute-start(f32[5,8,256]{2,1,0:T(8,128)S(1)} %get-tuple-element.38), channel_id=1, source_target_pairs={{0,1},{1,0},{2,3},{3,2},{4,5},{5,4},{6,7},{7,6},{8,9},{9,8},{10,11... | collective-permute-start | bytes 122888 | tf_op jit(solution)/shard_map/ppermute | solution.py:466
  7.1 2.5 %collective-permute-start.2 = (f32[5,8,256]{2,1,0:T(8,128)S(1)}, f32[5,8,256]{2,1,0:T(8,128)S(1)}, u32[]{:S(2)}, u32[]{:S(2)}) collective-permute-start(f32[5,8,256]{2,1,0:T(8,128)S(1)} %get-tuple-element.39), channel_id=1, source_target_pairs={{0,4},{1,2},{2,1},{3,7},{4,0},{5,6},{6,5},{7,3},{8,12},{9,10},{10,... | collective-permute-start | bytes 122888 | tf_op jit(solution)/shard_map/ppermute | solution.py:466
  9.7 6.6 %collective-permute-start.4 = (f32[4,8,256]{2,1,0:T(8,128)S(1)}, f32[4,8,256]{2,1,0:T(8,128)S(1)}, u32[]{:S(2)}, u32[]{:S(2)}) collective-permute-start(f32[4,8,256]{2,1,0:T(8,128)S(1)} %get-tuple-element.43), channel_id=1, source_target_pairs={{0,4},{1,5},{2,6},{3,7},{4,0},{5,1},{6,2},{7,3},{8,12},{9,13},{10,... | collective-permute-start | bytes 98312 | tf_op jit(solution)/shard_map/ppermute | solution.py:466
  9.7 8.0 %collective-permute-start.3 = (f32[4,8,256]{2,1,0:T(8,128)S(1)}, f32[4,8,256]{2,1,0:T(8,128)S(1)}, u32[]{:S(2)}, u32[]{:S(2)}) collective-permute-start(f32[4,8,256]{2,1,0:T(8,128)S(1)} %get-tuple-element.42), channel_id=1, source_target_pairs={{0,2},{1,3},{2,0},{3,1},{4,8},{5,9},{6,10},{7,11},{8,4},{9,5},{10,... | collective-permute-start | bytes 98312 | tf_op jit(solution)/shard_map/ppermute | solution.py:466

commit v7 on v6

--- a/solution.py
+++ b/solution.py
@@ -13,6 +13,7 @@
 OFF = 16
 DEEP = 3
 ROWS = 5
+STEP = 2
 PART = 16
 SUMS = 5
 MIB = 1 << 20
@@ -302,12 +303,8 @@
     return jnp.where(xodd, 1, 4), jnp.where(xodd, 2, 5), jnp.where(xodd, 3, 6), jnp.where(xodd, par[2], par[3])
 
 
-def inner_kernel(sizes, dens, src, near, dx, sx, wx, wy, wz, sc, g0, g1, w0):
-    par = position(sizes)
+def inner_kernel(sizes, dens, src, dx, sx, wx, wy, wz, sc, g0, g1, w0):
     nx, ny, _ = dens.shape
-    xodd = par[0] == 1
-    first, second, _, has = near_side(par)
-    has_near = has == 1
     own = slice(OFF, OFF + ny)
 
     def fill(k):
@@ -315,11 +312,24 @@
         put_plane(sx, k + DEEP, own, src[k])
 
     loop(nx, fill)
+    weigh(dx, sx, wx, wy, wz, sc, g0, DEEP + 1, nx - 2, row_tiles(ny, 1), unroll=2)
+    apply_first(sx, wx, wy, wz, sc, g0, g1, w0, DEEP + 2, nx - 4, row_tiles(ny, 2), unroll=4)
+
+
+def beside_kernel(sizes, near, *refs):
+    dx, sx, wx, wy, wz, sc, g0, g1, w0 = refs[9:]
+    par = position(sizes)
+    ny = near.shape[1]
+    nx = dx.shape[0] - 2 * DEEP
+    xodd = par[0] == 1
+    has = near_side(par)[3]
+    has_near = has == 1
+    own = slice(OFF, OFF + ny)
     near_third, near_beyond = jnp.where(xodd, 0, nx + 3), jnp.where(xodd, 1, nx + 3)
     loop(3, lambda k: put_plane(dx, near_third + k, own, jnp.where(has_near, 0.5 * near[k], 0.0)))
     loop(2, lambda k: put_plane(sx, near_beyond + k, own, jnp.where(has_near, near[3 + k], 0.0)))
-    weigh(dx, sx, wx, wy, wz, sc, g0, first, nx + 1, row_tiles(ny, 1), unroll=3)
-    apply_first(sx, wx, wy, wz, sc, g0, g1, w0, second, nx - 1, row_tiles(ny, 2), unroll=7)
+    weigh(dx, sx, wx, wy, wz, sc, g0, jnp.where(xodd, 1, nx + 2), 3, row_tiles(ny, 1), unroll=1)
+    apply_first(sx, wx, wy, wz, sc, g0, g1, w0, jnp.where(xodd, 2, nx + 1), 3, row_tiles(ny, 2), unroll=3)
     clear_plane(g1, jnp.where(xodd, 2, nx + 3), has, row_tiles(ny, 2))
 
 
@@ -425,25 +435,31 @@
     d = jnp.broadcast_to(a0 * a1, (TILE, LANES))
 
     def out(i):
-        return (pltpu.make_async_copy(p_buf.at[pl.ds(i, 1)], p_out.at[pl.ds(i, 1)], sems.at[0, i]),
-                pltpu.make_async_copy(r_buf.at[pl.ds(i, 1)], r_out.at[pl.ds(i, 1)], sems.at[1, i]))
-
-    def plane(i, carry):
-        e = i + DEEP
-        for r in range(0, ny, TILE):
-            for h, at in halves(nz):
-                here = pl.ds(OFF + r, TILE)
-                s = sc[e, h, here]
-                r0 = s * sx[e, h, here]
-                v0 = w0[e, h, here]
-                p_buf[i, pl.ds(r, TILE), at] = s * (c * r0 - d * v0)
-                r_buf[i, pl.ds(r, TILE), at] = r0 - c * v0 + d * n0[e, h, here]
+        here = pl.ds(i * STEP, STEP)
+        return (pltpu.make_async_copy(p_buf.at[here], p_out.at[here], sems.at[0, i]),
+                pltpu.make_async_copy(r_buf.at[here], r_out.at[here], sems.at[1, i]))
+
+    def group(i, carry):
+        for k in range(STEP):
+            plane = i * STEP + k
+            e = plane + DEEP
+            stores = Stores(2)
+            for r in range(0, ny, TILE):
+                here, there = pl.ds(OFF + r, TILE), pl.ds(r, TILE)
+                items = []
+                for h, at in halves(nz):
+                    s, q, v0, v1 = sc[e, h, here], sx[e, h, here], w0[e, h, here], n0[e, h, here]
+                    r0 = s * q
+                    items.append((p_buf, (plane, there, at), s * (c * r0 - d * v0)))
+                    items.append((r_buf, (plane, there, at), r0 - c * v0 + d * v1))
+                stores.put(items)
+            stores.flush()
         for copy in out(i):
             copy.start()
         return carry
 
-    lax.fori_loop(0, nx, plane, 0)
-    for i in range(nx):
+    lax.fori_loop(0, nx // STEP, group, 0)
+    for i in range(nx // STEP):
         for copy in out(i):
             copy.wait()
 
@@ -482,7 +498,8 @@
 
     ext = VMEM((nx + 2 * DEEP, nz // LANES, ny + 2 * OFF, LANES), jnp.float32)
     sums = VMEM((SUMS, TILE, LANES), jnp.float32)
-    held = call(inner_kernel, 3, (ext,) * 9, 8)(dens, src, near)
+    held = call(inner_kernel, 2, (ext,) * 9, 8)(dens, src)
+    held = call(beside_kernel, 10, (ext,) * 9, 8, input_output_aliases={1 + k: k for k in range(9)})(near, *held)
     dx, sx, wx, wy, wz, sc, g0, g1, w0 = held
     n0, part = call(inner_second_kernel, 7, (ext, sums), 8)(sx, wx, wy, wz, sc, g1, w0)
     held = (*held, n0)

time: 32.3 us -> 32.2 us (level)
    pallas_call x1 -> x2, Pallas kernels: 2.55 us -> 2.4 us  [the longest x1 1.33 us: shards(): held = call(inner_kernel, 2, (ext,) * 9, 8)(dens, src)]
where the time goes in v7:
time: 32.2 us; the launch traced here: 32 us
  blocking collectives  10.8 us (34%)
  Pallas kernels  9.83 us (31%)
  starting transfers between devices  8.14 us (25%)
  waiting for transfers between devices  2.52 us (8%)
  between operations  0.71 us (2%)
    all_to_all x1, blocking collectives, shards(): got = lax.all_to_all(sent, both, 0, 0, tiled=True).reshape(n, LANES)  10.8 us
    ppermute x6, starting transfers between devices, send(): return lax.ppermute(value, both, pairs)  8.14 us
    ppermute x6, waiting for transfers between devices, send(): return lax.ppermute(value, both, pairs)  2.52 us
    pallas_call x1, Pallas kernels, shards(): call(far_kernel, 13, (VMEM((1, LANES), jnp.float32),) + (ext,) * 10, 8, i...  1.85 us
    pallas_call x1, Pallas kernels, shards(): pl.pallas_call(functools.partial(load_kernel, sizes), out_shape=shapes, i...  1.84 us
    pallas_call x1, Pallas kernels, shards(): pl.pallas_call(last_kernel, out_shape=(whole, whole), in_specs=[vmem] * 5...  1.76 us
    pallas_call x1, Pallas kernels, shards(): call(edge_kernel, 14, (sums,) + (ext,) * 10, 8, input_output_aliases={4 +...  1.43 us
    pallas_call x1, Pallas kernels, shards(): held = call(inner_kernel, 2, (ext,) * 9, 8)(dens, src)  1.33 us
  transfers between devices with their start and end apart: 6, of which 1 were waited for; matrix products, arithmetic and copies ran while one was open for 0% of the time, Pallas kernels for 14%

profile of v7, /device:TPU:0, one launch (start us, length us, event | category | flops | bytes accessed | tf_op | source)
XLA Modules:
  0.0 32.0 jit_solution(18077887278623677453)
XLA Ops:
  0.6 1.8 %load_kernel.1 = (f32[4,128,256]{2,1,0:T(8,128)S(1)}, f32[5,128,256]{2,1,0:T(8,128)S(1)}, f32[5,8,256]{2,1,0:T(8,128)S(1)}, f32[5,8,256]{2,1,0:T(8,128)S(1)}, f3...) custom-call(f32[8,128,256]{2,1,0:T(8,128)} %dens_hbm.1, f32[8,128,256]{2,1,0:T(8,128)} %src_hbm.1), custom_call_target="tpu_custom_call" | custom-call | tf_op jit(solution)/shard_map/load_kernel/pallas_call | solution.py:486
  2.5 0.6 %collective-permute-start.5 = (f32[5,128,256]{2,1,0:T(8,128)S(1)}, f32[5,128,256]{2,1,0:T(8,128)S(1)}, u32[]{:S(2)}, u32[]{:S(2)}) collective-permute-start(f32[5,128,256]{2,1,0:T(8,128)S(1)} %get-tuple-element.53), channel_id=1, source_target_pairs={{0,4},{1,5},{2,6},{3,7},{4,0},{5,1},{6,2},{7,3},{8,12},{9,13},{10,... | collective-permute-start | bytes 1966088 | tf_op jit(solution)/shard_map/ppermute | solution.py:482
  3.0 2.6 %collective-permute-start = (f32[4,128,256]{2,1,0:T(8,128)S(1)}, f32[4,128,256]{2,1,0:T(8,128)S(1)}, u32[]{:S(2)}, u32[]{:S(2)}) collective-permute-start(f32[4,128,256]{2,1,0:T(8,128)S(1)} %get-tuple-element.46), channel_id=1, source_target_pairs={{0,2},{1,3},{2,0},{3,1},{4,8},{5,9},{6,10},{7,11},{8,4},{9,5},{10,... | collective-permute-start | bytes 1572872 | tf_op jit(solution)/shard_map/ppermute | solution.py:482
  5.6 1.5 %collective-permute-start.1 = (f32[5,8,256]{2,1,0:T(8,128)S(1)}, f32[5,8,256]{2,1,0:T(8,128)S(1)}, u32[]{:S(2)}, u32[]{:S(2)}) collective-permute-start(f32[5,8,256]{2,1,0:T(8,128)S(1)} %get-tuple-element.47), channel_id=1, source_target_pairs={{0,1},{1,0},{2,3},{3,2},{4,5},{5,4},{6,7},{7,6},{8,9},{9,8},{10,11... | collective-permute-start | bytes 122888 | tf_op jit(solution)/shard_map/ppermute | solution.py:482
  7.1 0.0 collective-permute-start.2
  7.1 2.5 %collective-permute-done.1.rxs = f32[5,8,256]{2,1,0:T(8,128)S(1)} collective-permute-done((f32[5,8,256]{2,1,0:T(8,128)S(1)}, f32[5,8,256]{2,1,0:T(8,128)S(1)}, u32[]{:S(2)}, u32[]{:S(2)}) %collective-permute-start.1) | collective-permute-done | bytes 40992 | tf_op jit(solution)/shard_map/ppermute | solution.py:482
  9.6 0.0 collective-permute-done.2.rdg
  9.7 0.1 collective-permute-start.4
  9.7 3.4 %collective-permute-start.3 = (f32[4,8,256]{2,1,0:T(8,128)S(1)}, f32[4,8,256]{2,1,0:T(8,128)S(1)}, u32[]{:S(2)}, u32[]{:S(2)}) collective-permute-start(f32[4,8,256]{2,1,0:T(8,128)S(1)} %get-tuple-element.51), channel_id=1, source_target_pairs={{0,2},{1,3},{2,0},{3,1},{4,8},{5,9},{6,10},{7,11},{8,4},{9,5},{10,... | collective-permute-start | bytes 98312 | tf_op jit(solution)/shard_map/ppermute | solution.py:482
  13.2 1.3 %shard_map.42 = (f32[14,2,160,128]{3,2,1,0:T(8,128)S(1)}, f32[14,2,160,128]{3,2,1,0:T(8,128)S(1)}, f32[14,2,160,128]{3,2,1,0:T(8,128)S(1)}, f32[14,2,160,128]{3,...) custom-call(f32[8,128,256]{2,1,0:T(8,128)S(1)} %get-tuple-element.49, ...), custom_call_target="tpu_custom_call" | custom-call | tf_op jit(solution)/shard_map/pallas_call | solution.py:501
  14.5 0.0 collective-permute-done.5.near
  14.5 1.1 %shard_map.43 = (f32[14,2,160,128]{3,2,1,0:T(8,128)S(1)}, f32[14,2,160,128]{3,2,1,0:T(8,128)S(1)}, f32[14,2,160,128]{3,2,1,0:T(8,128)S(1)}, f32[14,2,160,128]{3,...) custom-call(f32[5,128,256]{2,1,0:T(8,128)S(1)} %collective-permute-d, ...), custom_call_target="tpu_custom_call", output_to_operand_aliasing={{0}: (1, {}), {1}: (2, {}), {2}: (3, {}), {3}: (4, {}), {4}... | custom-call | tf_op jit(solution)/shard_map/pallas_call | solution.py:502
  15.6 0.5 %shard_map.44 = (f32[14,2,160,128]{3,2,1,0:T(8,128)S(1)}, f32[5,8,128]{2,1,0:T(8,128)S(1)}) custom-call(f32[14,2,160,128]{3,2,1,0:T(8,128)S(1)} %get-tuple-element.63.sx.refs_1_, f32[14,2,160,128]{3,2,1,0:T(8,128)S(1)} %get-tuple-element.64.wx.refs_2_, f32[14,2,160,128]{3,2,1,0:T(8,128)S(1)} %get-tuple-element.65.wy.refs_3_, ...), custom_call_target="tpu_custom_call" | custom-call | tf_op jit(solution)/shard_map/pallas_call | solution.py:504
  16.1 0.0 collective-permute-done.4.rnc
  16.1 1.4 %shard_map.45 = (f32[5,8,128]{2,1,0:T(8,128)S(1)}, f32[14,2,160,128]{3,2,1,0:T(8,128)S(1)}, f32[14,2,160,128]{3,2,1,0:T(8,128)S(1)}, f32[14,2,160,128]{3,2,1,0:T...) custom-call(f32[5,8,256]{2,1,0:T(8,128)S(1)} %collective-permute-don, ...), custom_call_target="tpu_custom_call", output_to_operand_aliasing={{1}: (4, {}), {2}: (5, {}), {3}: (6, {}), {4}: (7, {}), {5}... | custom-call | tf_op jit(solution)/shard_map/pallas_call | solution.py:506
  17.6 0.0 collective-permute-done.3.rfc
  17.6 0.0 collective-permute-done.far
  17.6 1.9 %shard_map.46 = (f32[1,128]{1,0:T(1,128)S(1)}, f32[14,2,160,128]{3,2,1,0:T(8,128)S(1)}, f32[14,2,160,128]{3,2,1,0:T(8,128)S(1)}, f32[14,2,160,128]{3,2,1,0:T(8,1...) custom-call(f32[4,128,256]{2,1,0:T(8,128)S(1)} %collective-permute-d, ...), custom_call_target="tpu_custom_call", output_to_operand_aliasing={{1}: (3, {}), {2}: (4, {}), {3}: (5, {}), {4}: (6, {}), {5}... | custom-call | tf_op jit(solution)/shard_map/pallas_call | solution.py:508
  19.5 10.8 %all_to_all.5 = f32[32,1,128]{2,1,0:T(1,128)S(1)} all-to-all(f32[32,1,128]{2,1,0:T(1,128)S(1)} %broadcast_in_dim.9), channel_id=1, replica_groups=mesh['gx'=8,'gy'=4] {'gx','gy'}, dimensions={0} | all-to-all | bytes 32768 | tf_op jit(solution)/shard_map/all_to_all | solution.py:514
  30.2 1.8 %last_kernel.1 = (f32[8,128,256]{2,1,0:T(8,128)}, f32[8,128,256]{2,1,0:T(8,128)}) custom-call(f32[32,128]{1,0:T(8,128)S(1)} %bitcast.2, f32[14,2,160,128]{3,2,1,0:T(8,128)S(1)} %get-tuple-element.86.sx, f32[14,2,160,128]{3,2,1,0:T(8,128)S(1)} %get-tuple-element.87.sc, f32[14,2,160,128]{3,2,1,0:T(8,128)S(1)} %get-tuple-element.88.w0, ...), custom_call_target="tpu_custom_call" | custom-call | tf_op jit(solution)/shard_map/last_kernel/pallas_call | solution.py:517
  (2 shorter events, 0.0 us)
Async XLA Ops:
  2.5 12.0 %collective-permute-start.5 = (f32[5,128,256]{2,1,0:T(8,128)S(1)}, f32[5,128,256]{2,1,0:T(8,128)S(1)}, u32[]{:S(2)}, u32[]{:S(2)}) collective-permute-start(f32[5,128,256]{2,1,0:T(8,128)S(1)} %get-tuple-element.53), channel_id=1, source_target_pairs={{0,4},{1,5},{2,6},{3,7},{4,0},{5,1},{6,2},{7,3},{8,12},{9,13},{10,... | collective-permute-start | bytes 1966088 | tf_op jit(solution)/shard_map/ppermute | solution.py:482
  3.0 14.5 %collective-permute-start = (f32[4,128,256]{2,1,0:T(8,128)S(1)}, f32[4,128,256]{2,1,0:T(8,128)S(1)}, u32[]{:S(2)}, u32[]{:S(2)}) collective-permute-start(f32[4,128,256]{2,1,0:T(8,128)S(1)} %get-tuple-element.46), channel_id=1, source_target_pairs={{0,2},{1,3},{2,0},{3,1},{4,8},{5,9},{6,10},{7,11},{8,4},{9,5},{10,... | collective-permute-start | bytes 1572872 | tf_op jit(solution)/shard_map/ppermute | solution.py:482
  5.6 4.0 %collective-permute-start.1 = (f32[5,8,256]{2,1,0:T(8,128)S(1)}, f32[5,8,256]{2,1,0:T(8,128)S(1)}, u32[]{:S(2)}, u32[]{:S(2)}) collective-permute-start(f32[5,8,256]{2,1,0:T(8,128)S(1)} %get-tuple-element.47), channel_id=1, source_target_pairs={{0,1},{1,0},{2,3},{3,2},{4,5},{5,4},{6,7},{7,6},{8,9},{9,8},{10,11... | collective-permute-start | bytes 122888 | tf_op jit(solution)/shard_map/ppermute | solution.py:482
  7.1 2.5 %collective-permute-start.2 = (f32[5,8,256]{2,1,0:T(8,128)S(1)}, f32[5,8,256]{2,1,0:T(8,128)S(1)}, u32[]{:S(2)}, u32[]{:S(2)}) collective-permute-start(f32[5,8,256]{2,1,0:T(8,128)S(1)} %get-tuple-element.48), channel_id=1, source_target_pairs={{0,4},{1,2},{2,1},{3,7},{4,0},{5,6},{6,5},{7,3},{8,12},{9,10},{10,... | collective-permute-start | bytes 122888 | tf_op jit(solution)/shard_map/ppermute | solution.py:482
  9.7 6.5 %collective-permute-start.4 = (f32[4,8,256]{2,1,0:T(8,128)S(1)}, f32[4,8,256]{2,1,0:T(8,128)S(1)}, u32[]{:S(2)}, u32[]{:S(2)}) collective-permute-start(f32[4,8,256]{2,1,0:T(8,128)S(1)} %get-tuple-element.52), channel_id=1, source_target_pairs={{0,4},{1,5},{2,6},{3,7},{4,0},{5,1},{6,2},{7,3},{8,12},{9,13},{10,... | collective-permute-start | bytes 98312 | tf_op jit(solution)/shard_map/ppermute | solution.py:482
  9.7 7.8 %collective-permute-start.3 = (f32[4,8,256]{2,1,0:T(8,128)S(1)}, f32[4,8,256]{2,1,0:T(8,128)S(1)}, u32[]{:S(2)}, u32[]{:S(2)}) collective-permute-start(f32[4,8,256]{2,1,0:T(8,128)S(1)} %get-tuple-element.51), channel_id=1, source_target_pairs={{0,2},{1,3},{2,0},{3,1},{4,8},{5,9},{6,10},{7,11},{8,4},{9,5},{10,... | collective-permute-start | bytes 98312 | tf_op jit(solution)/shard_map/ppermute | solution.py:482
